TPU v7x, 32 devices: a whole 2x2x4 slice. The times are simulated.
32 devices in a mesh: seq: 4 (over y, core), tp: 4 (over z), dp: 2 (over x).
Axes of the slice: x: 2, y: 2, z: 4, core: 2. Of those that a mesh axis runs over, the one named last changes fastest.
Arguments:
- queries: bfloat16 [2048, 4096], P(('dp', 'seq'), 'tp'), parts along dimension 0, may hold values from -36 to 36
- key_rows: bfloat16 [2048, 4096], P(('dp', 'seq'), 'tp'), parts along dimension 0, may hold values from -36 to 36
- values: bfloat16 [2048, 4096], P(('dp', 'seq'), 'tp'), parts along dimension 0, may hold values from -6 to 6
- modality: int32 [2048], P(('dp', 'seq')), parts along dimension 0, may hold values from 0 to 1, as said below
- out_weight: bfloat16 [2, 4096, 4096], P(None, 'tp'), may hold values from -0.125 to 0.125
Outputs:
- layer_out: bfloat16 [2048, 4096], P(('dp', 'seq'), 'tp'), parts along dimension 0
There are 2 independent parts, one for each index of `dp`. A program takes and returns all parts, laid end to end along the dimension named above; an argument that names none is the same for every part. Nothing has to cross between parts.
Inputs may be any that keep to these rules, and one draw needn't show every extreme that they name: `modality`: 1 marks an image token, 0 a text token.
All inputs are finite; a program needn't handle non-finite values.
Results may differ from a plain program's by a relative error of at most 0.013.
Values may be sent and summed in bfloat16 or wider, within the bound.
No kernel may reach another device: no remote copies, remote signals or barrier semaphores. Data moves between devices by JAX's collectives and lax.ppermute only.
A program may use at most 64 MiB of HBM per device.

v0:
```python
import functools

import jax
import jax.numpy as jnp
import numpy as np
from jax import lax
from jax.experimental import pallas as pl
from jax.experimental.pallas import tpu as pltpu
from jax.sharding import PartitionSpec as P


HD = 128
LANES = 128
SHARES = (1, 2)
BLOCK = 256
LOG2E = float(np.log2(np.e))
LSE_STEP = 32


def params(mib):
    return pltpu.CompilerParams(vmem_limit_bytes=mib * 1024 * 1024)


def in_hbm(x):
    return pltpu.with_memory_space_constraint(x, pltpu.HBM)


def softmax_rows(query, keys, values, masks, scale):
    scores = []
    for key, mask in zip(keys, masks):
        s = lax.dot_general(query, key, (((1,), (1,)), ((), ())), preferred_element_type=jnp.float32)
        scores.append(s if mask is None else jnp.where(mask, s, -jnp.inf))
    largest = functools.reduce(jnp.maximum, [jnp.max(s, axis=1, keepdims=True) for s in scores])
    total = None
    for s, value in zip(scores, values):
        weights = jnp.exp2((s - largest) * (scale * LOG2E)).astype(jnp.bfloat16)
        ones = jnp.ones((value.shape[0], LANES), jnp.bfloat16)
        part = jnp.dot(weights, jnp.concatenate([value, ones], axis=1), preferred_element_type=jnp.float32)
        total = part if total is None else total + part
    head = value.shape[1]
    sums = total[:, head : head + LANES]
    return total[:, :head] / sums, largest * (scale * LOG2E) + jnp.log2(sums[:, :1])


def column_copies(place_ref, offsets, w_hbm, w_ref, sems, first):
    chunk = w_ref.shape[2] // len(offsets)
    copies = []
    for i, offset in enumerate(offsets):
        start = pl.multiple_of(jnp.bitwise_xor(place_ref[1], offset) * chunk, chunk)
        src, dst = w_hbm.at[:, :, pl.ds(start, chunk)], w_ref.at[:, :, pl.ds(i * chunk, chunk)]
        copies.append(pltpu.make_async_copy(src, dst, sems.at[first + i]))
    return copies


def own_kernel(offsets, loads, place_ref, kinds_ref, q_hbm, k_hbm, v_hbm, w_hbm, *refs):
    others = len(offsets) - 1
    k_refs, v_refs = refs[:others], refs[others : 2 * others]
    out_ref, lse_ref, k_ref, v_ref, columns_ref, w_ref, q_ref, sems = refs[2 * others :]
    pairs = [(q_hbm, q_ref), (k_hbm, k_ref), (v_hbm, v_ref)]
    copies = [pltpu.make_async_copy(src, dst, sems.at[i]) for i, (src, dst) in enumerate(pairs)]
    later = column_copies(place_ref, loads, w_hbm, w_ref, sems, len(pairs))
    for copy in copies + later:
        copy.start()
    me = place_ref[0]
    rows = q_ref.shape[0]
    columns_ref[...] = jnp.broadcast_to(kinds_ref[...].astype(jnp.float32), (LANES, rows)).T
    for copy in copies:
        copy.wait()
    below = lax.broadcasted_iota(jnp.int32, (rows, rows), 0) >= lax.broadcasted_iota(jnp.int32, (rows, rows), 1)
    masks = [below if o == 0 else lax.broadcast(jnp.bitwise_xor(me, o), (rows, rows)) < me for o in offsets]
    for h in range(q_ref.shape[1] // HD):
        at = slice(h * HD, (h + 1) * HD)
        keys = [k[:, at] for k in (k_ref, *k_refs)]
        vals = [v[:, at] for v in (v_ref, *v_refs)]
        result, lse = softmax_rows(q_ref[:, at], keys, vals, masks, HD**-0.5)
        out_ref[:, at] = result.astype(out_ref.dtype)
        lse_ref[:, h : h + 1] = lse
    for copy in later:
        copy.wait()


def cross_kernel(count, half, loads, place_ref, q_ref, *refs):
    k_refs, v_refs = refs[:count], refs[count : 2 * count]
    later = []
    if loads:
        w_hbm, out_ref, w_ref, sems = refs[2 * count :]
        later = column_copies(place_ref, loads, w_hbm, w_ref, sems, 0)
    else:
        (out_ref,) = refs[2 * count :]
    for copy in later:
        copy.start()
    width = q_ref.shape[1]

    @pl.when(place_ref[0] < half)
    def _():
        out_ref[:, width:] = jnp.zeros((out_ref.shape[0], out_ref.shape[1] - width), out_ref.dtype)
        for h in range(width // HD):
            at = slice(h * HD, (h + 1) * HD)
            result, lse = softmax_rows(
                q_ref[:, at], [k[:, at] for k in k_refs], [v[:, at] for v in v_refs], [None] * count, HD**-0.5
            )
            out_ref[:, at] = result.astype(out_ref.dtype)
            for step in range(3):
                piece = lse.astype(jnp.bfloat16)
                col = width + step * LSE_STEP + h
                out_ref[:, col : col + 1] = piece
                lse = lse - piece.astype(jnp.float32)

    for copy in later:
        copy.wait()


def project(rows, image, first, w_ref, out_ref):
    chunk = out_ref.shape[1]
    block = min(chunk, BLOCK)
    nothing = jnp.zeros_like(rows)
    text_rows, image_rows = jnp.where(image, nothing, rows), jnp.where(image, rows, nothing)
    for b in range(0, chunk, block):
        at = slice(first + b, first + b + block)
        total = jnp.dot(text_rows, w_ref[0, :, at], preferred_element_type=jnp.float32)
        total += jnp.dot(image_rows, w_ref[1, :, at], preferred_element_type=jnp.float32)
        out_ref[:, b : b + block] = total.astype(out_ref.dtype)


def merge_kernel(half, lo, first, place_ref, own_ref, lse_ref, far_ref, kinds_ref, w_ref, att_ref, out_ref):
    count, width = att_ref.shape
    rows = slice(lo, lo + count)
    upper = place_ref[0] >= half
    for h in range(width // HD):
        at = slice(h * HD, (h + 1) * HD)
        cols = [width + i * LSE_STEP + h for i in range(3)]
        far_lse = sum(far_ref[:, c : c + 1].astype(jnp.float32) for c in cols)
        mine = 1.0 / (1.0 + jnp.exp2(far_lse - lse_ref[rows, h : h + 1]))
        mine = jnp.where(upper, mine, 1.0)
        mixed = own_ref[rows, at].astype(jnp.float32) * mine + far_ref[:, at].astype(jnp.float32) * (1.0 - mine)
        att_ref[:, at] = mixed.astype(att_ref.dtype)
    project(att_ref[...], kinds_ref[rows, :1] == 1, first, w_ref, out_ref)


def project_kernel(lo, first, kinds_ref, w_ref, *refs):
    att_refs, out_ref = refs[:-1], refs[-1]
    rows = jnp.concatenate([x[...] for x in att_refs], axis=0)
    project(rows, kinds_ref[lo : lo + rows.shape[0], :1] == 1, first, w_ref, out_ref)


def on_device(queries, key_rows, values, modality, out_weight):
    seq_count = lax.axis_size("seq")
    tp_count = lax.axis_size("tp")
    half = seq_count // 2
    place = jnp.stack([lax.axis_index("seq"), lax.axis_index("tp")]).astype(jnp.int32)
    rows, width = queries.shape
    chunk = out_weight.shape[2] // tp_count
    vmem = pl.BlockSpec(memory_space=pltpu.VMEM)
    smem = pl.BlockSpec(memory_space=pltpu.SMEM)
    hbm = pl.BlockSpec(memory_space=pltpu.HBM)
    edges = [0, *(rows * share // SHARES[-1] for share in SHARES)]
    parts = list(zip(edges[:-1], edges[1:]))

    def xor(count, bit):
        return [(i, i ^ bit) for i in range(count)]

    order = sorted(range(tp_count), reverse=True)
    early_loads, late_loads = order[: tp_count // 2], order[tp_count // 2 :]

    def columns_shape(loads):
        return jax.ShapeDtypeStruct((out_weight.shape[0], width, chunk * len(loads)), out_weight.dtype)

    offsets, keys, vals = [0], [key_rows], [values]
    bit = half // 2
    while bit:
        keys = keys + [lax.ppermute(x, "seq", xor(seq_count, bit)) for x in keys]
        vals = vals + [lax.ppermute(x, "seq", xor(seq_count, bit)) for x in vals]
        offsets = offsets + [o ^ bit for o in offsets]
        bit //= 2
    count = len(offsets)

    far_queries = []
    for lo, hi in parts:
        far_queries.append(lax.ppermute(queries[lo:hi], "seq", [(i + half, i) for i in range(half)]))

    own, own_lse, keys[0], vals[0], kinds, early = pl.pallas_call(
        functools.partial(own_kernel, tuple(offsets), tuple(early_loads)),
        out_shape=(
            jax.ShapeDtypeStruct((rows, width), jnp.bfloat16),
            jax.ShapeDtypeStruct((rows, LANES), jnp.float32),
            jax.ShapeDtypeStruct(key_rows.shape, key_rows.dtype),
            jax.ShapeDtypeStruct(values.shape, values.dtype),
            jax.ShapeDtypeStruct((rows, LANES), jnp.float32),
            columns_shape(early_loads),
        ),
        in_specs=[smem, vmem] + [hbm] * 4 + [vmem] * (2 * count - 2),
        out_specs=(vmem,) * 6,
        scratch_shapes=[
            pltpu.VMEM(queries.shape, queries.dtype),
            pltpu.SemaphoreType.DMA((3 + len(early_loads),)),
        ],
        compiler_params=params(8),
        name="own",
    )(place, modality.reshape(1, rows), *(in_hbm(x) for x in (queries, key_rows, values, out_weight)), *keys[1:], *vals[1:])

    far = []
    for p, (lo, hi) in enumerate(parts):
        loads = tuple(late_loads) if p == 0 else ()
        found = pl.pallas_call(
            functools.partial(cross_kernel, count, half, loads),
            out_shape=(jax.ShapeDtypeStruct((hi - lo, width + LANES), jnp.bfloat16),)
            + ((columns_shape(loads),) if loads else ()),
            in_specs=[smem] + [vmem] * (1 + 2 * count) + [hbm] * bool(loads),
            out_specs=(vmem,) * (1 + bool(loads)),
            scratch_shapes=[pltpu.SemaphoreType.DMA((len(loads),))] if loads else [],
            compiler_params=params(8),
            name="cross",
        )(place, far_queries[p], *keys, *vals, *((in_hbm(out_weight),) if loads else ()))
        if loads:
            late = found[1]
        found = found[0]
        far.append(lax.ppermute(found, "seq", [(i, i + half) for i in range(half)]))

    def columns_of(offset):
        if offset in early_loads:
            return early, early_loads.index(offset) * chunk
        return late, late_loads.index(offset) * chunk

    def merged(p, offset):
        weight, first = columns_of(offset)
        lo, hi = parts[p]
        return pl.pallas_call(
            functools.partial(merge_kernel, half, lo, first),
            out_shape=(
                jax.ShapeDtypeStruct((hi - lo, width), jnp.bfloat16),
                jax.ShapeDtypeStruct((hi - lo, chunk), jnp.bfloat16),
            ),
            in_specs=[smem] + [vmem] * 5,
            out_specs=(vmem, vmem),
            compiler_params=params(8),
            name="merge",
        )(place, own, own_lse, far[p], kinds, weight)

    def projected(lo, attended, offset):
        weight, first = columns_of(offset)
        return pl.pallas_call(
            functools.partial(project_kernel, lo, first),
            out_shape=jax.ShapeDtypeStruct((sum(x.shape[0] for x in attended), chunk), jnp.bfloat16),
            in_specs=[vmem] * (2 + len(attended)),
            out_specs=vmem,
            compiler_params=params(8),
            name="project",
        )(kinds, weight, *attended)

    def add(*terms):
        return sum(x.astype(jnp.float32) for x in terms)

    attended, sums = [], []
    for p in range(len(parts)):
        here, first = merged(p, tp_count - 1)
        attended.append(here)
        have = {tp_count - 1: first}
        for offset in range(2, tp_count - 1):
            have[offset] = projected(parts[p][0], [here], offset)
        bit, arrivals = 1, []
        while bit < tp_count:
            keep = dict(have)
            for offset in sorted(have, reverse=True):
                if offset & bit:
                    arrived = lax.ppermute(keep.pop(offset), "tp", xor(tp_count, bit))
                    if offset == bit:
                        arrivals.append(arrived)
                    else:
                        keep[offset ^ bit] = add(have[offset ^ bit], arrived).astype(jnp.bfloat16)
            have = keep
            bit *= 2
        sums.append(arrivals)
    beside = projected(0, attended, 1)
    beside = lax.ppermute(beside, "tp", xor(tp_count, 1))
    total = projected(0, attended, 0)
    total = add(total, beside)
    for arrivals in zip(*sums):
        total = add(total, jnp.concatenate(arrivals, axis=0))
    return total.astype(jnp.bfloat16)


def solution(mesh):
    in_specs = (
        P(("dp", "seq"), "tp"),
        P(("dp", "seq"), "tp"),
        P(("dp", "seq"), "tp"),
        P(("dp", "seq")),
        P(None, "tp", None),
    )
    out_specs = P(("dp", "seq"), "tp")

    return jax.shard_map(on_device, mesh=mesh, in_specs=in_specs, out_specs=out_specs, check_vma=False)
```

profile of v0, /device:TPU:0, one launch (start us, length us, event | category | flops | bytes accessed | tf_op | source)
XLA Modules:
  0.0 67.1 jit_solution(9508710572290280809)
XLA Ops:
  0.0 0.5 collective-permute-start
  0.5 0.0 collective-permute-start.1
  0.5 1.1 %fusion = (bf16[128,1024]{1,0:T(8,128)(2,1)S(1)}, bf16[128,1024]{1,0:T(8,128)(2,1)S(1)}) fusion(bf16[256,1024]{1,0:T(8,128)(2,1)} %q_hbm.1), kind=kLoop, calls=%fused_computation.4 | loop fusion | bytes 1048576 | tf_op jit(solution)/shard_map/slice | solution.py:179
  1.6 1.3 %collective-permute-start.4 = (bf16[128,1024]{1,0:T(8,128)(2,1)S(1)}, bf16[128,1024]{1,0:T(8,128)(2,1)S(1)}, u32[]{:S(2)}, u32[]{:S(2)}) collective-permute-start(bf16[128,1024]{1,0:T(8,128)(2,1)S(1)} %get-tuple-element.29), channel_id=1, source_target_pairs={{16,0},{24,8},{17,1},{25,9},{18,2},{26,10},{19,3},{27,11},{20,4},{... | collective-permute-start | bytes 786440 | tf_op jit(solution)/shard_map/ppermute | solution.py:179
  2.9 1.3 %collective-permute-start.2 = (bf16[128,1024]{1,0:T(8,128)(2,1)S(1)}, bf16[128,1024]{1,0:T(8,128)(2,1)S(1)}, u32[]{:S(2)}, u32[]{:S(2)}) collective-permute-start(bf16[128,1024]{1,0:T(8,128)(2,1)S(1)} %get-tuple-element.30), channel_id=1, source_target_pairs={{16,0},{24,8},{17,1},{25,9},{18,2},{26,10},{19,3},{27,11},{20,4},{... | collective-permute-start | bytes 786440 | tf_op jit(solution)/shard_map/ppermute | solution.py:179
  4.2 0.1 pad_add_fusion.place_ref
  4.3 0.0 collective-permute-done.refs_0_.refs_1_
  4.3 0.0 collective-permute-done.1.refs_1_.refs_3_
  4.3 0.0 copy-start
  4.3 0.7 %copy-done = s32[256]{0:T(256)S(1)} copy-done((s32[256]{0:T(256)S(1)}, s32[256]{0:T(256)}, u32[]{:S(2)}) %copy-start) | copy-done | bytes 1048
  4.9 4.5 %own.1 = (bf16[256,1024]{1,0:T(8,128)(2,1)S(1)}, f32[256,128]{1,0:T(8,128)S(1)}, bf16[256,1024]{1,0:T(8,128)(2,1)S(1)}, bf16[256,1024]{1,0:T(8,128)(2,1)S(1)}, f...) custom-call(s32[2]{0:T(128)S(1)} %pad_add_fusion.place_ref, s32[1,256]{1,0:T(1,128)S(1)} %bitcast.3, ...), custom_call_target="tpu_custom_call" | custom-call | tf_op jit(solution)/shard_map/own/pallas_call | solution.py:181
  9.5 3.5 %collective-permute-done.4.q_ref = bf16[128,1024]{1,0:T(8,128)(2,1)S(1)} collective-permute-done((bf16[128,1024]{1,0:T(8,128)(2,1)S(1)}, bf16[128,1024]{1,0:T(8,128)(2,1)S(1)}, u32[]{:S(2)}, u32[]{:S(2)}) %collective-permute-start.4) | collective-permute-done | bytes 262176 | tf_op jit(solution)/shard_map/ppermute | solution.py:179
  13.0 2.6 %cross.3 = bf16[128,1152]{1,0:T(8,128)(2,1)S(1)} custom-call(s32[2]{0:T(128)S(1)} %pad_add_fusion.place_ref, bf16[128,1024]{1,0:T(8,128)(2,1)S(1)} %collective-permute-done.4.q_ref, bf16[256,1024]{1,0:T(8,128)(2,1)S(1)} %get-tuple-element.18.refs_0_, bf16[256,1024]{1,0:T(8,128)(2,1)S(1)} %collective-permute-done.refs_0_.refs_1_, ...), custom_call_target="tpu_custom_call" | custom-call | tf_op jit(solution)/shard_map/cross/pallas_call | solution.py:204
  15.7 1.3 %collective-permute-start.5 = (bf16[128,1152]{1,0:T(8,128)(2,1)S(1)}, bf16[128,1152]{1,0:T(8,128)(2,1)S(1)}, u32[]{:S(2)}, u32[]{:S(2)}) collective-permute-start(bf16[128,1152]{1,0:T(8,128)(2,1)S(1)} %cross.3), channel_id=1, source_target_pairs={{0,16},{8,24},{1,17},{9,25},{2,18},{10,26},{3,19},{11,27},{4,20},{... | collective-permute-start | bytes 884744 | tf_op jit(solution)/shard_map/ppermute | solution.py:217
  17.0 1.0 %collective-permute-done.2.q_ref = bf16[128,1024]{1,0:T(8,128)(2,1)S(1)} collective-permute-done((bf16[128,1024]{1,0:T(8,128)(2,1)S(1)}, bf16[128,1024]{1,0:T(8,128)(2,1)S(1)}, u32[]{:S(2)}, u32[]{:S(2)}) %collective-permute-start.2) | collective-permute-done | bytes 262176 | tf_op jit(solution)/shard_map/ppermute | solution.py:179
  17.9 4.0 %cross.2 = (bf16[128,1152]{1,0:T(8,128)(2,1)S(1)}, bf16[2,1024,2048]{2,1,0:T(8,128)(2,1)S(1)}) custom-call(s32[2]{0:T(128)S(1)} %pad_add_fusion.place_ref, bf16[128,1024]{1,0:T(8,128)(2,1)S(1)} %collective-permute-done.2.q_ref, bf16[256,1024]{1,0:T(8,128)(2,1)S(1)} %get-tuple-element.18.refs_0_, bf16[256,1024]{1,0:T(8,128)(2,1)S(1)} %collective-permute-done.refs_0_.refs_1_, ...), custom_call_target="tpu_custom_call" | custom-call | tf_op jit(solution)/shard_map/cross/pallas_call | solution.py:204
  22.0 1.5 %collective-permute-start.3 = (bf16[128,1152]{1,0:T(8,128)(2,1)S(1)}, bf16[128,1152]{1,0:T(8,128)(2,1)S(1)}, u32[]{:S(2)}, u32[]{:S(2)}) collective-permute-start(bf16[128,1152]{1,0:T(8,128)(2,1)S(1)} %get-tuple-element.23), channel_id=1, source_target_pairs={{0,16},{8,24},{1,17},{9,25},{2,18},{10,26},{3,19},{11,27},{4,20},{... | collective-permute-start | bytes 884744 | tf_op jit(solution)/shard_map/ppermute | solution.py:217
  23.5 0.0 collective-permute-done.5.far_ref
  23.5 1.9 %merge.3 = (bf16[128,1024]{1,0:T(8,128)(2,1)S(1)}, bf16[128,1024]{1,0:T(8,128)(2,1)S(1)}) custom-call(s32[2]{0:T(128)S(1)} %pad_add_fusion.place_ref, bf16[256,1024]{1,0:T(8,128)(2,1)S(1)} %get-tuple-element.21.own_ref, f32[256,128]{1,0:T(8,128)S(1)} %get-tuple-element.22.lse_ref, bf16[128,1152]{1,0:T(8,128)(2,1)S(1)} %collective-permute-done.5.far_ref, ...), custom_call_target="tpu_custom_call" | custom-call | tf_op jit(solution)/shard_map/merge/pallas_call | solution.py:227
  25.3 2.5 %collective-permute-start.9 = (bf16[128,1024]{1,0:T(8,128)(2,1)S(1)}, bf16[128,1024]{1,0:T(8,128)(2,1)S(1)}, u32[]{:S(2)}, u32[]{:S(2)}) collective-permute-start(bf16[128,1024]{1,0:T(8,128)(2,1)S(1)} %get-tuple-element.28), channel_id=1, source_target_pairs={{0,2},{2,0},{4,6},{6,4},{1,3},{3,1},{5,7},{7,5},{8,10},{10,8},{12,... | collective-permute-start | bytes 786440 | tf_op jit(solution)/shard_map/ppermute | solution.py:265
  27.8 1.6 %collective-permute-done.3.far_ref = bf16[128,1152]{1,0:T(8,128)(2,1)S(1)} collective-permute-done((bf16[128,1152]{1,0:T(8,128)(2,1)S(1)}, bf16[128,1152]{1,0:T(8,128)(2,1)S(1)}, u32[]{:S(2)}, u32[]{:S(2)}) %collective-permute-start.3) | collective-permute-done | bytes 294944 | tf_op jit(solution)/shard_map/ppermute | solution.py:217
  29.4 1.9 %merge.2 = (bf16[128,1024]{1,0:T(8,128)(2,1)S(1)}, bf16[128,1024]{1,0:T(8,128)(2,1)S(1)}) custom-call(s32[2]{0:T(128)S(1)} %pad_add_fusion.place_ref, bf16[256,1024]{1,0:T(8,128)(2,1)S(1)} %get-tuple-element.21.own_ref, f32[256,128]{1,0:T(8,128)S(1)} %get-tuple-element.22.lse_ref, bf16[128,1152]{1,0:T(8,128)(2,1)S(1)} %collective-permute-done.3.far_ref, ...), custom_call_target="tpu_custom_call" | custom-call | tf_op jit(solution)/shard_map/merge/pallas_call | solution.py:227
  31.3 2.2 %collective-permute-start.7 = (bf16[128,1024]{1,0:T(8,128)(2,1)S(1)}, bf16[128,1024]{1,0:T(8,128)(2,1)S(1)}, u32[]{:S(2)}, u32[]{:S(2)}) collective-permute-start(bf16[128,1024]{1,0:T(8,128)(2,1)S(1)} %get-tuple-element.27), channel_id=1, source_target_pairs={{0,2},{2,0},{4,6},{6,4},{1,3},{3,1},{5,7},{7,5},{8,10},{10,8},{12,... | collective-permute-start | bytes 786440 | tf_op jit(solution)/shard_map/ppermute | solution.py:265
  33.5 0.8 %project.7 = bf16[128,1024]{1,0:T(8,128)(2,1)S(1)} custom-call(f32[256,128]{1,0:T(8,128)S(1)} %get-tuple-element.17.kinds_ref, bf16[2,1024,2048]{2,1,0:T(8,128)(2,1)S(1)} %get-tuple-element.24.w_ref, bf16[128,1024]{1,0:T(8,128)(2,1)S(1)} %get-tuple-element.26.refs_1_.refs_0_), custom_call_target="tpu_custom_call" | custom-call | tf_op jit(solution)/shard_map/project/pallas_call | solution.py:241
  34.3 0.8 %project.6 = bf16[128,1024]{1,0:T(8,128)(2,1)S(1)} custom-call(f32[256,128]{1,0:T(8,128)S(1)} %get-tuple-element.17.kinds_ref, bf16[2,1024,2048]{2,1,0:T(8,128)(2,1)S(1)} %get-tuple-element.24.w_ref, bf16[128,1024]{1,0:T(8,128)(2,1)S(1)} %get-tuple-element.25.refs_0_), custom_call_target="tpu_custom_call" | custom-call | tf_op jit(solution)/shard_map/project/pallas_call | solution.py:241
  35.0 1.3 %project.5 = bf16[256,1024]{1,0:T(8,128)(2,1)S(1)} custom-call(f32[256,128]{1,0:T(8,128)S(1)} %get-tuple-element.17.kinds_ref, bf16[2,1024,2048]{2,1,0:T(8,128)(2,1)S(1)} %get-tuple-element.20.w_ref, bf16[128,1024]{1,0:T(8,128)(2,1)S(1)} %get-tuple-element.25.refs_0_, bf16[128,1024]{1,0:T(8,128)(2,1)S(1)} %get-tuple-element.26.refs_1_.refs_0_), custom_call_target="tpu_custom_call" | custom-call | tf_op jit(solution)/shard_map/project/pallas_call | solution.py:241
  36.4 0.1 collective-permute-start.6
  36.4 0.0 collective-permute-done.9
  36.4 0.1 add_convert_fusion.1
  36.5 3.1 %collective-permute-start.10 = (bf16[128,1024]{1,0:T(8,128)(2,1)S(1)}, bf16[128,1024]{1,0:T(8,128)(2,1)S(1)}, u32[]{:S(2)}, u32[]{:S(2)}) collective-permute-start(bf16[128,1024]{1,0:T(8,128)(2,1)S(1)} %add_convert_fusion.1), channel_id=1, source_target_pairs={{0,4},{2,6},{4,0},{6,2},{1,5},{3,7},{5,1},{7,3},{8,12},{10,14},{12... | collective-permute-start | bytes 786440 | tf_op jit(solution)/shard_map/ppermute | solution.py:265
  39.6 9.5 %collective-permute-done.7 = bf16[128,1024]{1,0:T(8,128)(2,1)S(1)} collective-permute-done((bf16[128,1024]{1,0:T(8,128)(2,1)S(1)}, bf16[128,1024]{1,0:T(8,128)(2,1)S(1)}, u32[]{:S(2)}, u32[]{:S(2)}) %collective-permute-start.7) | collective-permute-done | bytes 262176 | tf_op jit(solution)/shard_map/ppermute | solution.py:265
  49.1 0.1 add_convert_fusion.2
  49.1 2.2 %collective-permute-start.8 = (bf16[128,1024]{1,0:T(8,128)(2,1)S(1)}, bf16[128,1024]{1,0:T(8,128)(2,1)S(1)}, u32[]{:S(2)}, u32[]{:S(2)}) collective-permute-start(bf16[128,1024]{1,0:T(8,128)(2,1)S(1)} %add_convert_fusion.2), channel_id=1, source_target_pairs={{0,4},{2,6},{4,0},{6,2},{1,5},{3,7},{5,1},{7,3},{8,12},{10,14},{12... | collective-permute-start | bytes 786440 | tf_op jit(solution)/shard_map/ppermute | solution.py:265
  51.3 1.3 %project.4 = bf16[256,1024]{1,0:T(8,128)(2,1)S(1)} custom-call(f32[256,128]{1,0:T(8,128)S(1)} %get-tuple-element.17.kinds_ref, bf16[2,1024,2048]{2,1,0:T(8,128)(2,1)S(1)} %get-tuple-element.20.w_ref, bf16[128,1024]{1,0:T(8,128)(2,1)S(1)} %get-tuple-element.25.refs_0_, bf16[128,1024]{1,0:T(8,128)(2,1)S(1)} %get-tuple-element.26.refs_1_.refs_0_), custom_call_target="tpu_custom_call" | custom-call | tf_op jit(solution)/shard_map/project/pallas_call | solution.py:241
  52.6 4.4 %collective-permute-done.10 = bf16[128,1024]{1,0:T(8,128)(2,1)S(1)} collective-permute-done((bf16[128,1024]{1,0:T(8,128)(2,1)S(1)}, bf16[128,1024]{1,0:T(8,128)(2,1)S(1)}, u32[]{:S(2)}, u32[]{:S(2)}) %collective-permute-start.10) | collective-permute-done | bytes 262176 | tf_op jit(solution)/shard_map/ppermute | solution.py:265
  57.1 9.0 %collective-permute-done.8 = bf16[128,1024]{1,0:T(8,128)(2,1)S(1)} collective-permute-done((bf16[128,1024]{1,0:T(8,128)(2,1)S(1)}, bf16[128,1024]{1,0:T(8,128)(2,1)S(1)}, u32[]{:S(2)}, u32[]{:S(2)}) %collective-permute-start.8) | collective-permute-done | bytes 262176 | tf_op jit(solution)/shard_map/ppermute | solution.py:265
  66.1 0.0 collective-permute-done.6
  66.1 1.1 %add_convert_fusion = bf16[256,1024]{1,0:T(8,128)(2,1)} fusion(bf16[256,1024]{1,0:T(8,128)(2,1)S(1)} %collective-permute-done.6, bf16[256,1024]{1,0:T(8,128)(2,1)S(1)} %project.4, bf16[128,1024]{1,0:T(8,128)(2,1)S(1)} %collective-permute-done.10, bf16[128,1024]{1,0:T(8,128)(2,1)S(1)} %collective-permute-done.8), kind=kLoop, calls=%fused_computation | loop fusion | flops 2359296 | bytes 2097152 | tf_op jit(solution)/shard_map/convert_element_type | solution.py:279
Async XLA Ops:
  0.0 4.3 %collective-permute-start = (bf16[256,1024]{1,0:T(8,128)(2,1)}, bf16[256,1024]{1,0:T(8,128)(2,1)S(1)}, u32[]{:S(2)}, u32[]{:S(2)}) collective-permute-start(bf16[256,1024]{1,0:T(8,128)(2,1)} %k_hbm.1), channel_id=1, source_target_pairs={{0,8},{8,0},{16,24},{24,16},{1,9},{9,1},{17,25},{25,17},{2,10},{10... | collective-permute-start | bytes 1572872 | tf_op jit(solution)/shard_map/ppermute | solution.py:171
  0.5 3.8 %collective-permute-start.1 = (bf16[256,1024]{1,0:T(8,128)(2,1)}, bf16[256,1024]{1,0:T(8,128)(2,1)S(1)}, u32[]{:S(2)}, u32[]{:S(2)}) collective-permute-start(bf16[256,1024]{1,0:T(8,128)(2,1)} %v_hbm.1), channel_id=1, source_target_pairs={{0,8},{8,0},{16,24},{24,16},{1,9},{9,1},{17,25},{25,17},{2,10},{10... | collective-permute-start | bytes 1572872 | tf_op jit(solution)/shard_map/ppermute | solution.py:172
  1.6 11.4 %collective-permute-start.4 = (bf16[128,1024]{1,0:T(8,128)(2,1)S(1)}, bf16[128,1024]{1,0:T(8,128)(2,1)S(1)}, u32[]{:S(2)}, u32[]{:S(2)}) collective-permute-start(bf16[128,1024]{1,0:T(8,128)(2,1)S(1)} %get-tuple-element.29), channel_id=1, source_target_pairs={{16,0},{24,8},{17,1},{25,9},{18,2},{26,10},{19,3},{27,11},{20,4},{... | collective-permute-start | bytes 786440 | tf_op jit(solution)/shard_map/ppermute | solution.py:179
  2.9 15.1 %collective-permute-start.2 = (bf16[128,1024]{1,0:T(8,128)(2,1)S(1)}, bf16[128,1024]{1,0:T(8,128)(2,1)S(1)}, u32[]{:S(2)}, u32[]{:S(2)}) collective-permute-start(bf16[128,1024]{1,0:T(8,128)(2,1)S(1)} %get-tuple-element.30), channel_id=1, source_target_pairs={{16,0},{24,8},{17,1},{25,9},{18,2},{26,10},{19,3},{27,11},{20,4},{... | collective-permute-start | bytes 786440 | tf_op jit(solution)/shard_map/ppermute | solution.py:179
  4.3 0.7 %copy-start = (s32[256]{0:T(256)S(1)}, s32[256]{0:T(256)}, u32[]{:S(2)}) copy-start(s32[256]{0:T(256)} %param.8) | copy-start | bytes 3076
  15.7 7.8 %collective-permute-start.5 = (bf16[128,1152]{1,0:T(8,128)(2,1)S(1)}, bf16[128,1152]{1,0:T(8,128)(2,1)S(1)}, u32[]{:S(2)}, u32[]{:S(2)}) collective-permute-start(bf16[128,1152]{1,0:T(8,128)(2,1)S(1)} %cross.3), channel_id=1, source_target_pairs={{0,16},{8,24},{1,17},{9,25},{2,18},{10,26},{3,19},{11,27},{4,20},{... | collective-permute-start | bytes 884744 | tf_op jit(solution)/shard_map/ppermute | solution.py:217
  22.0 7.4 %collective-permute-start.3 = (bf16[128,1152]{1,0:T(8,128)(2,1)S(1)}, bf16[128,1152]{1,0:T(8,128)(2,1)S(1)}, u32[]{:S(2)}, u32[]{:S(2)}) collective-permute-start(bf16[128,1152]{1,0:T(8,128)(2,1)S(1)} %get-tuple-element.23), channel_id=1, source_target_pairs={{0,16},{8,24},{1,17},{9,25},{2,18},{10,26},{3,19},{11,27},{4,20},{... | collective-permute-start | bytes 884744 | tf_op jit(solution)/shard_map/ppermute | solution.py:217
  25.3 11.1 %collective-permute-start.9 = (bf16[128,1024]{1,0:T(8,128)(2,1)S(1)}, bf16[128,1024]{1,0:T(8,128)(2,1)S(1)}, u32[]{:S(2)}, u32[]{:S(2)}) collective-permute-start(bf16[128,1024]{1,0:T(8,128)(2,1)S(1)} %get-tuple-element.28), channel_id=1, source_target_pairs={{0,2},{2,0},{4,6},{6,4},{1,3},{3,1},{5,7},{7,5},{8,10},{10,8},{12,... | collective-permute-start | bytes 786440 | tf_op jit(solution)/shard_map/ppermute | solution.py:265
  31.3 17.8 %collective-permute-start.7 = (bf16[128,1024]{1,0:T(8,128)(2,1)S(1)}, bf16[128,1024]{1,0:T(8,128)(2,1)S(1)}, u32[]{:S(2)}, u32[]{:S(2)}) collective-permute-start(bf16[128,1024]{1,0:T(8,128)(2,1)S(1)} %get-tuple-element.27), channel_id=1, source_target_pairs={{0,2},{2,0},{4,6},{6,4},{1,3},{3,1},{5,7},{7,5},{8,10},{10,8},{12,... | collective-permute-start | bytes 786440 | tf_op jit(solution)/shard_map/ppermute | solution.py:265
  36.4 29.7 %collective-permute-start.6 = (bf16[256,1024]{1,0:T(8,128)(2,1)S(1)}, bf16[256,1024]{1,0:T(8,128)(2,1)S(1)}, u32[]{:S(2)}, u32[]{:S(2)}) collective-permute-start(bf16[256,1024]{1,0:T(8,128)(2,1)S(1)} %project.5), channel_id=1, source_target_pairs={{0,2},{2,0},{4,6},{6,4},{1,3},{3,1},{5,7},{7,5},{8,10},{10,8},{12,... | collective-permute-start | bytes 1572872 | tf_op jit(solution)/shard_map/ppermute | solution.py:274
  36.5 20.6 %collective-permute-start.10 = (bf16[128,1024]{1,0:T(8,128)(2,1)S(1)}, bf16[128,1024]{1,0:T(8,128)(2,1)S(1)}, u32[]{:S(2)}, u32[]{:S(2)}) collective-permute-start(bf16[128,1024]{1,0:T(8,128)(2,1)S(1)} %add_convert_fusion.1), channel_id=1, source_target_pairs={{0,4},{2,6},{4,0},{6,2},{1,5},{3,7},{5,1},{7,3},{8,12},{10,14},{12... | collective-permute-start | bytes 786440 | tf_op jit(solution)/shard_map/ppermute | solution.py:265
  49.1 16.9 %collective-permute-start.8 = (bf16[128,1024]{1,0:T(8,128)(2,1)S(1)}, bf16[128,1024]{1,0:T(8,128)(2,1)S(1)}, u32[]{:S(2)}, u32[]{:S(2)}) collective-permute-start(bf16[128,1024]{1,0:T(8,128)(2,1)S(1)} %add_convert_fusion.2), channel_id=1, source_target_pairs={{0,4},{2,6},{4,0},{6,2},{1,5},{3,7},{5,1},{7,3},{8,12},{10,14},{12... | collective-permute-start | bytes 786440 | tf_op jit(solution)/shard_map/ppermute | solution.py:265
where the time goes:
time: 67.4 us; the launch traced here: 67.1 us
  waiting for transfers between devices  29 us (43%)
  Pallas kernels  19.1 us (28%)
  starting transfers between devices  15.9 us (24%)
  local copies, waits for them, and re-layouts  1.74 us (3%)
  other arithmetic  1.27 us (2%)
    ppermute x4, waiting for transfers between devices, on_device(): arrived = lax.ppermute(keep.pop(offset), 'tp', xor(tp_count, bit))  22.9 us
    ppermute x4, starting transfers between devices, on_device(): arrived = lax.ppermute(keep.pop(offset), 'tp', xor(tp_count, bit))  9.95 us
    pallas_call x2, Pallas kernels, on_device(): pl.pallas_call(functools.partial(cross_kernel, count, half, loads), out_s...  6.69 us
    pallas_call x1, Pallas kernels, on_device(): pl.pallas_call(functools.partial(own_kernel, tuple(offsets), tuple(early_...  4.51 us
    ppermute x2, waiting for transfers between devices, on_device(): lax.ppermute(queries[lo:hi], 'seq', [(i + half, i) for i in range(half)])  4.5 us
    pallas_call x4, Pallas kernels, projected(): pl.pallas_call(functools.partial(project_kernel, lo, first), out_shape=ja...  4.17 us
    pallas_call x2, Pallas kernels, merged(): pl.pallas_call(functools.partial(merge_kernel, half, lo, first), out_shap...  3.71 us
    ppermute x2, starting transfers between devices, on_device(): far.append(lax.ppermute(found, 'seq', [(i, i + half) for i in range(half)]))  2.77 us
  transfers between devices with their start and end apart: 11, of which 6 were waited for; matrix products, arithmetic and copies ran while one was open for 2% of the time, Pallas kernels for 28%

commit v1 on v0

--- a/solution.py
+++ b/solution.py
@@ -14,7 +14,6 @@
 SHARES = (1, 2)
 BLOCK = 256
 LOG2E = float(np.log2(np.e))
-LSE_STEP = 32
 
 
 def params(mib):
@@ -79,7 +78,24 @@
         copy.wait()
 
 
-def cross_kernel(count, half, loads, place_ref, q_ref, *refs):
+def put_lse(found, h, shipped, lse):
+    lanes = lax.broadcasted_iota(jnp.int32, found.shape, 1)
+    return jnp.where(lanes % shipped == h, lse, found)
+
+
+def lse_terms(found, shipped):
+    lanes = lax.broadcasted_iota(jnp.int32, found.shape, 1)
+    high = found.astype(jnp.bfloat16).astype(jnp.float32)
+    middle = (found - high).astype(jnp.bfloat16).astype(jnp.float32)
+    low = found - high - middle
+    return jnp.where(lanes < shipped, high, jnp.where(lanes < 2 * shipped, middle, low))
+
+
+def lse_rows(shipped):
+    return -(-3 * shipped // 16) * 16
+
+
+def cross_kernel(count, half, skip, loads, place_ref, q_ref, *refs):
     k_refs, v_refs = refs[:count], refs[count : 2 * count]
     later = []
     if loads:
@@ -89,25 +105,51 @@
         (out_ref,) = refs[2 * count :]
     for copy in later:
         copy.start()
-    width = q_ref.shape[1]
+    rows, width = q_ref.shape
+    shipped = width // HD
 
     @pl.when(place_ref[0] < half)
     def _():
-        out_ref[:, width:] = jnp.zeros((out_ref.shape[0], out_ref.shape[1] - width), out_ref.dtype)
+        found = jnp.zeros((rows, LANES), jnp.float32)
+        for h in range(width // HD):
+            at, there = slice(h * HD, (h + 1) * HD), slice(skip + h * HD, skip + (h + 1) * HD)
+            result, lse = softmax_rows(
+                q_ref[:, at], [k[:, there] for k in k_refs], [v[:, there] for v in v_refs], [None] * count, HD**-0.5
+            )
+            out_ref[:rows, at] = result.astype(out_ref.dtype)
+            found = put_lse(found, h, shipped, lse)
+        extra = out_ref.shape[0] - rows
+        out_ref[rows:, :rows] = lse_terms(found, shipped).T[:extra].astype(out_ref.dtype)
+
+    for copy in later:
+        copy.wait()
+
+
+def mix(own, own_lse, far, far_lse, out_dtype):
+    mine = 1.0 / (1.0 + jnp.exp2(far_lse - own_lse))
+    return (own.astype(jnp.float32) * mine + far.astype(jnp.float32) * (1.0 - mine)).astype(out_dtype)
+
+
+def far_kernel(count, half, place_ref, q_hbm, own_ref, lse_ref, *refs):
+    k_refs, v_refs = refs[:count], refs[count : 2 * count]
+    out_ref, q_ref, sem = refs[2 * count :]
+    width = out_ref.shape[1]
+    copy = pltpu.make_async_copy(q_hbm.at[:, :width], q_ref, sem)
+    copy.start()
+    copy.wait()
+
+    @pl.when(place_ref[0] < half)
+    def _():
+        out_ref[...] = own_ref[:, :width]
+
+    @pl.when(place_ref[0] >= half)
+    def _():
         for h in range(width // HD):
             at = slice(h * HD, (h + 1) * HD)
             result, lse = softmax_rows(
                 q_ref[:, at], [k[:, at] for k in k_refs], [v[:, at] for v in v_refs], [None] * count, HD**-0.5
             )
-            out_ref[:, at] = result.astype(out_ref.dtype)
-            for step in range(3):
-                piece = lse.astype(jnp.bfloat16)
-                col = width + step * LSE_STEP + h
-                out_ref[:, col : col + 1] = piece
-                lse = lse - piece.astype(jnp.float32)
-
-    for copy in later:
-        copy.wait()
+            out_ref[:, at] = mix(own_ref[:, at], lse_ref[:, h : h + 1], result, lse, out_ref.dtype)
 
 
 def project(rows, image, first, w_ref, out_ref):
@@ -122,18 +164,28 @@
         out_ref[:, b : b + block] = total.astype(out_ref.dtype)
 
 
-def merge_kernel(half, lo, first, place_ref, own_ref, lse_ref, far_ref, kinds_ref, w_ref, att_ref, out_ref):
-    count, width = att_ref.shape
+def merge_kernel(half, lo, first, place_ref, own_ref, lse_ref, near_ref, back_ref, kinds_ref, w_ref, att_ref, out_ref):
+    count, _ = att_ref.shape
     rows = slice(lo, lo + count)
-    upper = place_ref[0] >= half
-    for h in range(width // HD):
-        at = slice(h * HD, (h + 1) * HD)
-        cols = [width + i * LSE_STEP + h for i in range(3)]
-        far_lse = sum(far_ref[:, c : c + 1].astype(jnp.float32) for c in cols)
-        mine = 1.0 / (1.0 + jnp.exp2(far_lse - lse_ref[rows, h : h + 1]))
-        mine = jnp.where(upper, mine, 1.0)
-        mixed = own_ref[rows, at].astype(jnp.float32) * mine + far_ref[:, at].astype(jnp.float32) * (1.0 - mine)
-        att_ref[:, at] = mixed.astype(att_ref.dtype)
+    skip, shipped = near_ref.shape[1], back_ref.shape[1] // HD
+    att_ref[:, :skip] = near_ref[rows, :]
+
+    @pl.when(place_ref[0] < half)
+    def _():
+        att_ref[:, skip:] = own_ref[rows, skip:]
+
+    @pl.when(place_ref[0] >= half)
+    def _():
+        terms = back_ref[own_ref.shape[0] :, rows].astype(jnp.float32)
+        terms = jnp.concatenate([terms, jnp.zeros((LANES - terms.shape[0], count), jnp.float32)], axis=0).T
+        for h in range(shipped):
+            at, there = slice(h * HD, (h + 1) * HD), slice(skip + h * HD, skip + (h + 1) * HD)
+            far_lse = sum(terms[:, c : c + 1] for c in (h, shipped + h, 2 * shipped + h))
+            own_h = skip // HD + h
+            att_ref[:, there] = mix(
+                own_ref[rows, there], lse_ref[rows, own_h : own_h + 1], back_ref[rows, at], far_lse, att_ref.dtype
+            )
+
     project(att_ref[...], kinds_ref[rows, :1] == 1, first, w_ref, out_ref)
 
 
@@ -174,9 +226,20 @@
         bit //= 2
     count = len(offsets)
 
-    far_queries = []
-    for lo, hi in parts:
-        far_queries.append(lax.ppermute(queries[lo:hi], "seq", [(i + half, i) for i in range(half)]))
+    heads = width // HD
+    shipped = heads // 2
+    skip = (heads - shipped) * HD
+    up = [(i, i + half) for i in range(half)]
+    met = lax.ppermute(
+        jnp.where(place[0] >= half, queries[:, skip:], key_rows[:, : width - skip]), "seq", xor(seq_count, half)
+    )
+    far_keys = [met]
+    far_vals = [lax.ppermute(values[:, :skip], "seq", up)]
+    bit = half // 2
+    while bit:
+        far_keys = far_keys + [lax.ppermute(x, "seq", xor(seq_count, bit)) for x in far_keys]
+        far_vals = far_vals + [lax.ppermute(x, "seq", xor(seq_count, bit)) for x in far_vals]
+        bit //= 2
 
     own, own_lse, keys[0], vals[0], kinds, early = pl.pallas_call(
         functools.partial(own_kernel, tuple(offsets), tuple(early_loads)),
@@ -198,23 +261,26 @@
         name="own",
     )(place, modality.reshape(1, rows), *(in_hbm(x) for x in (queries, key_rows, values, out_weight)), *keys[1:], *vals[1:])
 
-    far = []
-    for p, (lo, hi) in enumerate(parts):
-        loads = tuple(late_loads) if p == 0 else ()
-        found = pl.pallas_call(
-            functools.partial(cross_kernel, count, half, loads),
-            out_shape=(jax.ShapeDtypeStruct((hi - lo, width + LANES), jnp.bfloat16),)
-            + ((columns_shape(loads),) if loads else ()),
-            in_specs=[smem] + [vmem] * (1 + 2 * count) + [hbm] * bool(loads),
-            out_specs=(vmem,) * (1 + bool(loads)),
-            scratch_shapes=[pltpu.SemaphoreType.DMA((len(loads),))] if loads else [],
-            compiler_params=params(8),
-            name="cross",
-        )(place, far_queries[p], *keys, *vals, *((in_hbm(out_weight),) if loads else ()))
-        if loads:
-            late = found[1]
-        found = found[0]
-        far.append(lax.ppermute(found, "seq", [(i, i + half) for i in range(half)]))
+    loads = tuple(late_loads)
+    found, late = pl.pallas_call(
+        functools.partial(cross_kernel, count, half, skip, loads),
+        out_shape=(jax.ShapeDtypeStruct((rows + lse_rows(shipped), width - skip), jnp.bfloat16), columns_shape(loads)),
+        in_specs=[smem] + [vmem] * (1 + 2 * count) + [hbm],
+        out_specs=(vmem, vmem),
+        scratch_shapes=[pltpu.SemaphoreType.DMA((len(loads),))],
+        compiler_params=params(8),
+        name="cross",
+    )(place, met, *keys, *vals, in_hbm(out_weight))
+    back = lax.ppermute(found, "seq", up)
+    near = pl.pallas_call(
+        functools.partial(far_kernel, count, half),
+        out_shape=jax.ShapeDtypeStruct((rows, skip), jnp.bfloat16),
+        in_specs=[smem, hbm] + [vmem] * (2 + 2 * count),
+        out_specs=vmem,
+        scratch_shapes=[pltpu.VMEM((rows, skip), jnp.bfloat16), pltpu.SemaphoreType.DMA],
+        compiler_params=params(8),
+        name="far",
+    )(place, in_hbm(queries), own, own_lse, *far_keys, *far_vals)
 
     def columns_of(offset):
         if offset in early_loads:
@@ -230,11 +296,11 @@
                 jax.ShapeDtypeStruct((hi - lo, width), jnp.bfloat16),
                 jax.ShapeDtypeStruct((hi - lo, chunk), jnp.bfloat16),
             ),
-            in_specs=[smem] + [vmem] * 5,
+            in_specs=[smem] + [vmem] * 6,
             out_specs=(vmem, vmem),
             compiler_params=params(8),
             name="merge",
-        )(place, own, own_lse, far[p], kinds, weight)
+        )(place, own, own_lse, near, back, kinds, weight)
 
     def projected(lo, attended, offset):
         weight, first = columns_of(offset)

time: 67.4 us -> 66.5 us (0.987)
  starting transfers between devices: 15.9 us -> 20.4 us
  waiting for transfers between devices: 29 us -> 24.8 us
  Pallas kernels: 19.1 us -> 16.9 us
  other arithmetic: 1.27 us -> 2.33 us
    ppermute x4, waiting for transfers between devices: 22.9 us -> 15.2 us  [on_device(): arrived = lax.ppermute(keep.pop(offset), 'tp', xor(tp_count, bit))]
    ppermute x1, waiting for transfers between devices: 0.01 us -> 7.16 us  [on_device(): beside = lax.ppermute(beside, 'tp', xor(tp_count, 1))]
    ppermute x4 -> x5, waiting for transfers between devices: 6.08 us -> 2.37 us  [the longest x2 1.4 us: on_device(): lax.ppermute(x, 'seq', xor(seq_count, bit))]
    ppermute x4 -> x5, starting transfers between devices: 5.36 us -> 8.44 us  [the longest x1 3.06 us: on_device(): lax.ppermute(jnp.where(place[0] >= half, queries[:, skip:], key_rows[:, :...]
    ppermute x1, starting transfers between devices: 0.08 us -> 1.84 us  [on_device(): beside = lax.ppermute(beside, 'tp', xor(tp_count, 1))]
    pallas_call x2, Pallas kernels: 6.69 us -> 5.56 us  [the longest x1 4.04 us: on_device(): pl.pallas_call(functools.partial(cross_kernel, count, half, skip, loads),...]
    select_n x0 -> x1, other arithmetic: none -> 1.06 us  [on_device(): jnp.where(place[0] >= half, queries[:, skip:], key_rows[:, :width - skip])]
    pallas_call x2, Pallas kernels: 3.71 us -> 2.68 us  [merged(): pl.pallas_call(functools.partial(merge_kernel, half, lo, first), out_shap...]
  transfers between devices with their start and end apart: 11 -> 12, of which waited for: 6 -> 7; matrix products, arithmetic and copies ran while one was open for 2% -> 3% of each run, Pallas kernels for 28% -> 24%
where the time goes in v1:
time: 66.5 us; the launch traced here: 66.3 us
  waiting for transfers between devices  24.8 us (37%)
  starting transfers between devices  20.4 us (31%)
  Pallas kernels  16.9 us (25%)
  other arithmetic  2.33 us (4%)
  local copies, waits for them, and re-layouts  1.65 us (2%)
    ppermute x4, waiting for transfers between devices, on_device(): arrived = lax.ppermute(keep.pop(offset), 'tp', xor(tp_count, bit))  15.2 us
    ppermute x4, starting transfers between devices, on_device(): arrived = lax.ppermute(keep.pop(offset), 'tp', xor(tp_count, bit))  9.64 us
    ppermute x1, waiting for transfers between devices, on_device(): beside = lax.ppermute(beside, 'tp', xor(tp_count, 1))  7.16 us
    pallas_call x1, Pallas kernels, on_device(): pl.pallas_call(functools.partial(own_kernel, tuple(offsets), tuple(early_...  4.51 us
    pallas_call x4, Pallas kernels, projected(): pl.pallas_call(functools.partial(project_kernel, lo, first), out_shape=ja...  4.19 us
    pallas_call x1, Pallas kernels, on_device(): pl.pallas_call(functools.partial(cross_kernel, count, half, skip, loads),...  4.04 us
    ppermute x1, starting transfers between devices, on_device(): lax.ppermute(jnp.where(place[0] >= half, queries[:, skip:], key_rows[:, :...  3.06 us
    ppermute x1, starting transfers between devices, on_device(): back = lax.ppermute(found, 'seq', up)  2.88 us
  transfers between devices with their start and end apart: 12, of which 7 were waited for; matrix products, arithmetic and copies ran while one was open for 3% of the time, Pallas kernels for 24%

profile of v1, /device:TPU:0, one launch (start us, length us, event | category | flops | bytes accessed | tf_op | source)
XLA Modules:
  0.0 66.3 jit_solution(5367351336945503670)
XLA Ops:
  0.0 0.5 collective-permute-start
  0.5 0.0 collective-permute-start.1
  0.5 1.1 %slice_select_fusion = bf16[256,512]{1,0:T(8,128)(2,1)S(1)} fusion(bf16[256,1024]{1,0:T(8,128)(2,1)} %k_hbm.1, bf16[256,1024]{1,0:T(8,128)(2,1)} %q_hbm.3, pred[]{:T(512)S(6)} %ge.3), kind=kLoop, calls=%fused_computation.3 | loop fusion | flops 131072 | bytes 786433 | tf_op jit(solution)/shard_map/jit(_where)/select_n | solution.py:234
  1.6 3.1 %collective-permute-start.2 = (bf16[256,512]{1,0:T(8,128)(2,1)S(1)}, bf16[256,512]{1,0:T(8,128)(2,1)S(1)}, u32[]{:S(2)}, u32[]{:S(2)}) collective-permute-start(bf16[256,512]{1,0:T(8,128)(2,1)S(1)} %slice_select_fusion), channel_id=1, source_target_pairs={{0,16},{8,24},{16,0},{24,8},{1,17},{9,25},{17,1},{25,9},{2,18},{10... | collective-permute-start | bytes 786440 | tf_op jit(solution)/shard_map/ppermute | solution.py:233
  4.6 1.0 %slice.11 = bf16[256,512]{1,0:T(8,128)(2,1)S(1)} slice(bf16[256,1024]{1,0:T(8,128)(2,1)} %v_hbm.1), slice={[0:256], [0:512]} | slice | bytes 524288 | tf_op jit(solution)/shard_map/slice | solution.py:237
  5.6 1.9 %collective-permute-start.4 = (bf16[256,512]{1,0:T(8,128)(2,1)S(1)}, bf16[256,512]{1,0:T(8,128)(2,1)S(1)}, u32[]{:S(2)}, u32[]{:S(2)}) collective-permute-start(bf16[256,512]{1,0:T(8,128)(2,1)S(1)} %slice.11), channel_id=1, source_target_pairs={{0,16},{8,24},{1,17},{9,25},{2,18},{10,26},{3,19},{11,27},{4,20},{... | collective-permute-start | bytes 786440 | tf_op jit(solution)/shard_map/ppermute | solution.py:237
  7.6 0.1 pad_add_fusion.place_ref
  7.6 0.0 collective-permute-done.refs_0_.refs_1_
  7.6 0.0 collective-permute-done.1.refs_1_.refs_3_
  7.6 0.0 copy-start
  7.6 0.7 %copy-done = s32[256]{0:T(256)S(1)} copy-done((s32[256]{0:T(256)S(1)}, s32[256]{0:T(256)}, u32[]{:S(2)}) %copy-start) | copy-done | bytes 1048
  8.3 4.5 %own.1 = (bf16[256,1024]{1,0:T(8,128)(2,1)S(1)}, f32[256,128]{1,0:T(8,128)S(1)}, bf16[256,1024]{1,0:T(8,128)(2,1)S(1)}, bf16[256,1024]{1,0:T(8,128)(2,1)S(1)}, f...) custom-call(s32[2]{0:T(128)S(1)} %pad_add_fusion.place_ref, s32[1,256]{1,0:T(1,128)S(1)} %bitcast.3, ...), custom_call_target="tpu_custom_call" | custom-call | tf_op jit(solution)/shard_map/own/pallas_call | solution.py:244
  12.8 0.0 collective-permute-done.2.q_ref.refs_0_
  12.8 4.0 %cross.1 = (bf16[272,512]{1,0:T(8,128)(2,1)S(1)}, bf16[2,1024,2048]{2,1,0:T(8,128)(2,1)S(1)}) custom-call(s32[2]{0:T(128)S(1)} %pad_add_fusion.place_ref, bf16[256,512]{1,0:T(8,128)(2,1)S(1)} %collective-permute-done.2.q_ref.refs_0_, bf16[256,1024]{1,0:T(8,128)(2,1)S(1)} %get-tuple-element.18.refs_0_, ...), custom_call_target="tpu_custom_call" | custom-call | tf_op jit(solution)/shard_map/cross/pallas_call | solution.py:265
  16.9 2.9 %collective-permute-start.6 = (bf16[272,512]{1,0:T(8,128)(2,1)S(1)}, bf16[272,512]{1,0:T(8,128)(2,1)S(1)}, u32[]{:S(2)}, u32[]{:S(2)}) collective-permute-start(bf16[272,512]{1,0:T(8,128)(2,1)S(1)} %get-tuple-element.23), channel_id=1, source_target_pairs={{0,16},{8,24},{1,17},{9,25},{2,18},{10,26},{3,19},{11,27},{4,20},{... | collective-permute-start | bytes 835592 | tf_op jit(solution)/shard_map/ppermute | solution.py:274
  19.8 0.1 collective-permute-start.3
  19.9 0.0 collective-permute-done.4.refs_2_
  19.9 0.5 collective-permute-start.5
  20.4 1.0 %collective-permute-done.3.refs_1_ = bf16[256,512]{1,0:T(8,128)(2,1)S(1)} collective-permute-done((bf16[256,512]{1,0:T(8,128)(2,1)S(1)}, bf16[256,512]{1,0:T(8,128)(2,1)S(1)}, u32[]{:S(2)}, u32[]{:S(2)}) %collective-permute-start.3) | collective-permute-done | bytes 262176 | tf_op jit(solution)/shard_map/ppermute | solution.py:240
  21.4 0.4 collective-permute-done.5.refs_3_
  21.8 1.5 %far.1.near_ref = bf16[256,512]{1,0:T(8,128)(2,1)S(1)} custom-call(s32[2]{0:T(128)S(1)} %pad_add_fusion.place_ref, bf16[256,1024]{1,0:T(8,128)(2,1)} %q_hbm.3, bf16[256,1024]{1,0:T(8,128)(2,1)S(1)} %get-tuple-element.21.own_ref, f32[256,128]{1,0:T(8,128)S(1)} %get-tuple-element.22.lse_ref, bf16[256,512]{1,0:T(8,128)(2,1)S(1)} %collective-permute-done.2.q_ref.refs_0_, ...), custom_call_target="tpu_custom_call" | custom-call | tf_op jit(solution)/shard_map/far/pallas_call | solution.py:275
  23.3 1.0 %collective-permute-done.6.back_ref = bf16[272,512]{1,0:T(8,128)(2,1)S(1)} collective-permute-done((bf16[272,512]{1,0:T(8,128)(2,1)S(1)}, bf16[272,512]{1,0:T(8,128)(2,1)S(1)}, u32[]{:S(2)}, u32[]{:S(2)}) %collective-permute-start.6) | collective-permute-done | bytes 278560 | tf_op jit(solution)/shard_map/ppermute | solution.py:274
  24.3 1.3 %merge.3 = (bf16[128,1024]{1,0:T(8,128)(2,1)S(1)}, bf16[128,1024]{1,0:T(8,128)(2,1)S(1)}) custom-call(s32[2]{0:T(128)S(1)} %pad_add_fusion.place_ref, bf16[256,1024]{1,0:T(8,128)(2,1)S(1)} %get-tuple-element.21.own_ref, f32[256,128]{1,0:T(8,128)S(1)} %get-tuple-element.22.lse_ref, bf16[256,512]{1,0:T(8,128)(2,1)S(1)} %far.1.near_ref, ...), custom_call_target="tpu_custom_call" | custom-call | tf_op jit(solution)/shard_map/merge/pallas_call | solution.py:293
  25.6 1.9 %collective-permute-start.10 = (bf16[128,1024]{1,0:T(8,128)(2,1)S(1)}, bf16[128,1024]{1,0:T(8,128)(2,1)S(1)}, u32[]{:S(2)}, u32[]{:S(2)}) collective-permute-start(bf16[128,1024]{1,0:T(8,128)(2,1)S(1)} %get-tuple-element.28), channel_id=1, source_target_pairs={{0,2},{2,0},{4,6},{6,4},{1,3},{3,1},{5,7},{7,5},{8,10},{10,8},{12,... | collective-permute-start | bytes 786440 | tf_op jit(solution)/shard_map/ppermute | solution.py:331
  27.5 1.3 %merge.2 = (bf16[128,1024]{1,0:T(8,128)(2,1)S(1)}, bf16[128,1024]{1,0:T(8,128)(2,1)S(1)}) custom-call(s32[2]{0:T(128)S(1)} %pad_add_fusion.place_ref, bf16[256,1024]{1,0:T(8,128)(2,1)S(1)} %get-tuple-element.21.own_ref, f32[256,128]{1,0:T(8,128)S(1)} %get-tuple-element.22.lse_ref, bf16[256,512]{1,0:T(8,128)(2,1)S(1)} %far.1.near_ref, ...), custom_call_target="tpu_custom_call" | custom-call | tf_op jit(solution)/shard_map/merge/pallas_call | solution.py:293
  28.8 0.3 collective-permute-start.8
  29.1 0.8 %project.7 = bf16[128,1024]{1,0:T(8,128)(2,1)S(1)} custom-call(f32[256,128]{1,0:T(8,128)S(1)} %get-tuple-element.17.kinds_ref, bf16[2,1024,2048]{2,1,0:T(8,128)(2,1)S(1)} %get-tuple-element.24.w_ref, bf16[128,1024]{1,0:T(8,128)(2,1)S(1)} %get-tuple-element.26.refs_1_.refs_0_), custom_call_target="tpu_custom_call" | custom-call | tf_op jit(solution)/shard_map/project/pallas_call | solution.py:307
  29.9 0.8 %project.6 = bf16[128,1024]{1,0:T(8,128)(2,1)S(1)} custom-call(f32[256,128]{1,0:T(8,128)S(1)} %get-tuple-element.17.kinds_ref, bf16[2,1024,2048]{2,1,0:T(8,128)(2,1)S(1)} %get-tuple-element.24.w_ref, bf16[128,1024]{1,0:T(8,128)(2,1)S(1)} %get-tuple-element.25.refs_0_), custom_call_target="tpu_custom_call" | custom-call | tf_op jit(solution)/shard_map/project/pallas_call | solution.py:307
  30.7 1.3 %project.5 = bf16[256,1024]{1,0:T(8,128)(2,1)S(1)} custom-call(f32[256,128]{1,0:T(8,128)S(1)} %get-tuple-element.17.kinds_ref, bf16[2,1024,2048]{2,1,0:T(8,128)(2,1)S(1)} %get-tuple-element.20.w_ref, bf16[128,1024]{1,0:T(8,128)(2,1)S(1)} %get-tuple-element.25.refs_0_, bf16[128,1024]{1,0:T(8,128)(2,1)S(1)} %get-tuple-element.26.refs_1_.refs_0_), custom_call_target="tpu_custom_call" | custom-call | tf_op jit(solution)/shard_map/project/pallas_call | solution.py:307
  32.0 1.8 %collective-permute-start.7 = (bf16[256,1024]{1,0:T(8,128)(2,1)S(1)}, bf16[256,1024]{1,0:T(8,128)(2,1)S(1)}, u32[]{:S(2)}, u32[]{:S(2)}) collective-permute-start(bf16[256,1024]{1,0:T(8,128)(2,1)S(1)} %project.5), channel_id=1, source_target_pairs={{0,2},{2,0},{4,6},{6,4},{1,3},{3,1},{5,7},{7,5},{8,10},{10,8},{12,... | collective-permute-start | bytes 1572872 | tf_op jit(solution)/shard_map/ppermute | solution.py:340
  33.9 1.0 %collective-permute-done.10 = bf16[128,1024]{1,0:T(8,128)(2,1)S(1)} collective-permute-done((bf16[128,1024]{1,0:T(8,128)(2,1)S(1)}, bf16[128,1024]{1,0:T(8,128)(2,1)S(1)}, u32[]{:S(2)}, u32[]{:S(2)}) %collective-permute-start.10) | collective-permute-done | bytes 262176 | tf_op jit(solution)/shard_map/ppermute | solution.py:331
  34.9 0.1 add_convert_fusion.1
  34.9 2.9 %collective-permute-start.11 = (bf16[128,1024]{1,0:T(8,128)(2,1)S(1)}, bf16[128,1024]{1,0:T(8,128)(2,1)S(1)}, u32[]{:S(2)}, u32[]{:S(2)}) collective-permute-start(bf16[128,1024]{1,0:T(8,128)(2,1)S(1)} %add_convert_fusion.1), channel_id=1, source_target_pairs={{0,4},{2,6},{4,0},{6,2},{1,5},{3,7},{5,1},{7,3},{8,12},{10,14},{12... | collective-permute-start | bytes 786440 | tf_op jit(solution)/shard_map/ppermute | solution.py:331
  37.8 8.3 %collective-permute-done.8 = bf16[128,1024]{1,0:T(8,128)(2,1)S(1)} collective-permute-done((bf16[128,1024]{1,0:T(8,128)(2,1)S(1)}, bf16[128,1024]{1,0:T(8,128)(2,1)S(1)}, u32[]{:S(2)}, u32[]{:S(2)}) %collective-permute-start.8) | collective-permute-done | bytes 262176 | tf_op jit(solution)/shard_map/ppermute | solution.py:331
  46.1 0.1 add_convert_fusion.2
  46.2 4.6 %collective-permute-start.9 = (bf16[128,1024]{1,0:T(8,128)(2,1)S(1)}, bf16[128,1024]{1,0:T(8,128)(2,1)S(1)}, u32[]{:S(2)}, u32[]{:S(2)}) collective-permute-start(bf16[128,1024]{1,0:T(8,128)(2,1)S(1)} %add_convert_fusion.2), channel_id=1, source_target_pairs={{0,4},{2,6},{4,0},{6,2},{1,5},{3,7},{5,1},{7,3},{8,12},{10,14},{12... | collective-permute-start | bytes 786440 | tf_op jit(solution)/shard_map/ppermute | solution.py:331
  50.8 1.3 %project.4 = bf16[256,1024]{1,0:T(8,128)(2,1)S(1)} custom-call(f32[256,128]{1,0:T(8,128)S(1)} %get-tuple-element.17.kinds_ref, bf16[2,1024,2048]{2,1,0:T(8,128)(2,1)S(1)} %get-tuple-element.20.w_ref, bf16[128,1024]{1,0:T(8,128)(2,1)S(1)} %get-tuple-element.25.refs_0_, bf16[128,1024]{1,0:T(8,128)(2,1)S(1)} %get-tuple-element.26.refs_1_.refs_0_), custom_call_target="tpu_custom_call" | custom-call | tf_op jit(solution)/shard_map/project/pallas_call | solution.py:307
  52.1 7.2 %collective-permute-done.7 = bf16[256,1024]{1,0:T(8,128)(2,1)S(1)} collective-permute-done((bf16[256,1024]{1,0:T(8,128)(2,1)S(1)}, bf16[256,1024]{1,0:T(8,128)(2,1)S(1)}, u32[]{:S(2)}, u32[]{:S(2)}) %collective-permute-start.7) | collective-permute-done | bytes 524320 | tf_op jit(solution)/shard_map/ppermute | solution.py:340
  59.3 0.0 collective-permute-done.11
  59.3 5.9 %collective-permute-done.9 = bf16[128,1024]{1,0:T(8,128)(2,1)S(1)} collective-permute-done((bf16[128,1024]{1,0:T(8,128)(2,1)S(1)}, bf16[128,1024]{1,0:T(8,128)(2,1)S(1)}, u32[]{:S(2)}, u32[]{:S(2)}) %collective-permute-start.9) | collective-permute-done | bytes 262176 | tf_op jit(solution)/shard_map/ppermute | solution.py:331
  65.2 1.1 %add_convert_fusion = bf16[256,1024]{1,0:T(8,128)(2,1)} fusion(bf16[256,1024]{1,0:T(8,128)(2,1)S(1)} %collective-permute-done.7, bf16[256,1024]{1,0:T(8,128)(2,1)S(1)} %project.4, bf16[128,1024]{1,0:T(8,128)(2,1)S(1)} %collective-permute-done.11, bf16[128,1024]{1,0:T(8,128)(2,1)S(1)} %collective-permute-done.9), kind=kLoop, calls=%fused_computation | loop fusion | flops 2359296 | bytes 2097152 | tf_op jit(solution)/shard_map/convert_element_type | solution.py:345
Async XLA Ops:
  0.0 7.6 %collective-permute-start = (bf16[256,1024]{1,0:T(8,128)(2,1)}, bf16[256,1024]{1,0:T(8,128)(2,1)S(1)}, u32[]{:S(2)}, u32[]{:S(2)}) collective-permute-start(bf16[256,1024]{1,0:T(8,128)(2,1)} %k_hbm.1), channel_id=1, source_target_pairs={{0,8},{8,0},{16,24},{24,16},{1,9},{9,1},{17,25},{25,17},{2,10},{10... | collective-permute-start | bytes 1572872 | tf_op jit(solution)/shard_map/ppermute | solution.py:223
  0.5 7.1 %collective-permute-start.1 = (bf16[256,1024]{1,0:T(8,128)(2,1)}, bf16[256,1024]{1,0:T(8,128)(2,1)S(1)}, u32[]{:S(2)}, u32[]{:S(2)}) collective-permute-start(bf16[256,1024]{1,0:T(8,128)(2,1)} %v_hbm.1), channel_id=1, source_target_pairs={{0,8},{8,0},{16,24},{24,16},{1,9},{9,1},{17,25},{25,17},{2,10},{10... | collective-permute-start | bytes 1572872 | tf_op jit(solution)/shard_map/ppermute | solution.py:224
  1.6 11.3 %collective-permute-start.2 = (bf16[256,512]{1,0:T(8,128)(2,1)S(1)}, bf16[256,512]{1,0:T(8,128)(2,1)S(1)}, u32[]{:S(2)}, u32[]{:S(2)}) collective-permute-start(bf16[256,512]{1,0:T(8,128)(2,1)S(1)} %slice_select_fusion), channel_id=1, source_target_pairs={{0,16},{8,24},{16,0},{24,8},{1,17},{9,25},{17,1},{25,9},{2,18},{10... | collective-permute-start | bytes 786440 | tf_op jit(solution)/shard_map/ppermute | solution.py:233
  5.6 14.3 %collective-permute-start.4 = (bf16[256,512]{1,0:T(8,128)(2,1)S(1)}, bf16[256,512]{1,0:T(8,128)(2,1)S(1)}, u32[]{:S(2)}, u32[]{:S(2)}) collective-permute-start(bf16[256,512]{1,0:T(8,128)(2,1)S(1)} %slice.11), channel_id=1, source_target_pairs={{0,16},{8,24},{1,17},{9,25},{2,18},{10,26},{3,19},{11,27},{4,20},{... | collective-permute-start | bytes 786440 | tf_op jit(solution)/shard_map/ppermute | solution.py:237
  7.6 0.7 %copy-start = (s32[256]{0:T(256)S(1)}, s32[256]{0:T(256)}, u32[]{:S(2)}) copy-start(s32[256]{0:T(256)} %param.8) | copy-start | bytes 3076
  16.9 7.4 %collective-permute-start.6 = (bf16[272,512]{1,0:T(8,128)(2,1)S(1)}, bf16[272,512]{1,0:T(8,128)(2,1)S(1)}, u32[]{:S(2)}, u32[]{:S(2)}) collective-permute-start(bf16[272,512]{1,0:T(8,128)(2,1)S(1)} %get-tuple-element.23), channel_id=1, source_target_pairs={{0,16},{8,24},{1,17},{9,25},{2,18},{10,26},{3,19},{11,27},{4,20},{... | collective-permute-start | bytes 835592 | tf_op jit(solution)/shard_map/ppermute | solution.py:274
  19.8 1.6 %collective-permute-start.3 = (bf16[256,512]{1,0:T(8,128)(2,1)S(1)}, bf16[256,512]{1,0:T(8,128)(2,1)S(1)}, u32[]{:S(2)}, u32[]{:S(2)}) collective-permute-start(bf16[256,512]{1,0:T(8,128)(2,1)S(1)} %collective-permute-done.2.q_ref.refs_0_), channel_id=1, source_target_pairs={{0,8},{8,0},{16,24},{24,16},{1,9},{9,1},{17,25},{25,17},{2,10},{10... | collective-permute-start | bytes 786440 | tf_op jit(solution)/shard_map/ppermute | solution.py:240
  19.9 1.9 %collective-permute-start.5 = (bf16[256,512]{1,0:T(8,128)(2,1)S(1)}, bf16[256,512]{1,0:T(8,128)(2,1)S(1)}, u32[]{:S(2)}, u32[]{:S(2)}) collective-permute-start(bf16[256,512]{1,0:T(8,128)(2,1)S(1)} %collective-permute-done.4.refs_2_), channel_id=1, source_target_pairs={{0,8},{8,0},{16,24},{24,16},{1,9},{9,1},{17,25},{25,17},{2,10},{10... | collective-permute-start | bytes 786440 | tf_op jit(solution)/shard_map/ppermute | solution.py:241
  25.6 9.2 %collective-permute-start.10 = (bf16[128,1024]{1,0:T(8,128)(2,1)S(1)}, bf16[128,1024]{1,0:T(8,128)(2,1)S(1)}, u32[]{:S(2)}, u32[]{:S(2)}) collective-permute-start(bf16[128,1024]{1,0:T(8,128)(2,1)S(1)} %get-tuple-element.28), channel_id=1, source_target_pairs={{0,2},{2,0},{4,6},{6,4},{1,3},{3,1},{5,7},{7,5},{8,10},{10,8},{12,... | collective-permute-start | bytes 786440 | tf_op jit(solution)/shard_map/ppermute | solution.py:331
  28.8 17.3 %collective-permute-start.8 = (bf16[128,1024]{1,0:T(8,128)(2,1)S(1)}, bf16[128,1024]{1,0:T(8,128)(2,1)S(1)}, u32[]{:S(2)}, u32[]{:S(2)}) collective-permute-start(bf16[128,1024]{1,0:T(8,128)(2,1)S(1)} %get-tuple-element.27), channel_id=1, source_target_pairs={{0,2},{2,0},{4,6},{6,4},{1,3},{3,1},{5,7},{7,5},{8,10},{10,8},{12,... | collective-permute-start | bytes 786440 | tf_op jit(solution)/shard_map/ppermute | solution.py:331
  32.0 27.2 %collective-permute-start.7 = (bf16[256,1024]{1,0:T(8,128)(2,1)S(1)}, bf16[256,1024]{1,0:T(8,128)(2,1)S(1)}, u32[]{:S(2)}, u32[]{:S(2)}) collective-permute-start(bf16[256,1024]{1,0:T(8,128)(2,1)S(1)} %project.5), channel_id=1, source_target_pairs={{0,2},{2,0},{4,6},{6,4},{1,3},{3,1},{5,7},{7,5},{8,10},{10,8},{12,... | collective-permute-start | bytes 1572872 | tf_op jit(solution)/shard_map/ppermute | solution.py:340
  34.9 24.3 %collective-permute-start.11 = (bf16[128,1024]{1,0:T(8,128)(2,1)S(1)}, bf16[128,1024]{1,0:T(8,128)(2,1)S(1)}, u32[]{:S(2)}, u32[]{:S(2)}) collective-permute-start(bf16[128,1024]{1,0:T(8,128)(2,1)S(1)} %add_convert_fusion.1), channel_id=1, source_target_pairs={{0,4},{2,6},{4,0},{6,2},{1,5},{3,7},{5,1},{7,3},{8,12},{10,14},{12... | collective-permute-start | bytes 786440 | tf_op jit(solution)/shard_map/ppermute | solution.py:331
  46.2 19.0 %collective-permute-start.9 = (bf16[128,1024]{1,0:T(8,128)(2,1)S(1)}, bf16[128,1024]{1,0:T(8,128)(2,1)S(1)}, u32[]{:S(2)}, u32[]{:S(2)}) collective-permute-start(bf16[128,1024]{1,0:T(8,128)(2,1)S(1)} %add_convert_fusion.2), channel_id=1, source_target_pairs={{0,4},{2,6},{4,0},{6,2},{1,5},{3,7},{5,1},{7,3},{8,12},{10,14},{12... | collective-permute-start | bytes 786440 | tf_op jit(solution)/shard_map/ppermute | solution.py:331

commit v2 on v1

--- a/solution.py
+++ b/solution.py
@@ -13,6 +13,7 @@
 LANES = 128
 SHARES = (1, 2)
 BLOCK = 256
+PIECES = 4
 LOG2E = float(np.log2(np.e))
 
 
@@ -42,29 +43,35 @@
 
 
 def column_copies(place_ref, offsets, w_hbm, w_ref, sems, first):
-    chunk = w_ref.shape[2] // len(offsets)
+    kinds, depth, width = w_ref.shape
+    chunk = width // len(offsets)
+    piece = depth // PIECES
     copies = []
     for i, offset in enumerate(offsets):
         start = pl.multiple_of(jnp.bitwise_xor(place_ref[1], offset) * chunk, chunk)
-        src, dst = w_hbm.at[:, :, pl.ds(start, chunk)], w_ref.at[:, :, pl.ds(i * chunk, chunk)]
-        copies.append(pltpu.make_async_copy(src, dst, sems.at[first + i]))
+        for kind in range(kinds):
+            for rows in (pl.ds(r * piece, piece) for r in range(PIECES)):
+                src = w_hbm.at[kind, rows, pl.ds(start, chunk)]
+                dst = w_ref.at[kind, rows, pl.ds(i * chunk, chunk)]
+                copies.append(pltpu.make_async_copy(src, dst, sems.at[first + len(copies)]))
     return copies
 
 
-def own_kernel(offsets, loads, place_ref, kinds_ref, q_hbm, k_hbm, v_hbm, w_hbm, *refs):
+def own_kernel(offsets, loads, place_ref, kinds_hbm, q_hbm, k_hbm, v_hbm, w_hbm, *refs):
     others = len(offsets) - 1
     k_refs, v_refs = refs[:others], refs[others : 2 * others]
-    out_ref, lse_ref, k_ref, v_ref, columns_ref, w_ref, q_ref, sems = refs[2 * others :]
-    pairs = [(q_hbm, q_ref), (k_hbm, k_ref), (v_hbm, v_ref)]
+    out_ref, lse_ref, q_ref, k_ref, v_ref, columns_ref, w_ref, kinds_ref, sems = refs[2 * others :]
+    pairs = [(kinds_hbm, kinds_ref), (v_hbm, v_ref), (q_hbm, q_ref), (k_hbm, k_ref)]
     copies = [pltpu.make_async_copy(src, dst, sems.at[i]) for i, (src, dst) in enumerate(pairs)]
     later = column_copies(place_ref, loads, w_hbm, w_ref, sems, len(pairs))
     for copy in copies + later:
         copy.start()
     me = place_ref[0]
     rows = q_ref.shape[0]
-    columns_ref[...] = jnp.broadcast_to(kinds_ref[...].astype(jnp.float32), (LANES, rows)).T
     for copy in copies:
         copy.wait()
+    lse_ref[...] = jnp.zeros_like(lse_ref)
+    columns_ref[...] = jnp.broadcast_to(kinds_ref[...].astype(jnp.float32), (LANES, rows)).T
     below = lax.broadcasted_iota(jnp.int32, (rows, rows), 0) >= lax.broadcasted_iota(jnp.int32, (rows, rows), 1)
     masks = [below if o == 0 else lax.broadcast(jnp.bitwise_xor(me, o), (rows, rows)) < me for o in offsets]
     for h in range(q_ref.shape[1] // HD):
@@ -95,16 +102,9 @@
     return -(-3 * shipped // 16) * 16
 
 
-def cross_kernel(count, half, skip, loads, place_ref, q_ref, *refs):
+def cross_kernel(count, half, skip, place_ref, q_ref, *refs):
     k_refs, v_refs = refs[:count], refs[count : 2 * count]
-    later = []
-    if loads:
-        w_hbm, out_ref, w_ref, sems = refs[2 * count :]
-        later = column_copies(place_ref, loads, w_hbm, w_ref, sems, 0)
-    else:
-        (out_ref,) = refs[2 * count :]
-    for copy in later:
-        copy.start()
+    (out_ref,) = refs[2 * count :]
     rows, width = q_ref.shape
     shipped = width // HD
 
@@ -121,22 +121,23 @@
         extra = out_ref.shape[0] - rows
         out_ref[rows:, :rows] = lse_terms(found, shipped).T[:extra].astype(out_ref.dtype)
 
-    for copy in later:
+
+def mix(own, far, share, out_dtype):
+    return (own.astype(jnp.float32) * share + far.astype(jnp.float32) * (1.0 - share)).astype(out_dtype)
+
+
+def load_kernel(loads, place_ref, w_hbm, w_ref, sems):
+    copies = column_copies(place_ref, loads, w_hbm, w_ref, sems, 0)
+    for copy in copies:
+        copy.start()
+    for copy in copies:
         copy.wait()
 
 
-def mix(own, own_lse, far, far_lse, out_dtype):
-    mine = 1.0 / (1.0 + jnp.exp2(far_lse - own_lse))
-    return (own.astype(jnp.float32) * mine + far.astype(jnp.float32) * (1.0 - mine)).astype(out_dtype)
-
-
-def far_kernel(count, half, place_ref, q_hbm, own_ref, lse_ref, *refs):
+def far_kernel(count, half, place_ref, q_ref, own_ref, lse_ref, *refs):
     k_refs, v_refs = refs[:count], refs[count : 2 * count]
-    out_ref, q_ref, sem = refs[2 * count :]
+    (out_ref,) = refs[2 * count :]
     width = out_ref.shape[1]
-    copy = pltpu.make_async_copy(q_hbm.at[:, :width], q_ref, sem)
-    copy.start()
-    copy.wait()
 
     @pl.when(place_ref[0] < half)
     def _():
@@ -149,7 +150,8 @@
             result, lse = softmax_rows(
                 q_ref[:, at], [k[:, at] for k in k_refs], [v[:, at] for v in v_refs], [None] * count, HD**-0.5
             )
-            out_ref[:, at] = mix(own_ref[:, at], lse_ref[:, h : h + 1], result, lse, out_ref.dtype)
+            share = 1.0 / (1.0 + jnp.exp2(lse - lse_ref[:, h : h + 1]))
+            out_ref[:, at] = mix(own_ref[:, at], result, share, out_ref.dtype)
 
 
 def project(rows, image, first, w_ref, out_ref):
@@ -177,16 +179,33 @@
     @pl.when(place_ref[0] >= half)
     def _():
         terms = back_ref[own_ref.shape[0] :, rows].astype(jnp.float32)
-        terms = jnp.concatenate([terms, jnp.zeros((LANES - terms.shape[0], count), jnp.float32)], axis=0).T
+        far_lse = sum(terms[i * shipped : (i + 1) * shipped] for i in range(3))
+        before = skip // HD
+        far_lse = jnp.concatenate(
+            [
+                jnp.zeros((before, count), jnp.float32),
+                far_lse,
+                jnp.zeros((LANES - before - shipped, count), jnp.float32),
+            ],
+            axis=0,
+        ).T
+        mine = 1.0 / (1.0 + jnp.exp2(far_lse - lse_ref[rows, :]))
         for h in range(shipped):
             at, there = slice(h * HD, (h + 1) * HD), slice(skip + h * HD, skip + (h + 1) * HD)
-            far_lse = sum(terms[:, c : c + 1] for c in (h, shipped + h, 2 * shipped + h))
-            own_h = skip // HD + h
-            att_ref[:, there] = mix(
-                own_ref[rows, there], lse_ref[rows, own_h : own_h + 1], back_ref[rows, at], far_lse, att_ref.dtype
-            )
+            share = mine[:, before + h : before + h + 1]
+            att_ref[:, there] = mix(own_ref[rows, there], back_ref[rows, at], share, att_ref.dtype)
 
     project(att_ref[...], kinds_ref[rows, :1] == 1, first, w_ref, out_ref)
+
+
+def stream_kernel(offset, place_ref, w_hbm, kinds_ref, *refs):
+    *att_refs, out_ref, w_ref, sems = refs
+    copies = column_copies(place_ref, (offset,), w_hbm, w_ref, sems, 0)
+    for copy in copies:
+        copy.start()
+    for copy in copies:
+        copy.wait()
+    project_kernel(0, 0, kinds_ref, w_ref, *att_refs, out_ref)
 
 
 def project_kernel(lo, first, kinds_ref, w_ref, *refs):
@@ -212,11 +231,20 @@
         return [(i, i ^ bit) for i in range(count)]
 
     order = sorted(range(tp_count), reverse=True)
-    early_loads, late_loads = order[: tp_count // 2], order[tp_count // 2 :]
+    loads = [tuple(order[:1]), tuple(order[1:-1])]
+    columns = {}
+    pieces = PIECES * out_weight.shape[0]
 
     def columns_shape(loads):
         return jax.ShapeDtypeStruct((out_weight.shape[0], width, chunk * len(loads)), out_weight.dtype)
 
+    heads = width // HD
+    shipped = heads // 2
+    skip = (heads - shipped) * HD
+    up = [(i, i + half) for i in range(half)]
+    met = lax.ppermute(
+        jnp.where(place[0] >= half, queries[:, skip:], key_rows[:, : width - skip]), "seq", xor(seq_count, half)
+    )
     offsets, keys, vals = [0], [key_rows], [values]
     bit = half // 2
     while bit:
@@ -226,12 +254,27 @@
         bit //= 2
     count = len(offsets)
 
-    heads = width // HD
-    shipped = heads // 2
-    skip = (heads - shipped) * HD
-    up = [(i, i + half) for i in range(half)]
-    met = lax.ppermute(
-        jnp.where(place[0] >= half, queries[:, skip:], key_rows[:, : width - skip]), "seq", xor(seq_count, half)
+    own, own_lse, own_queries, keys[0], vals[0], kinds, columns[loads[0]] = pl.pallas_call(
+        functools.partial(own_kernel, tuple(offsets), loads[0]),
+        out_shape=(
+            jax.ShapeDtypeStruct((rows, width), jnp.bfloat16),
+            jax.ShapeDtypeStruct((rows, LANES), jnp.float32),
+            jax.ShapeDtypeStruct(queries.shape, queries.dtype),
+            jax.ShapeDtypeStruct(key_rows.shape, key_rows.dtype),
+            jax.ShapeDtypeStruct(values.shape, values.dtype),
+            jax.ShapeDtypeStruct((rows, LANES), jnp.float32),
+            columns_shape(loads[0]),
+        ),
+        in_specs=[smem] + [hbm] * 5 + [vmem] * (2 * count - 2),
+        out_specs=(vmem,) * 7,
+        scratch_shapes=[pltpu.VMEM((1, rows), modality.dtype), pltpu.SemaphoreType.DMA((4 + pieces * len(loads[0]),))],
+        compiler_params=params(8),
+        name="own",
+    )(
+        place,
+        *(in_hbm(x) for x in (modality.reshape(1, rows), queries, key_rows, values, out_weight)),
+        *keys[1:],
+        *vals[1:],
     )
     far_keys = [met]
     far_vals = [lax.ppermute(values[:, :skip], "seq", up)]
@@ -241,51 +284,37 @@
         far_vals = far_vals + [lax.ppermute(x, "seq", xor(seq_count, bit)) for x in far_vals]
         bit //= 2
 
-    own, own_lse, keys[0], vals[0], kinds, early = pl.pallas_call(
-        functools.partial(own_kernel, tuple(offsets), tuple(early_loads)),
-        out_shape=(
-            jax.ShapeDtypeStruct((rows, width), jnp.bfloat16),
-            jax.ShapeDtypeStruct((rows, LANES), jnp.float32),
-            jax.ShapeDtypeStruct(key_rows.shape, key_rows.dtype),
-            jax.ShapeDtypeStruct(values.shape, values.dtype),
-            jax.ShapeDtypeStruct((rows, LANES), jnp.float32),
-            columns_shape(early_loads),
-        ),
-        in_specs=[smem, vmem] + [hbm] * 4 + [vmem] * (2 * count - 2),
-        out_specs=(vmem,) * 6,
-        scratch_shapes=[
-            pltpu.VMEM(queries.shape, queries.dtype),
-            pltpu.SemaphoreType.DMA((3 + len(early_loads),)),
-        ],
-        compiler_params=params(8),
-        name="own",
-    )(place, modality.reshape(1, rows), *(in_hbm(x) for x in (queries, key_rows, values, out_weight)), *keys[1:], *vals[1:])
-
-    loads = tuple(late_loads)
-    found, late = pl.pallas_call(
-        functools.partial(cross_kernel, count, half, skip, loads),
-        out_shape=(jax.ShapeDtypeStruct((rows + lse_rows(shipped), width - skip), jnp.bfloat16), columns_shape(loads)),
-        in_specs=[smem] + [vmem] * (1 + 2 * count) + [hbm],
-        out_specs=(vmem, vmem),
-        scratch_shapes=[pltpu.SemaphoreType.DMA((len(loads),))],
+
+    found = pl.pallas_call(
+        functools.partial(cross_kernel, count, half, skip),
+        out_shape=jax.ShapeDtypeStruct((rows + lse_rows(shipped), width - skip), jnp.bfloat16),
+        in_specs=[smem] + [vmem] * (1 + 2 * count),
+        out_specs=vmem,
         compiler_params=params(8),
         name="cross",
-    )(place, met, *keys, *vals, in_hbm(out_weight))
+    )(place, met, *keys, *vals)
     back = lax.ppermute(found, "seq", up)
     near = pl.pallas_call(
         functools.partial(far_kernel, count, half),
         out_shape=jax.ShapeDtypeStruct((rows, skip), jnp.bfloat16),
-        in_specs=[smem, hbm] + [vmem] * (2 + 2 * count),
+        in_specs=[smem] + [vmem] * (3 + 2 * count),
         out_specs=vmem,
-        scratch_shapes=[pltpu.VMEM((rows, skip), jnp.bfloat16), pltpu.SemaphoreType.DMA],
         compiler_params=params(8),
         name="far",
-    )(place, in_hbm(queries), own, own_lse, *far_keys, *far_vals)
+    )(place, own_queries, own, own_lse, *far_keys, *far_vals)
+    columns[loads[1]] = pl.pallas_call(
+        functools.partial(load_kernel, loads[1]),
+        out_shape=columns_shape(loads[1]),
+        in_specs=[smem, hbm],
+        out_specs=vmem,
+        scratch_shapes=[pltpu.SemaphoreType.DMA((pieces * len(loads[1]),))],
+        compiler_params=params(8),
+        name="load",
+    )(place, in_hbm(out_weight))
 
     def columns_of(offset):
-        if offset in early_loads:
-            return early, early_loads.index(offset) * chunk
-        return late, late_loads.index(offset) * chunk
+        (held,) = (x for x in loads if offset in x)
+        return columns[held], held.index(offset) * chunk
 
     def merged(p, offset):
         weight, first = columns_of(offset)
@@ -301,6 +330,20 @@
             compiler_params=params(8),
             name="merge",
         )(place, own, own_lse, near, back, kinds, weight)
+
+    def streamed(attended, offset):
+        return pl.pallas_call(
+            functools.partial(stream_kernel, offset),
+            out_shape=jax.ShapeDtypeStruct((rows, chunk), jnp.bfloat16),
+            in_specs=[smem, hbm] + [vmem] * (1 + len(attended)),
+            out_specs=vmem,
+            scratch_shapes=[
+                pltpu.VMEM((out_weight.shape[0], width, chunk), out_weight.dtype),
+                pltpu.SemaphoreType.DMA((pieces,)),
+            ],
+            compiler_params=params(12),
+            name="stream",
+        )(place, in_hbm(out_weight), kinds, *attended)
 
     def projected(lo, attended, offset):
         weight, first = columns_of(offset)
@@ -338,7 +381,7 @@
         sums.append(arrivals)
     beside = projected(0, attended, 1)
     beside = lax.ppermute(beside, "tp", xor(tp_count, 1))
-    total = projected(0, attended, 0)
+    total = streamed(attended, 0)
     total = add(total, beside)
     for arrivals in zip(*sums):
         total = add(total, jnp.concatenate(arrivals, axis=0))

time: 66.5 us -> 64.3 us (0.967)
  starting transfers between devices: 20.4 us -> 17.3 us
  Pallas kernels: 16.9 us -> 19.8 us
  waiting for transfers between devices: 24.8 us -> 23.6 us
  local copies, waits for them, and re-layouts: 1.65 us -> 0.97 us
    ppermute x1, waiting for transfers between devices: 7.16 us -> 0.01 us  [on_device(): beside = lax.ppermute(beside, 'tp', xor(tp_count, 1))]
    pallas_call x2 -> x4, Pallas kernels: 8.56 us -> 13.7 us  [the longest x1 4.09 us: on_device(): pl.pallas_call(functools.partial(load_kernel, loads[1]), out_shape=column...]
    ppermute x4, waiting for transfers between devices: 15.2 us -> 19 us  [on_device(): arrived = lax.ppermute(keep.pop(offset), 'tp', xor(tp_count, bit))]
    ppermute x4, starting transfers between devices: 9.64 us -> 6.58 us  [on_device(): arrived = lax.ppermute(keep.pop(offset), 'tp', xor(tp_count, bit))]
    ppermute x1, waiting for transfers between devices: 0.97 us -> 2.51 us  [on_device(): back = lax.ppermute(found, 'seq', up)]
    pallas_call x4 -> x3, Pallas kernels: 4.19 us -> 2.83 us  [projected(): pl.pallas_call(functools.partial(project_kernel, lo, first), out_shape=ja...]
    pallas_call x1, Pallas kernels: 1.52 us -> 0.57 us  [on_device(): pl.pallas_call(functools.partial(far_kernel, count, half), out_shape=jax....]
    unnamed x2 -> x0, local copies, waits for them, and re-layouts: 0.68 us -> none
  transfers between devices with their start and end apart: 12 -> 12, of which waited for: 7 -> 7; matrix products, arithmetic and copies ran while one was open for 3% -> 3% of each run, Pallas kernels for 24% -> 29%
where the time goes in v2:
time: 64.3 us; the launch traced here: 64.1 us
  waiting for transfers between devices  23.6 us (37%)
  Pallas kernels  19.8 us (31%)
  starting transfers between devices  17.3 us (27%)
  other arithmetic  2.33 us (4%)
  local copies, waits for them, and re-layouts  0.97 us (2%)
    ppermute x4, waiting for transfers between devices, on_device(): arrived = lax.ppermute(keep.pop(offset), 'tp', xor(tp_count, bit))  19 us
    ppermute x4, starting transfers between devices, on_device(): arrived = lax.ppermute(keep.pop(offset), 'tp', xor(tp_count, bit))  6.58 us
    pallas_call x1, Pallas kernels, on_device(): pl.pallas_call(functools.partial(load_kernel, loads[1]), out_shape=column...  4.09 us
    pallas_call x1, Pallas kernels, streamed(): pl.pallas_call(functools.partial(stream_kernel, offset), out_shape=jax.Sh...  4.06 us
    pallas_call x1, Pallas kernels, on_device(): pl.pallas_call(functools.partial(own_kernel, tuple(offsets), loads[0]), o...  3.84 us
    ppermute x1, starting transfers between devices, on_device(): back = lax.ppermute(found, 'seq', up)  3.08 us
    ppermute x1, starting transfers between devices, on_device(): lax.ppermute(jnp.where(place[0] >= half, queries[:, skip:], key_rows[:, :...  3.06 us
    pallas_call x3, Pallas kernels, projected(): pl.pallas_call(functools.partial(project_kernel, lo, first), out_shape=ja...  2.83 us
  transfers between devices with their start and end apart: 12, of which 7 were waited for; matrix products, arithmetic and copies ran while one was open for 3% of the time, Pallas kernels for 29%

profile of v2, /device:TPU:0, one launch (start us, length us, event | category | flops | bytes accessed | tf_op | source)
XLA Modules:
  0.0 64.1 jit_solution(11208771659600459925)
XLA Ops:
  0.0 0.5 collective-permute-start
  0.5 0.0 collective-permute-start.1
  0.5 1.1 %slice_select_fusion = bf16[256,512]{1,0:T(8,128)(2,1)S(1)} fusion(bf16[256,1024]{1,0:T(8,128)(2,1)} %k_hbm.1, bf16[256,1024]{1,0:T(8,128)(2,1)} %q_hbm.1, pred[]{:T(512)S(6)} %ge.3), kind=kLoop, calls=%fused_computation.3 | loop fusion | flops 131072 | bytes 786433 | tf_op jit(solution)/shard_map/jit(_where)/select_n | solution.py:246
  1.6 3.1 %collective-permute-start.2 = (bf16[256,512]{1,0:T(8,128)(2,1)S(1)}, bf16[256,512]{1,0:T(8,128)(2,1)S(1)}, u32[]{:S(2)}, u32[]{:S(2)}) collective-permute-start(bf16[256,512]{1,0:T(8,128)(2,1)S(1)} %slice_select_fusion), channel_id=1, source_target_pairs={{0,16},{8,24},{16,0},{24,8},{1,17},{9,25},{17,1},{25,9},{2,18},{10... | collective-permute-start | bytes 786440 | tf_op jit(solution)/shard_map/ppermute | solution.py:245
  4.6 1.0 %slice.11 = bf16[256,512]{1,0:T(8,128)(2,1)S(1)} slice(bf16[256,1024]{1,0:T(8,128)(2,1)} %v_hbm.1), slice={[0:256], [0:512]} | slice | bytes 524288 | tf_op jit(solution)/shard_map/slice | solution.py:280
  5.6 1.9 %collective-permute-start.4 = (bf16[256,512]{1,0:T(8,128)(2,1)S(1)}, bf16[256,512]{1,0:T(8,128)(2,1)S(1)}, u32[]{:S(2)}, u32[]{:S(2)}) collective-permute-start(bf16[256,512]{1,0:T(8,128)(2,1)S(1)} %slice.11), channel_id=1, source_target_pairs={{0,16},{8,24},{1,17},{9,25},{2,18},{10,26},{3,19},{11,27},{4,20},{... | collective-permute-start | bytes 786440 | tf_op jit(solution)/shard_map/ppermute | solution.py:280
  7.6 0.1 pad_add_fusion.place_ref
  7.6 0.0 collective-permute-done.refs_0_.refs_1_
  7.6 0.0 collective-permute-done.1.refs_1_.refs_3_
  7.6 3.8 %own.1 = (bf16[256,1024]{1,0:T(8,128)(2,1)S(1)}, f32[256,128]{1,0:T(8,128)S(1)}, bf16[256,1024]{1,0:T(8,128)(2,1)S(1)}, bf16[256,1024]{1,0:T(8,128)(2,1)S(1)}, b...) custom-call(s32[2]{0:T(128)S(1)} %pad_add_fusion.place_ref, ...), custom_call_target="tpu_custom_call" | custom-call | tf_op jit(solution)/shard_map/own/pallas_call | solution.py:257
  11.5 0.0 collective-permute-done.2.refs_0_.q_ref
  11.5 1.7 %cross.1 = bf16[272,512]{1,0:T(8,128)(2,1)S(1)} custom-call(s32[2]{0:T(128)S(1)} %pad_add_fusion.place_ref, bf16[256,512]{1,0:T(8,128)(2,1)S(1)} %collective-permute-done.2.refs_0_.q_ref, bf16[256,1024]{1,0:T(8,128)(2,1)S(1)} %get-tuple-element.20.refs_0_, bf16[256,1024]{1,0:T(8,128)(2,1)S(1)} %collective-permute-done.refs_0_.refs_1_, ...), custom_call_target="tpu_custom_call" | custom-call | tf_op jit(solution)/shard_map/cross/pallas_call | solution.py:288
  13.2 3.1 %collective-permute-start.6 = (bf16[272,512]{1,0:T(8,128)(2,1)S(1)}, bf16[272,512]{1,0:T(8,128)(2,1)S(1)}, u32[]{:S(2)}, u32[]{:S(2)}) collective-permute-start(bf16[272,512]{1,0:T(8,128)(2,1)S(1)} %cross.1), channel_id=1, source_target_pairs={{0,16},{8,24},{1,17},{9,25},{2,18},{10,26},{3,19},{11,27},{4,20},{... | collective-permute-start | bytes 835592 | tf_op jit(solution)/shard_map/ppermute | solution.py:296
  16.3 0.7 %collective-permute-done.4.refs_2_ = bf16[256,512]{1,0:T(8,128)(2,1)S(1)} collective-permute-done((bf16[256,512]{1,0:T(8,128)(2,1)S(1)}, bf16[256,512]{1,0:T(8,128)(2,1)S(1)}, u32[]{:S(2)}, u32[]{:S(2)}) %collective-permute-start.4) | collective-permute-done | bytes 262176 | tf_op jit(solution)/shard_map/ppermute | solution.py:280
  17.0 0.0 collective-permute-start.5
  17.0 0.5 collective-permute-start.3
  17.5 1.0 %collective-permute-done.5.refs_3_ = bf16[256,512]{1,0:T(8,128)(2,1)S(1)} collective-permute-done((bf16[256,512]{1,0:T(8,128)(2,1)S(1)}, bf16[256,512]{1,0:T(8,128)(2,1)S(1)}, u32[]{:S(2)}, u32[]{:S(2)}) %collective-permute-start.5) | collective-permute-done | bytes 262176 | tf_op jit(solution)/shard_map/ppermute | solution.py:284
  18.5 0.4 collective-permute-done.3.refs_1_
  18.9 0.6 far.1.near_ref
  19.4 2.5 %collective-permute-done.6.back_ref = bf16[272,512]{1,0:T(8,128)(2,1)S(1)} collective-permute-done((bf16[272,512]{1,0:T(8,128)(2,1)S(1)}, bf16[272,512]{1,0:T(8,128)(2,1)S(1)}, u32[]{:S(2)}, u32[]{:S(2)}) %collective-permute-start.6) | collective-permute-done | bytes 278560 | tf_op jit(solution)/shard_map/ppermute | solution.py:296
  22.0 1.3 %merge.2 = (bf16[128,1024]{1,0:T(8,128)(2,1)S(1)}, bf16[128,1024]{1,0:T(8,128)(2,1)S(1)}) custom-call(s32[2]{0:T(128)S(1)} %pad_add_fusion.place_ref, bf16[256,1024]{1,0:T(8,128)(2,1)S(1)} %get-tuple-element.17.own_ref, f32[256,128]{1,0:T(8,128)S(1)} %get-tuple-element.18.lse_ref, bf16[256,512]{1,0:T(8,128)(2,1)S(1)} %far.1.near_ref, ...), custom_call_target="tpu_custom_call" | custom-call | tf_op jit(solution)/shard_map/merge/pallas_call | solution.py:322
  23.3 1.6 %collective-permute-start.8 = (bf16[128,1024]{1,0:T(8,128)(2,1)S(1)}, bf16[128,1024]{1,0:T(8,128)(2,1)S(1)}, u32[]{:S(2)}, u32[]{:S(2)}) collective-permute-start(bf16[128,1024]{1,0:T(8,128)(2,1)S(1)} %get-tuple-element.25), channel_id=1, source_target_pairs={{0,2},{2,0},{4,6},{6,4},{1,3},{3,1},{5,7},{7,5},{8,10},{10,8},{12,... | collective-permute-start | bytes 786440 | tf_op jit(solution)/shard_map/ppermute | solution.py:374
  24.9 1.3 %merge.3 = (bf16[128,1024]{1,0:T(8,128)(2,1)S(1)}, bf16[128,1024]{1,0:T(8,128)(2,1)S(1)}) custom-call(s32[2]{0:T(128)S(1)} %pad_add_fusion.place_ref, bf16[256,1024]{1,0:T(8,128)(2,1)S(1)} %get-tuple-element.17.own_ref, f32[256,128]{1,0:T(8,128)S(1)} %get-tuple-element.18.lse_ref, bf16[256,512]{1,0:T(8,128)(2,1)S(1)} %far.1.near_ref, ...), custom_call_target="tpu_custom_call" | custom-call | tf_op jit(solution)/shard_map/merge/pallas_call | solution.py:322
  26.3 0.5 collective-permute-start.10
  26.8 4.1 %load.1.w_ref = bf16[2,1024,2048]{2,1,0:T(8,128)(2,1)S(1)} custom-call(s32[2]{0:T(128)S(1)} %pad_add_fusion.place_ref, bf16[2,1024,4096]{2,1,0:T(8,128)(2,1)} %w_hbm.5), custom_call_target="tpu_custom_call" | custom-call | tf_op jit(solution)/shard_map/load/pallas_call | solution.py:305
  30.9 0.8 %project.5 = bf16[128,1024]{1,0:T(8,128)(2,1)S(1)} custom-call(f32[256,128]{1,0:T(8,128)S(1)} %get-tuple-element.16.kinds_ref, bf16[2,1024,2048]{2,1,0:T(8,128)(2,1)S(1)} %load.1.w_ref, bf16[128,1024]{1,0:T(8,128)(2,1)S(1)} %get-tuple-element.24.refs_1_.refs_0_), custom_call_target="tpu_custom_call" | custom-call | tf_op jit(solution)/shard_map/project/pallas_call | solution.py:350
  31.7 1.3 %project.3 = bf16[256,1024]{1,0:T(8,128)(2,1)S(1)} custom-call(f32[256,128]{1,0:T(8,128)S(1)} %get-tuple-element.16.kinds_ref, bf16[2,1024,2048]{2,1,0:T(8,128)(2,1)S(1)} %load.1.w_ref, bf16[128,1024]{1,0:T(8,128)(2,1)S(1)} %get-tuple-element.23.refs_0_, bf16[128,1024]{1,0:T(8,128)(2,1)S(1)} %get-tuple-element.24.refs_1_.refs_0_), custom_call_target="tpu_custom_call" | custom-call | tf_op jit(solution)/shard_map/project/pallas_call | solution.py:350
  33.0 0.8 %project.4 = bf16[128,1024]{1,0:T(8,128)(2,1)S(1)} custom-call(f32[256,128]{1,0:T(8,128)S(1)} %get-tuple-element.16.kinds_ref, bf16[2,1024,2048]{2,1,0:T(8,128)(2,1)S(1)} %load.1.w_ref, bf16[128,1024]{1,0:T(8,128)(2,1)S(1)} %get-tuple-element.23.refs_0_), custom_call_target="tpu_custom_call" | custom-call | tf_op jit(solution)/shard_map/project/pallas_call | solution.py:350
  33.8 1.6 %collective-permute-start.7 = (bf16[256,1024]{1,0:T(8,128)(2,1)S(1)}, bf16[256,1024]{1,0:T(8,128)(2,1)S(1)}, u32[]{:S(2)}, u32[]{:S(2)}) collective-permute-start(bf16[256,1024]{1,0:T(8,128)(2,1)S(1)} %project.3), channel_id=1, source_target_pairs={{0,2},{2,0},{4,6},{6,4},{1,3},{3,1},{5,7},{7,5},{8,10},{10,8},{12,... | collective-permute-start | bytes 1572872 | tf_op jit(solution)/shard_map/ppermute | solution.py:383
  35.4 0.0 collective-permute-done.8
  35.4 0.1 add_convert_fusion.2
  35.5 2.7 %collective-permute-start.9 = (bf16[128,1024]{1,0:T(8,128)(2,1)S(1)}, bf16[128,1024]{1,0:T(8,128)(2,1)S(1)}, u32[]{:S(2)}, u32[]{:S(2)}) collective-permute-start(bf16[128,1024]{1,0:T(8,128)(2,1)S(1)} %add_convert_fusion.2), channel_id=1, source_target_pairs={{0,4},{2,6},{4,0},{6,2},{1,5},{3,7},{5,1},{7,3},{8,12},{10,14},{12... | collective-permute-start | bytes 786440 | tf_op jit(solution)/shard_map/ppermute | solution.py:374
  38.1 7.5 %collective-permute-done.10 = bf16[128,1024]{1,0:T(8,128)(2,1)S(1)} collective-permute-done((bf16[128,1024]{1,0:T(8,128)(2,1)S(1)}, bf16[128,1024]{1,0:T(8,128)(2,1)S(1)}, u32[]{:S(2)}, u32[]{:S(2)}) %collective-permute-start.10) | collective-permute-done | bytes 262176 | tf_op jit(solution)/shard_map/ppermute | solution.py:374
  45.7 0.1 add_convert_fusion.1
  45.8 1.8 %collective-permute-start.11 = (bf16[128,1024]{1,0:T(8,128)(2,1)S(1)}, bf16[128,1024]{1,0:T(8,128)(2,1)S(1)}, u32[]{:S(2)}, u32[]{:S(2)}) collective-permute-start(bf16[128,1024]{1,0:T(8,128)(2,1)S(1)} %add_convert_fusion.1), channel_id=1, source_target_pairs={{0,4},{2,6},{4,0},{6,2},{1,5},{3,7},{5,1},{7,3},{8,12},{10,14},{12... | collective-permute-start | bytes 786440 | tf_op jit(solution)/shard_map/ppermute | solution.py:374
  47.5 4.1 %stream.1 = bf16[256,1024]{1,0:T(8,128)(2,1)S(1)} custom-call(s32[2]{0:T(128)S(1)} %pad_add_fusion.place_ref, bf16[2,1024,4096]{2,1,0:T(8,128)(2,1)} %w_hbm.5, f32[256,128]{1,0:T(8,128)S(1)} %get-tuple-element.16.kinds_ref, bf16[128,1024]{1,0:T(8,128)(2,1)S(1)} %get-tuple-element.23.refs_0_, bf16[128,1024]{1,0:T(8,128)(2,1)S(1)} %get-tuple-element.24.refs_1_.refs_0_), custom_call_target="tpu_custom_call" | custom-call | tf_op jit(solution)/shard_map/stream/pallas_call | solution.py:335
  51.6 1.8 %collective-permute-done.9 = bf16[128,1024]{1,0:T(8,128)(2,1)S(1)} collective-permute-done((bf16[128,1024]{1,0:T(8,128)(2,1)S(1)}, bf16[128,1024]{1,0:T(8,128)(2,1)S(1)}, u32[]{:S(2)}, u32[]{:S(2)}) %collective-permute-start.9) | collective-permute-done | bytes 262176 | tf_op jit(solution)/shard_map/ppermute | solution.py:374
  53.4 9.7 %collective-permute-done.11 = bf16[128,1024]{1,0:T(8,128)(2,1)S(1)} collective-permute-done((bf16[128,1024]{1,0:T(8,128)(2,1)S(1)}, bf16[128,1024]{1,0:T(8,128)(2,1)S(1)}, u32[]{:S(2)}, u32[]{:S(2)}) %collective-permute-start.11) | collective-permute-done | bytes 262176 | tf_op jit(solution)/shard_map/ppermute | solution.py:374
  63.1 0.0 collective-permute-done.7
  63.1 1.1 %add_convert_fusion = bf16[256,1024]{1,0:T(8,128)(2,1)} fusion(bf16[256,1024]{1,0:T(8,128)(2,1)S(1)} %collective-permute-done.7, bf16[256,1024]{1,0:T(8,128)(2,1)S(1)} %stream.1, bf16[128,1024]{1,0:T(8,128)(2,1)S(1)} %collective-permute-done.11, bf16[128,1024]{1,0:T(8,128)(2,1)S(1)} %collective-permute-done.9), kind=kLoop, calls=%fused_computation | loop fusion | flops 2359296 | bytes 2097152 | tf_op jit(solution)/shard_map/convert_element_type | solution.py:388
Async XLA Ops:
  0.0 7.6 %collective-permute-start = (bf16[256,1024]{1,0:T(8,128)(2,1)}, bf16[256,1024]{1,0:T(8,128)(2,1)S(1)}, u32[]{:S(2)}, u32[]{:S(2)}) collective-permute-start(bf16[256,1024]{1,0:T(8,128)(2,1)} %k_hbm.1), channel_id=1, source_target_pairs={{0,8},{8,0},{16,24},{24,16},{1,9},{9,1},{17,25},{25,17},{2,10},{10... | collective-permute-start | bytes 1572872 | tf_op jit(solution)/shard_map/ppermute | solution.py:251
  0.5 7.1 %collective-permute-start.1 = (bf16[256,1024]{1,0:T(8,128)(2,1)}, bf16[256,1024]{1,0:T(8,128)(2,1)S(1)}, u32[]{:S(2)}, u32[]{:S(2)}) collective-permute-start(bf16[256,1024]{1,0:T(8,128)(2,1)} %v_hbm.1), channel_id=1, source_target_pairs={{0,8},{8,0},{16,24},{24,16},{1,9},{9,1},{17,25},{25,17},{2,10},{10... | collective-permute-start | bytes 1572872 | tf_op jit(solution)/shard_map/ppermute | solution.py:252
  1.6 9.9 %collective-permute-start.2 = (bf16[256,512]{1,0:T(8,128)(2,1)S(1)}, bf16[256,512]{1,0:T(8,128)(2,1)S(1)}, u32[]{:S(2)}, u32[]{:S(2)}) collective-permute-start(bf16[256,512]{1,0:T(8,128)(2,1)S(1)} %slice_select_fusion), channel_id=1, source_target_pairs={{0,16},{8,24},{16,0},{24,8},{1,17},{9,25},{17,1},{25,9},{2,18},{10... | collective-permute-start | bytes 786440 | tf_op jit(solution)/shard_map/ppermute | solution.py:245
  5.6 11.3 %collective-permute-start.4 = (bf16[256,512]{1,0:T(8,128)(2,1)S(1)}, bf16[256,512]{1,0:T(8,128)(2,1)S(1)}, u32[]{:S(2)}, u32[]{:S(2)}) collective-permute-start(bf16[256,512]{1,0:T(8,128)(2,1)S(1)} %slice.11), channel_id=1, source_target_pairs={{0,16},{8,24},{1,17},{9,25},{2,18},{10,26},{3,19},{11,27},{4,20},{... | collective-permute-start | bytes 786440 | tf_op jit(solution)/shard_map/ppermute | solution.py:280
  13.2 8.7 %collective-permute-start.6 = (bf16[272,512]{1,0:T(8,128)(2,1)S(1)}, bf16[272,512]{1,0:T(8,128)(2,1)S(1)}, u32[]{:S(2)}, u32[]{:S(2)}) collective-permute-start(bf16[272,512]{1,0:T(8,128)(2,1)S(1)} %cross.1), channel_id=1, source_target_pairs={{0,16},{8,24},{1,17},{9,25},{2,18},{10,26},{3,19},{11,27},{4,20},{... | collective-permute-start | bytes 835592 | tf_op jit(solution)/shard_map/ppermute | solution.py:296
  17.0 1.5 %collective-permute-start.5 = (bf16[256,512]{1,0:T(8,128)(2,1)S(1)}, bf16[256,512]{1,0:T(8,128)(2,1)S(1)}, u32[]{:S(2)}, u32[]{:S(2)}) collective-permute-start(bf16[256,512]{1,0:T(8,128)(2,1)S(1)} %collective-permute-done.4.refs_2_), channel_id=1, source_target_pairs={{0,8},{8,0},{16,24},{24,16},{1,9},{9,1},{17,25},{25,17},{2,10},{10... | collective-permute-start | bytes 786440 | tf_op jit(solution)/shard_map/ppermute | solution.py:284
  17.0 1.9 %collective-permute-start.3 = (bf16[256,512]{1,0:T(8,128)(2,1)S(1)}, bf16[256,512]{1,0:T(8,128)(2,1)S(1)}, u32[]{:S(2)}, u32[]{:S(2)}) collective-permute-start(bf16[256,512]{1,0:T(8,128)(2,1)S(1)} %collective-permute-done.2.refs_0_.q_ref), channel_id=1, source_target_pairs={{0,8},{8,0},{16,24},{24,16},{1,9},{9,1},{17,25},{25,17},{2,10},{10... | collective-permute-start | bytes 786440 | tf_op jit(solution)/shard_map/ppermute | solution.py:283
  23.3 12.1 %collective-permute-start.8 = (bf16[128,1024]{1,0:T(8,128)(2,1)S(1)}, bf16[128,1024]{1,0:T(8,128)(2,1)S(1)}, u32[]{:S(2)}, u32[]{:S(2)}) collective-permute-start(bf16[128,1024]{1,0:T(8,128)(2,1)S(1)} %get-tuple-element.25), channel_id=1, source_target_pairs={{0,2},{2,0},{4,6},{6,4},{1,3},{3,1},{5,7},{7,5},{8,10},{10,8},{12,... | collective-permute-start | bytes 786440 | tf_op jit(solution)/shard_map/ppermute | solution.py:374
  26.3 19.4 %collective-permute-start.10 = (bf16[128,1024]{1,0:T(8,128)(2,1)S(1)}, bf16[128,1024]{1,0:T(8,128)(2,1)S(1)}, u32[]{:S(2)}, u32[]{:S(2)}) collective-permute-start(bf16[128,1024]{1,0:T(8,128)(2,1)S(1)} %get-tuple-element.26), channel_id=1, source_target_pairs={{0,2},{2,0},{4,6},{6,4},{1,3},{3,1},{5,7},{7,5},{8,10},{10,8},{12,... | collective-permute-start | bytes 786440 | tf_op jit(solution)/shard_map/ppermute | solution.py:374
  33.8 29.3 %collective-permute-start.7 = (bf16[256,1024]{1,0:T(8,128)(2,1)S(1)}, bf16[256,1024]{1,0:T(8,128)(2,1)S(1)}, u32[]{:S(2)}, u32[]{:S(2)}) collective-permute-start(bf16[256,1024]{1,0:T(8,128)(2,1)S(1)} %project.3), channel_id=1, source_target_pairs={{0,2},{2,0},{4,6},{6,4},{1,3},{3,1},{5,7},{7,5},{8,10},{10,8},{12,... | collective-permute-start | bytes 1572872 | tf_op jit(solution)/shard_map/ppermute | solution.py:383
  35.5 17.9 %collective-permute-start.9 = (bf16[128,1024]{1,0:T(8,128)(2,1)S(1)}, bf16[128,1024]{1,0:T(8,128)(2,1)S(1)}, u32[]{:S(2)}, u32[]{:S(2)}) collective-permute-start(bf16[128,1024]{1,0:T(8,128)(2,1)S(1)} %add_convert_fusion.2), channel_id=1, source_target_pairs={{0,4},{2,6},{4,0},{6,2},{1,5},{3,7},{5,1},{7,3},{8,12},{10,14},{12... | collective-permute-start | bytes 786440 | tf_op jit(solution)/shard_map/ppermute | solution.py:374
  45.8 17.3 %collective-permute-start.11 = (bf16[128,1024]{1,0:T(8,128)(2,1)S(1)}, bf16[128,1024]{1,0:T(8,128)(2,1)S(1)}, u32[]{:S(2)}, u32[]{:S(2)}) collective-permute-start(bf16[128,1024]{1,0:T(8,128)(2,1)S(1)} %add_convert_fusion.1), channel_id=1, source_target_pairs={{0,4},{2,6},{4,0},{6,2},{1,5},{3,7},{5,1},{7,3},{8,12},{10,14},{12... | collective-permute-start | bytes 786440 | tf_op jit(solution)/shard_map/ppermute | solution.py:374

commit v3 on v2

--- a/solution.py
+++ b/solution.py
@@ -102,23 +102,25 @@
     return -(-3 * shipped // 16) * 16
 
 
-def cross_kernel(count, half, skip, place_ref, q_ref, *refs):
+def cross_kernel(count, half, skip, lo, place_ref, q_ref, *refs):
     k_refs, v_refs = refs[:count], refs[count : 2 * count]
     (out_ref,) = refs[2 * count :]
-    rows, width = q_ref.shape
+    width = q_ref.shape[1]
     shipped = width // HD
+    extra = lse_rows(shipped)
+    rows = out_ref.shape[0] - extra
 
     @pl.when(place_ref[0] < half)
     def _():
         found = jnp.zeros((rows, LANES), jnp.float32)
         for h in range(width // HD):
             at, there = slice(h * HD, (h + 1) * HD), slice(skip + h * HD, skip + (h + 1) * HD)
+            query = q_ref[lo : lo + rows, at]
             result, lse = softmax_rows(
-                q_ref[:, at], [k[:, there] for k in k_refs], [v[:, there] for v in v_refs], [None] * count, HD**-0.5
+                query, [k[:, there] for k in k_refs], [v[:, there] for v in v_refs], [None] * count, HD**-0.5
             )
             out_ref[:rows, at] = result.astype(out_ref.dtype)
             found = put_lse(found, h, shipped, lse)
-        extra = out_ref.shape[0] - rows
         out_ref[rows:, :rows] = lse_terms(found, shipped).T[:extra].astype(out_ref.dtype)
 
 
@@ -126,32 +128,25 @@
     return (own.astype(jnp.float32) * share + far.astype(jnp.float32) * (1.0 - share)).astype(out_dtype)
 
 
-def load_kernel(loads, place_ref, w_hbm, w_ref, sems):
-    copies = column_copies(place_ref, loads, w_hbm, w_ref, sems, 0)
-    for copy in copies:
-        copy.start()
-    for copy in copies:
-        copy.wait()
-
-
-def far_kernel(count, half, place_ref, q_ref, own_ref, lse_ref, *refs):
+def far_kernel(count, half, lo, place_ref, q_ref, own_ref, lse_ref, *refs):
     k_refs, v_refs = refs[:count], refs[count : 2 * count]
     (out_ref,) = refs[2 * count :]
     width = out_ref.shape[1]
+    rows = slice(lo, lo + out_ref.shape[0])
 
     @pl.when(place_ref[0] < half)
     def _():
-        out_ref[...] = own_ref[:, :width]
+        out_ref[...] = own_ref[rows, :width]
 
     @pl.when(place_ref[0] >= half)
     def _():
         for h in range(width // HD):
             at = slice(h * HD, (h + 1) * HD)
             result, lse = softmax_rows(
-                q_ref[:, at], [k[:, at] for k in k_refs], [v[:, at] for v in v_refs], [None] * count, HD**-0.5
+                q_ref[rows, at], [k[:, at] for k in k_refs], [v[:, at] for v in v_refs], [None] * count, HD**-0.5
             )
-            share = 1.0 / (1.0 + jnp.exp2(lse - lse_ref[:, h : h + 1]))
-            out_ref[:, at] = mix(own_ref[:, at], result, share, out_ref.dtype)
+            share = 1.0 / (1.0 + jnp.exp2(lse - lse_ref[rows, h : h + 1]))
+            out_ref[:, at] = mix(own_ref[rows, at], result, share, out_ref.dtype)
 
 
 def project(rows, image, first, w_ref, out_ref):
@@ -170,7 +165,7 @@
     count, _ = att_ref.shape
     rows = slice(lo, lo + count)
     skip, shipped = near_ref.shape[1], back_ref.shape[1] // HD
-    att_ref[:, :skip] = near_ref[rows, :]
+    att_ref[:, :skip] = near_ref[...]
 
     @pl.when(place_ref[0] < half)
     def _():
@@ -178,7 +173,7 @@
 
     @pl.when(place_ref[0] >= half)
     def _():
-        terms = back_ref[own_ref.shape[0] :, rows].astype(jnp.float32)
+        terms = back_ref[count:, :count].astype(jnp.float32)
         far_lse = sum(terms[i * shipped : (i + 1) * shipped] for i in range(3))
         before = skip // HD
         far_lse = jnp.concatenate(
@@ -193,7 +188,7 @@
         for h in range(shipped):
             at, there = slice(h * HD, (h + 1) * HD), slice(skip + h * HD, skip + (h + 1) * HD)
             share = mine[:, before + h : before + h + 1]
-            att_ref[:, there] = mix(own_ref[rows, there], back_ref[rows, at], share, att_ref.dtype)
+            att_ref[:, there] = mix(own_ref[rows, there], back_ref[:count, at], share, att_ref.dtype)
 
     project(att_ref[...], kinds_ref[rows, :1] == 1, first, w_ref, out_ref)
 
@@ -231,7 +226,7 @@
         return [(i, i ^ bit) for i in range(count)]
 
     order = sorted(range(tp_count), reverse=True)
-    loads = [tuple(order[:1]), tuple(order[1:-1])]
+    loads = [tuple(order[:-1])]
     columns = {}
     pieces = PIECES * out_weight.shape[0]
 
@@ -241,7 +236,6 @@
     heads = width // HD
     shipped = heads // 2
     skip = (heads - shipped) * HD
-    up = [(i, i + half) for i in range(half)]
     met = lax.ppermute(
         jnp.where(place[0] >= half, queries[:, skip:], key_rows[:, : width - skip]), "seq", xor(seq_count, half)
     )
@@ -277,7 +271,7 @@
         *vals[1:],
     )
     far_keys = [met]
-    far_vals = [lax.ppermute(values[:, :skip], "seq", up)]
+    far_vals = [lax.ppermute(values[:, :skip], "seq", xor(seq_count, half))]
     bit = half // 2
     while bit:
         far_keys = far_keys + [lax.ppermute(x, "seq", xor(seq_count, bit)) for x in far_keys]
@@ -285,32 +279,27 @@
         bit //= 2
 
 
-    found = pl.pallas_call(
-        functools.partial(cross_kernel, count, half, skip),
-        out_shape=jax.ShapeDtypeStruct((rows + lse_rows(shipped), width - skip), jnp.bfloat16),
-        in_specs=[smem] + [vmem] * (1 + 2 * count),
-        out_specs=vmem,
-        compiler_params=params(8),
-        name="cross",
-    )(place, met, *keys, *vals)
-    back = lax.ppermute(found, "seq", up)
-    near = pl.pallas_call(
-        functools.partial(far_kernel, count, half),
-        out_shape=jax.ShapeDtypeStruct((rows, skip), jnp.bfloat16),
-        in_specs=[smem] + [vmem] * (3 + 2 * count),
-        out_specs=vmem,
-        compiler_params=params(8),
-        name="far",
-    )(place, own_queries, own, own_lse, *far_keys, *far_vals)
-    columns[loads[1]] = pl.pallas_call(
-        functools.partial(load_kernel, loads[1]),
-        out_shape=columns_shape(loads[1]),
-        in_specs=[smem, hbm],
-        out_specs=vmem,
-        scratch_shapes=[pltpu.SemaphoreType.DMA((pieces * len(loads[1]),))],
-        compiler_params=params(8),
-        name="load",
-    )(place, in_hbm(out_weight))
+    back, near = [], []
+    for p, (lo, hi) in enumerate(parts):
+        found = pl.pallas_call(
+            functools.partial(cross_kernel, count, half, skip, lo),
+            out_shape=jax.ShapeDtypeStruct((hi - lo + lse_rows(shipped), width - skip), jnp.bfloat16),
+            in_specs=[smem] + [vmem] * (1 + 2 * count),
+            out_specs=vmem,
+            compiler_params=params(8),
+            name="cross",
+        )(place, met, *keys, *vals)
+        back.append(lax.ppermute(found, "seq", [xor(seq_count, half), xor(seq_count, half)][p]))
+        near.append(
+            pl.pallas_call(
+                functools.partial(far_kernel, count, half, lo),
+                out_shape=jax.ShapeDtypeStruct((hi - lo, skip), jnp.bfloat16),
+                in_specs=[smem] + [vmem] * (3 + 2 * count),
+                out_specs=vmem,
+                compiler_params=params(8),
+                name="far",
+            )(place, own_queries, own, own_lse, *far_keys, *far_vals)
+        )
 
     def columns_of(offset):
         (held,) = (x for x in loads if offset in x)
@@ -329,7 +318,7 @@
             out_specs=(vmem, vmem),
             compiler_params=params(8),
             name="merge",
-        )(place, own, own_lse, near, back, kinds, weight)
+        )(place, own, own_lse, near[p], back[p], kinds, weight)
 
     def streamed(attended, offset):
         return pl.pallas_call(

time: 64.3 us -> 76.5 us (1.19)
  waiting for transfers between devices: 23.6 us -> 41.8 us
  starting transfers between devices: 17.3 us -> 11.9 us
    ppermute x2 -> x3, waiting for transfers between devices: 3.17 us -> 14.4 us  [the longest x2 8.92 us: on_device(): lax.ppermute(found, 'seq', [xor(seq_count, half), xor(seq_count, half)][p])]
    ppermute x1, waiting for transfers between devices: 0.01 us -> 5.43 us  [on_device(): lax.ppermute(jnp.where(place[0] >= half, queries[:, skip:], key_rows[:, :...]
    ppermute x1, waiting for transfers between devices: 0.01 us -> 4.78 us  [on_device(): beside = lax.ppermute(beside, 'tp', xor(tp_count, 1))]
    ppermute x1, starting transfers between devices: 3.06 us -> 0.42 us  [on_device(): lax.ppermute(jnp.where(place[0] >= half, queries[:, skip:], key_rows[:, :...]
    pallas_call x3 -> x4, Pallas kernels: 6.38 us -> 3.8 us  [the longest x2 2.68 us: on_device(): pl.pallas_call(functools.partial(cross_kernel, count, half, skip, lo), ou...]
    pallas_call x1, Pallas kernels: 3.84 us -> 5.87 us  [on_device(): pl.pallas_call(functools.partial(own_kernel, tuple(offsets), loads[0]), o...]
    ppermute x4, waiting for transfers between devices: 19 us -> 17.2 us  [on_device(): arrived = lax.ppermute(keep.pop(offset), 'tp', xor(tp_count, bit))]
    ppermute x4, starting transfers between devices: 6.58 us -> 4.95 us  [on_device(): arrived = lax.ppermute(keep.pop(offset), 'tp', xor(tp_count, bit))]
  transfers between devices with their start and end apart: 12 -> 13, of which waited for: 7 -> 7; matrix products, arithmetic and copies ran while one was open for 3% -> 3% of each run, Pallas kernels for 29% -> 24%
where the time goes in v3:
time: 76.5 us; the launch traced here: 76.3 us
  waiting for transfers between devices  41.8 us (55%)
  Pallas kernels  19.3 us (25%)
  starting transfers between devices  11.9 us (16%)
  other arithmetic  2.33 us (3%)
  local copies, waits for them, and re-layouts  0.97 us (1%)
    ppermute x4, waiting for transfers between devices, on_device(): arrived = lax.ppermute(keep.pop(offset), 'tp', xor(tp_count, bit))  17.2 us
    ppermute x2, waiting for transfers between devices, on_device(): lax.ppermute(found, 'seq', [xor(seq_count, half), xor(seq_count, half)][p])  8.92 us
    pallas_call x1, Pallas kernels, on_device(): pl.pallas_call(functools.partial(own_kernel, tuple(offsets), loads[0]), o...  5.87 us
    ppermute x1, waiting for transfers between devices, on_device(): far_vals = [lax.ppermute(values[:, :skip], 'seq', xor(seq_count, half))]  5.45 us
    ppermute x1, waiting for transfers between devices, on_device(): lax.ppermute(jnp.where(place[0] >= half, queries[:, skip:], key_rows[:, :...  5.43 us
    ppermute x4, starting transfers between devices, on_device(): arrived = lax.ppermute(keep.pop(offset), 'tp', xor(tp_count, bit))  4.95 us
    ppermute x1, waiting for transfers between devices, on_device(): beside = lax.ppermute(beside, 'tp', xor(tp_count, 1))  4.78 us
    pallas_call x1, Pallas kernels, streamed(): pl.pallas_call(functools.partial(stream_kernel, offset), out_shape=jax.Sh...  4.07 us
  transfers between devices with their start and end apart: 13, of which 7 were waited for; matrix products, arithmetic and copies ran while one was open for 3% of the time, Pallas kernels for 24%

profile of v3, /device:TPU:0, one launch (start us, length us, event | category | flops | bytes accessed | tf_op | source)
XLA Modules:
  0.0 76.3 jit_solution(4566421027705170421)
XLA Ops:
  0.0 0.5 collective-permute-start.1
  0.5 1.0 %slice.11 = bf16[256,512]{1,0:T(8,128)(2,1)S(1)} slice(bf16[256,1024]{1,0:T(8,128)(2,1)} %v_hbm.1), slice={[0:256], [0:512]} | slice | bytes 524288 | tf_op jit(solution)/shard_map/slice | solution.py:274
  1.5 2.6 %collective-permute-start.4 = (bf16[256,512]{1,0:T(8,128)(2,1)S(1)}, bf16[256,512]{1,0:T(8,128)(2,1)S(1)}, u32[]{:S(2)}, u32[]{:S(2)}) collective-permute-start(bf16[256,512]{1,0:T(8,128)(2,1)S(1)} %slice.11), channel_id=1, source_target_pairs={{0,16},{8,24},{16,0},{24,8},{1,17},{9,25},{17,1},{25,9},{2,18},{10... | collective-permute-start | bytes 786440 | tf_op jit(solution)/shard_map/ppermute | solution.py:274
  4.0 0.2 collective-permute-start
  4.3 1.1 %slice_select_fusion = bf16[256,512]{1,0:T(8,128)(2,1)S(1)} fusion(bf16[256,1024]{1,0:T(8,128)(2,1)} %k_hbm.1, bf16[256,1024]{1,0:T(8,128)(2,1)} %q_hbm.1, pred[]{:T(512)S(6)} %ge.3), kind=kLoop, calls=%fused_computation.3 | loop fusion | flops 131072 | bytes 786433 | tf_op jit(solution)/shard_map/jit(_where)/select_n | solution.py:240
  5.3 0.4 collective-permute-start.2
  5.7 5.4 %collective-permute-done.4.refs_2_ = bf16[256,512]{1,0:T(8,128)(2,1)S(1)} collective-permute-done((bf16[256,512]{1,0:T(8,128)(2,1)S(1)}, bf16[256,512]{1,0:T(8,128)(2,1)S(1)}, u32[]{:S(2)}, u32[]{:S(2)}) %collective-permute-start.4) | collective-permute-done | bytes 262176 | tf_op jit(solution)/shard_map/ppermute | solution.py:274
  11.2 0.0 collective-permute-start.5
  11.2 5.4 %collective-permute-done.2.refs_0_.q_ref = bf16[256,512]{1,0:T(8,128)(2,1)S(1)} collective-permute-done((bf16[256,512]{1,0:T(8,128)(2,1)S(1)}, bf16[256,512]{1,0:T(8,128)(2,1)S(1)}, u32[]{:S(2)}, u32[]{:S(2)}) %collective-permute-start.2) | collective-permute-done | bytes 262176 | tf_op jit(solution)/shard_map/ppermute | solution.py:239
  16.6 0.0 collective-permute-start.3
  16.6 0.1 pad_add_fusion.place_ref
  16.7 0.0 collective-permute-done.refs_0_.refs_1_
  16.7 0.0 collective-permute-done.1.refs_1_.refs_3_
  16.7 5.9 %own.1 = (bf16[256,1024]{1,0:T(8,128)(2,1)S(1)}, f32[256,128]{1,0:T(8,128)S(1)}, bf16[256,1024]{1,0:T(8,128)(2,1)S(1)}, bf16[256,1024]{1,0:T(8,128)(2,1)S(1)}, b...) custom-call(s32[2]{0:T(128)S(1)} %pad_add_fusion.place_ref, ...), custom_call_target="tpu_custom_call" | custom-call | tf_op jit(solution)/shard_map/own/pallas_call | solution.py:251
  22.6 1.3 %cross.3 = bf16[144,512]{1,0:T(8,128)(2,1)S(1)} custom-call(s32[2]{0:T(128)S(1)} %pad_add_fusion.place_ref, bf16[256,512]{1,0:T(8,128)(2,1)S(1)} %collective-permute-done.2.refs_0_.q_ref, bf16[256,1024]{1,0:T(8,128)(2,1)S(1)} %get-tuple-element.20.refs_0_, bf16[256,1024]{1,0:T(8,128)(2,1)S(1)} %collective-permute-done.refs_0_.refs_1_, ...), custom_call_target="tpu_custom_call" | custom-call | tf_op jit(solution)/shard_map/cross/pallas_call | solution.py:284
  23.9 1.0 %collective-permute-start.7 = (bf16[144,512]{1,0:T(8,128)(2,1)S(1)}, bf16[144,512]{1,0:T(8,128)(2,1)S(1)}, u32[]{:S(2)}, u32[]{:S(2)}) collective-permute-start(bf16[144,512]{1,0:T(8,128)(2,1)S(1)} %cross.3), channel_id=1, source_target_pairs={{0,16},{8,24},{16,0},{24,8},{1,17},{9,25},{17,1},{25,9},{2,18},{10... | collective-permute-start | bytes 442376 | tf_op jit(solution)/shard_map/ppermute | solution.py:292
  25.0 0.0 collective-permute-done.5.refs_3_
  25.0 0.0 collective-permute-done.3.refs_1_
  25.0 0.6 far.3.near_ref
  25.5 4.7 %collective-permute-done.7.back_ref = bf16[144,512]{1,0:T(8,128)(2,1)S(1)} collective-permute-done((bf16[144,512]{1,0:T(8,128)(2,1)S(1)}, bf16[144,512]{1,0:T(8,128)(2,1)S(1)}, u32[]{:S(2)}, u32[]{:S(2)}) %collective-permute-start.7) | collective-permute-done | bytes 147488 | tf_op jit(solution)/shard_map/ppermute | solution.py:292
  30.2 1.3 %merge.3 = (bf16[128,1024]{1,0:T(8,128)(2,1)S(1)}, bf16[128,1024]{1,0:T(8,128)(2,1)S(1)}) custom-call(s32[2]{0:T(128)S(1)} %pad_add_fusion.place_ref, bf16[256,1024]{1,0:T(8,128)(2,1)S(1)} %get-tuple-element.17.own_ref, f32[256,128]{1,0:T(8,128)S(1)} %get-tuple-element.18.lse_ref, bf16[128,512]{1,0:T(8,128)(2,1)S(1)} %far.3.near_ref, ...), custom_call_target="tpu_custom_call" | custom-call | tf_op jit(solution)/shard_map/merge/pallas_call | solution.py:311
  31.6 1.9 %collective-permute-start.11 = (bf16[128,1024]{1,0:T(8,128)(2,1)S(1)}, bf16[128,1024]{1,0:T(8,128)(2,1)S(1)}, u32[]{:S(2)}, u32[]{:S(2)}) collective-permute-start(bf16[128,1024]{1,0:T(8,128)(2,1)S(1)} %get-tuple-element.26), channel_id=1, source_target_pairs={{0,2},{2,0},{4,6},{6,4},{1,3},{3,1},{5,7},{7,5},{8,10},{10,8},{12,... | collective-permute-start | bytes 786440 | tf_op jit(solution)/shard_map/ppermute | solution.py:363
  33.4 1.3 %cross.2 = bf16[144,512]{1,0:T(8,128)(2,1)S(1)} custom-call(s32[2]{0:T(128)S(1)} %pad_add_fusion.place_ref, bf16[256,512]{1,0:T(8,128)(2,1)S(1)} %collective-permute-done.2.refs_0_.q_ref, bf16[256,1024]{1,0:T(8,128)(2,1)S(1)} %get-tuple-element.20.refs_0_, bf16[256,1024]{1,0:T(8,128)(2,1)S(1)} %collective-permute-done.refs_0_.refs_1_, ...), custom_call_target="tpu_custom_call" | custom-call | tf_op jit(solution)/shard_map/cross/pallas_call | solution.py:284
  34.8 0.4 collective-permute-start.6
  35.2 0.6 far.2.near_ref
  35.7 4.2 %collective-permute-done.6.back_ref = bf16[144,512]{1,0:T(8,128)(2,1)S(1)} collective-permute-done((bf16[144,512]{1,0:T(8,128)(2,1)S(1)}, bf16[144,512]{1,0:T(8,128)(2,1)S(1)}, u32[]{:S(2)}, u32[]{:S(2)}) %collective-permute-start.6) | collective-permute-done | bytes 147488 | tf_op jit(solution)/shard_map/ppermute | solution.py:292
  39.9 1.3 %merge.2 = (bf16[128,1024]{1,0:T(8,128)(2,1)S(1)}, bf16[128,1024]{1,0:T(8,128)(2,1)S(1)}) custom-call(s32[2]{0:T(128)S(1)} %pad_add_fusion.place_ref, bf16[256,1024]{1,0:T(8,128)(2,1)S(1)} %get-tuple-element.17.own_ref, f32[256,128]{1,0:T(8,128)S(1)} %get-tuple-element.18.lse_ref, bf16[128,512]{1,0:T(8,128)(2,1)S(1)} %far.2.near_ref, ...), custom_call_target="tpu_custom_call" | custom-call | tf_op jit(solution)/shard_map/merge/pallas_call | solution.py:311
  41.3 0.4 collective-permute-start.9
  41.7 0.8 %project.5 = bf16[128,1024]{1,0:T(8,128)(2,1)S(1)} custom-call(f32[256,128]{1,0:T(8,128)S(1)} %get-tuple-element.16.kinds_ref, bf16[2,1024,3072]{2,1,0:T(8,128)(2,1)S(1)} %get-tuple-element.22.w_ref, bf16[128,1024]{1,0:T(8,128)(2,1)S(1)} %get-tuple-element.24.refs_1_.refs_0_), custom_call_target="tpu_custom_call" | custom-call | tf_op jit(solution)/shard_map/project/pallas_call | solution.py:339
  42.4 0.8 %project.4 = bf16[128,1024]{1,0:T(8,128)(2,1)S(1)} custom-call(f32[256,128]{1,0:T(8,128)S(1)} %get-tuple-element.16.kinds_ref, bf16[2,1024,3072]{2,1,0:T(8,128)(2,1)S(1)} %get-tuple-element.22.w_ref, bf16[128,1024]{1,0:T(8,128)(2,1)S(1)} %get-tuple-element.23.refs_0_), custom_call_target="tpu_custom_call" | custom-call | tf_op jit(solution)/shard_map/project/pallas_call | solution.py:339
  43.2 1.3 %project.3 = bf16[256,1024]{1,0:T(8,128)(2,1)S(1)} custom-call(f32[256,128]{1,0:T(8,128)S(1)} %get-tuple-element.16.kinds_ref, bf16[2,1024,3072]{2,1,0:T(8,128)(2,1)S(1)} %get-tuple-element.22.w_ref, bf16[128,1024]{1,0:T(8,128)(2,1)S(1)} %get-tuple-element.23.refs_0_, bf16[128,1024]{1,0:T(8,128)(2,1)S(1)} %get-tuple-element.24.refs_1_.refs_0_), custom_call_target="tpu_custom_call" | custom-call | tf_op jit(solution)/shard_map/project/pallas_call | solution.py:339
  44.5 1.8 %collective-permute-start.8 = (bf16[256,1024]{1,0:T(8,128)(2,1)S(1)}, bf16[256,1024]{1,0:T(8,128)(2,1)S(1)}, u32[]{:S(2)}, u32[]{:S(2)}) collective-permute-start(bf16[256,1024]{1,0:T(8,128)(2,1)S(1)} %project.3), channel_id=1, source_target_pairs={{0,2},{2,0},{4,6},{6,4},{1,3},{3,1},{5,7},{7,5},{8,10},{10,8},{12,... | collective-permute-start | bytes 1572872 | tf_op jit(solution)/shard_map/ppermute | solution.py:372
  46.3 0.0 collective-permute-done.11
  46.4 0.1 add_convert_fusion.1
  46.4 2.7 %collective-permute-start.12 = (bf16[128,1024]{1,0:T(8,128)(2,1)S(1)}, bf16[128,1024]{1,0:T(8,128)(2,1)S(1)}, u32[]{:S(2)}, u32[]{:S(2)}) collective-permute-start(bf16[128,1024]{1,0:T(8,128)(2,1)S(1)} %add_convert_fusion.1), channel_id=1, source_target_pairs={{0,4},{2,6},{4,0},{6,2},{1,5},{3,7},{5,1},{7,3},{8,12},{10,14},{12... | collective-permute-start | bytes 786440 | tf_op jit(solution)/shard_map/ppermute | solution.py:363
  49.1 9.9 %collective-permute-done.9 = bf16[128,1024]{1,0:T(8,128)(2,1)S(1)} collective-permute-done((bf16[128,1024]{1,0:T(8,128)(2,1)S(1)}, bf16[128,1024]{1,0:T(8,128)(2,1)S(1)}, u32[]{:S(2)}, u32[]{:S(2)}) %collective-permute-start.9) | collective-permute-done | bytes 262176 | tf_op jit(solution)/shard_map/ppermute | solution.py:363
  59.0 0.1 add_convert_fusion.2
  59.0 0.1 collective-permute-start.10
  59.1 4.1 %stream.1 = bf16[256,1024]{1,0:T(8,128)(2,1)S(1)} custom-call(s32[2]{0:T(128)S(1)} %pad_add_fusion.place_ref, bf16[2,1024,4096]{2,1,0:T(8,128)(2,1)} %w_hbm.3, f32[256,128]{1,0:T(8,128)S(1)} %get-tuple-element.16.kinds_ref, bf16[128,1024]{1,0:T(8,128)(2,1)S(1)} %get-tuple-element.23.refs_0_, bf16[128,1024]{1,0:T(8,128)(2,1)S(1)} %get-tuple-element.24.refs_1_.refs_0_), custom_call_target="tpu_custom_call" | custom-call | tf_op jit(solution)/shard_map/stream/pallas_call | solution.py:324
  63.2 4.8 %collective-permute-done.8 = bf16[256,1024]{1,0:T(8,128)(2,1)S(1)} collective-permute-done((bf16[256,1024]{1,0:T(8,128)(2,1)S(1)}, bf16[256,1024]{1,0:T(8,128)(2,1)S(1)}, u32[]{:S(2)}, u32[]{:S(2)}) %collective-permute-start.8) | collective-permute-done | bytes 524320 | tf_op jit(solution)/shard_map/ppermute | solution.py:372
  68.0 0.0 collective-permute-done.12
  68.0 7.3 %collective-permute-done.10 = bf16[128,1024]{1,0:T(8,128)(2,1)S(1)} collective-permute-done((bf16[128,1024]{1,0:T(8,128)(2,1)S(1)}, bf16[128,1024]{1,0:T(8,128)(2,1)S(1)}, u32[]{:S(2)}, u32[]{:S(2)}) %collective-permute-start.10) | collective-permute-done | bytes 262176 | tf_op jit(solution)/shard_map/ppermute | solution.py:363
  75.3 1.1 %add_convert_fusion = bf16[256,1024]{1,0:T(8,128)(2,1)} fusion(bf16[256,1024]{1,0:T(8,128)(2,1)S(1)} %collective-permute-done.8, bf16[256,1024]{1,0:T(8,128)(2,1)S(1)} %stream.1, bf16[128,1024]{1,0:T(8,128)(2,1)S(1)} %collective-permute-done.12, bf16[128,1024]{1,0:T(8,128)(2,1)S(1)} %collective-permute-done.10), kind=kLoop, calls=%fused_computation | loop fusion | flops 2359296 | bytes 2097152 | tf_op jit(solution)/shard_map/convert_element_type | solution.py:377
Async XLA Ops:
  0.0 16.7 %collective-permute-start.1 = (bf16[256,1024]{1,0:T(8,128)(2,1)}, bf16[256,1024]{1,0:T(8,128)(2,1)S(1)}, u32[]{:S(2)}, u32[]{:S(2)}) collective-permute-start(bf16[256,1024]{1,0:T(8,128)(2,1)} %v_hbm.1), channel_id=1, source_target_pairs={{0,8},{8,0},{16,24},{24,16},{1,9},{9,1},{17,25},{25,17},{2,10},{10... | collective-permute-start | bytes 1572872 | tf_op jit(solution)/shard_map/ppermute | solution.py:246
  1.5 9.7 %collective-permute-start.4 = (bf16[256,512]{1,0:T(8,128)(2,1)S(1)}, bf16[256,512]{1,0:T(8,128)(2,1)S(1)}, u32[]{:S(2)}, u32[]{:S(2)}) collective-permute-start(bf16[256,512]{1,0:T(8,128)(2,1)S(1)} %slice.11), channel_id=1, source_target_pairs={{0,16},{8,24},{16,0},{24,8},{1,17},{9,25},{17,1},{25,9},{2,18},{10... | collective-permute-start | bytes 786440 | tf_op jit(solution)/shard_map/ppermute | solution.py:274
  4.0 12.7 %collective-permute-start = (bf16[256,1024]{1,0:T(8,128)(2,1)}, bf16[256,1024]{1,0:T(8,128)(2,1)S(1)}, u32[]{:S(2)}, u32[]{:S(2)}) collective-permute-start(bf16[256,1024]{1,0:T(8,128)(2,1)} %k_hbm.1), channel_id=1, source_target_pairs={{0,8},{8,0},{16,24},{24,16},{1,9},{9,1},{17,25},{25,17},{2,10},{10... | collective-permute-start | bytes 1572872 | tf_op jit(solution)/shard_map/ppermute | solution.py:245
  5.3 11.3 %collective-permute-start.2 = (bf16[256,512]{1,0:T(8,128)(2,1)S(1)}, bf16[256,512]{1,0:T(8,128)(2,1)S(1)}, u32[]{:S(2)}, u32[]{:S(2)}) collective-permute-start(bf16[256,512]{1,0:T(8,128)(2,1)S(1)} %slice_select_fusion), channel_id=1, source_target_pairs={{0,16},{8,24},{16,0},{24,8},{1,17},{9,25},{17,1},{25,9},{2,18},{10... | collective-permute-start | bytes 786440 | tf_op jit(solution)/shard_map/ppermute | solution.py:239
  11.2 13.8 %collective-permute-start.5 = (bf16[256,512]{1,0:T(8,128)(2,1)S(1)}, bf16[256,512]{1,0:T(8,128)(2,1)S(1)}, u32[]{:S(2)}, u32[]{:S(2)}) collective-permute-start(bf16[256,512]{1,0:T(8,128)(2,1)S(1)} %collective-permute-done.4.refs_2_), channel_id=1, source_target_pairs={{0,8},{8,0},{16,24},{24,16},{1,9},{9,1},{17,25},{25,17},{2,10},{10... | collective-permute-start | bytes 786440 | tf_op jit(solution)/shard_map/ppermute | solution.py:278
  16.6 8.3 %collective-permute-start.3 = (bf16[256,512]{1,0:T(8,128)(2,1)S(1)}, bf16[256,512]{1,0:T(8,128)(2,1)S(1)}, u32[]{:S(2)}, u32[]{:S(2)}) collective-permute-start(bf16[256,512]{1,0:T(8,128)(2,1)S(1)} %collective-permute-done.2.refs_0_.q_ref), channel_id=1, source_target_pairs={{0,8},{8,0},{16,24},{24,16},{1,9},{9,1},{17,25},{25,17},{2,10},{10... | collective-permute-start | bytes 786440 | tf_op jit(solution)/shard_map/ppermute | solution.py:277
  23.9 6.3 %collective-permute-start.7 = (bf16[144,512]{1,0:T(8,128)(2,1)S(1)}, bf16[144,512]{1,0:T(8,128)(2,1)S(1)}, u32[]{:S(2)}, u32[]{:S(2)}) collective-permute-start(bf16[144,512]{1,0:T(8,128)(2,1)S(1)} %cross.3), channel_id=1, source_target_pairs={{0,16},{8,24},{16,0},{24,8},{1,17},{9,25},{17,1},{25,9},{2,18},{10... | collective-permute-start | bytes 442376 | tf_op jit(solution)/shard_map/ppermute | solution.py:292
  31.6 14.8 %collective-permute-start.11 = (bf16[128,1024]{1,0:T(8,128)(2,1)S(1)}, bf16[128,1024]{1,0:T(8,128)(2,1)S(1)}, u32[]{:S(2)}, u32[]{:S(2)}) collective-permute-start(bf16[128,1024]{1,0:T(8,128)(2,1)S(1)} %get-tuple-element.26), channel_id=1, source_target_pairs={{0,2},{2,0},{4,6},{6,4},{1,3},{3,1},{5,7},{7,5},{8,10},{10,8},{12,... | collective-permute-start | bytes 786440 | tf_op jit(solution)/shard_map/ppermute | solution.py:363
  34.8 5.2 %collective-permute-start.6 = (bf16[144,512]{1,0:T(8,128)(2,1)S(1)}, bf16[144,512]{1,0:T(8,128)(2,1)S(1)}, u32[]{:S(2)}, u32[]{:S(2)}) collective-permute-start(bf16[144,512]{1,0:T(8,128)(2,1)S(1)} %cross.2), channel_id=1, source_target_pairs={{0,16},{8,24},{16,0},{24,8},{1,17},{9,25},{17,1},{25,9},{2,18},{10... | collective-permute-start | bytes 442376 | tf_op jit(solution)/shard_map/ppermute | solution.py:292
  41.3 17.7 %collective-permute-start.9 = (bf16[128,1024]{1,0:T(8,128)(2,1)S(1)}, bf16[128,1024]{1,0:T(8,128)(2,1)S(1)}, u32[]{:S(2)}, u32[]{:S(2)}) collective-permute-start(bf16[128,1024]{1,0:T(8,128)(2,1)S(1)} %get-tuple-element.25), channel_id=1, source_target_pairs={{0,2},{2,0},{4,6},{6,4},{1,3},{3,1},{5,7},{7,5},{8,10},{10,8},{12,... | collective-permute-start | bytes 786440 | tf_op jit(solution)/shard_map/ppermute | solution.py:363
  44.5 23.5 %collective-permute-start.8 = (bf16[256,1024]{1,0:T(8,128)(2,1)S(1)}, bf16[256,1024]{1,0:T(8,128)(2,1)S(1)}, u32[]{:S(2)}, u32[]{:S(2)}) collective-permute-start(bf16[256,1024]{1,0:T(8,128)(2,1)S(1)} %project.3), channel_id=1, source_target_pairs={{0,2},{2,0},{4,6},{6,4},{1,3},{3,1},{5,7},{7,5},{8,10},{10,8},{12,... | collective-permute-start | bytes 1572872 | tf_op jit(solution)/shard_map/ppermute | solution.py:372
  46.4 21.6 %collective-permute-start.12 = (bf16[128,1024]{1,0:T(8,128)(2,1)S(1)}, bf16[128,1024]{1,0:T(8,128)(2,1)S(1)}, u32[]{:S(2)}, u32[]{:S(2)}) collective-permute-start(bf16[128,1024]{1,0:T(8,128)(2,1)S(1)} %add_convert_fusion.1), channel_id=1, source_target_pairs={{0,4},{2,6},{4,0},{6,2},{1,5},{3,7},{5,1},{7,3},{8,12},{10,14},{12... | collective-permute-start | bytes 786440 | tf_op jit(solution)/shard_map/ppermute | solution.py:363
  59.0 16.2 %collective-permute-start.10 = (bf16[128,1024]{1,0:T(8,128)(2,1)S(1)}, bf16[128,1024]{1,0:T(8,128)(2,1)S(1)}, u32[]{:S(2)}, u32[]{:S(2)}) collective-permute-start(bf16[128,1024]{1,0:T(8,128)(2,1)S(1)} %add_convert_fusion.2), channel_id=1, source_target_pairs={{0,4},{2,6},{4,0},{6,2},{1,5},{3,7},{5,1},{7,3},{8,12},{10,14},{12... | collective-permute-start | bytes 786440 | tf_op jit(solution)/shard_map/ppermute | solution.py:363

commit v4 on v3

--- a/solution.py
+++ b/solution.py
@@ -13,6 +13,7 @@
 LANES = 128
 SHARES = (1, 2)
 BLOCK = 256
+SLICES = 4
 PIECES = 4
 LOG2E = float(np.log2(np.e))
 
@@ -109,6 +110,7 @@
     shipped = width // HD
     extra = lse_rows(shipped)
     rows = out_ref.shape[0] - extra
+    out_ref[...] = jnp.zeros_like(out_ref)
 
     @pl.when(place_ref[0] < half)
     def _():
@@ -165,32 +167,28 @@
     count, _ = att_ref.shape
     rows = slice(lo, lo + count)
     skip, shipped = near_ref.shape[1], back_ref.shape[1] // HD
-    att_ref[:, :skip] = near_ref[...]
-
-    @pl.when(place_ref[0] < half)
-    def _():
-        att_ref[:, skip:] = own_ref[rows, skip:]
-
-    @pl.when(place_ref[0] >= half)
-    def _():
-        terms = back_ref[count:, :count].astype(jnp.float32)
-        far_lse = sum(terms[i * shipped : (i + 1) * shipped] for i in range(3))
-        before = skip // HD
-        far_lse = jnp.concatenate(
-            [
-                jnp.zeros((before, count), jnp.float32),
-                far_lse,
-                jnp.zeros((LANES - before - shipped, count), jnp.float32),
-            ],
-            axis=0,
-        ).T
-        mine = 1.0 / (1.0 + jnp.exp2(far_lse - lse_ref[rows, :]))
-        for h in range(shipped):
-            at, there = slice(h * HD, (h + 1) * HD), slice(skip + h * HD, skip + (h + 1) * HD)
-            share = mine[:, before + h : before + h + 1]
-            att_ref[:, there] = mix(own_ref[rows, there], back_ref[:count, at], share, att_ref.dtype)
-
-    project(att_ref[...], kinds_ref[rows, :1] == 1, first, w_ref, out_ref)
+    upper = place_ref[0] >= half
+    terms = back_ref[count:, :count].astype(jnp.float32)
+    far_lse = sum(terms[i * shipped : (i + 1) * shipped] for i in range(3))
+    before = skip // HD
+    far_lse = jnp.concatenate(
+        [
+            jnp.zeros((before, count), jnp.float32),
+            far_lse,
+            jnp.zeros((LANES - before - shipped, count), jnp.float32),
+        ],
+        axis=0,
+    ).T
+    mine = 1.0 / (1.0 + jnp.exp2(far_lse - lse_ref[rows, :]))
+    pieces = [near_ref[...]]
+    for h in range(shipped):
+        at, there = slice(h * HD, (h + 1) * HD), slice(skip + h * HD, skip + (h + 1) * HD)
+        share = mine[:, before + h : before + h + 1]
+        alone = own_ref[rows, there]
+        pieces.append(jnp.where(upper, mix(alone, back_ref[:count, at], share, att_ref.dtype), alone))
+    merged = jnp.concatenate(pieces, axis=1)
+    att_ref[...] = merged
+    project(merged, kinds_ref[rows, :1] == 1, first, w_ref, out_ref)
 
 
 def stream_kernel(offset, place_ref, w_hbm, kinds_ref, *refs):
@@ -207,6 +205,24 @@
     att_refs, out_ref = refs[:-1], refs[-1]
     rows = jnp.concatenate([x[...] for x in att_refs], axis=0)
     project(rows, kinds_ref[lo : lo + rows.shape[0], :1] == 1, first, w_ref, out_ref)
+
+
+def total_kernel(parts, first_ref, second_ref, *refs):
+    *arrived, out_hbm, out_ref, sems = refs
+    each = len(arrived) // len(parts)
+    copies = []
+    for p, (lo, hi) in enumerate(parts):
+        piece = (hi - lo) // SLICES
+        for start in range(0, hi - lo, piece):
+            rows, here = slice(lo + start, lo + start + piece), slice(start, start + piece)
+            total = first_ref[rows, :].astype(jnp.float32) + second_ref[rows, :].astype(jnp.float32)
+            for ref in arrived[p * each : (p + 1) * each]:
+                total += ref[here, :].astype(jnp.float32)
+            out_ref[rows, :] = total.astype(out_ref.dtype)
+            copies.append(pltpu.make_async_copy(out_ref.at[rows], out_hbm.at[rows], sems.at[len(copies)]))
+            copies[-1].start()
+    for copy in copies:
+        copy.wait()
 
 
 def on_device(queries, key_rows, values, modality, out_weight):
@@ -371,10 +387,15 @@
     beside = projected(0, attended, 1)
     beside = lax.ppermute(beside, "tp", xor(tp_count, 1))
     total = streamed(attended, 0)
-    total = add(total, beside)
-    for arrivals in zip(*sums):
-        total = add(total, jnp.concatenate(arrivals, axis=0))
-    return total.astype(jnp.bfloat16)
+    return pl.pallas_call(
+        functools.partial(total_kernel, tuple(parts)),
+        out_shape=jax.ShapeDtypeStruct((rows, chunk), jnp.bfloat16),
+        in_specs=[vmem] * (2 + sum(len(x) for x in sums)),
+        out_specs=pl.BlockSpec(memory_space=pltpu.HBM),
+        scratch_shapes=[pltpu.VMEM((rows, chunk), jnp.bfloat16), pltpu.SemaphoreType.DMA((len(parts) * SLICES,))],
+        compiler_params=params(8),
+        name="total",
+    )(total, beside, *(x for arrivals in sums for x in arrivals))
 
 
 def solution(mesh):

time: 76.5 us -> 76.7 us (level)
  Pallas kernels: 19.3 us -> 20.6 us
  other arithmetic: 2.33 us -> 1.27 us
    convert_element_type x1 -> x0, other arithmetic: 1.06 us -> none  [on_device(): return total.astype(jnp.bfloat16)]
    pallas_call x0 -> x1, Pallas kernels: none -> 0.89 us  [on_device(): pl.pallas_call(functools.partial(total_kernel, tuple(parts)), out_shape=j...]
where the time goes in v4:
time: 76.7 us; the launch traced here: 76.6 us
  waiting for transfers between devices  42.1 us (55%)
  Pallas kernels  20.6 us (27%)
  starting transfers between devices  11.5 us (15%)
  other arithmetic  1.27 us (2%)
  local copies, waits for them, and re-layouts  0.97 us (1%)
    ppermute x4, waiting for transfers between devices, on_device(): arrived = lax.ppermute(keep.pop(offset), 'tp', xor(tp_count, bit))  17.2 us
    ppermute x2, waiting for transfers between devices, on_device(): lax.ppermute(found, 'seq', [xor(seq_count, half), xor(seq_count, half)][p])  9.26 us
    pallas_call x1, Pallas kernels, on_device(): pl.pallas_call(functools.partial(own_kernel, tuple(offsets), loads[0]), o...  5.87 us
    ppermute x1, waiting for transfers between devices, on_device(): far_vals = [lax.ppermute(values[:, :skip], 'seq', xor(seq_count, half))]  5.45 us
    ppermute x1, waiting for transfers between devices, on_device(): lax.ppermute(jnp.where(place[0] >= half, queries[:, skip:], key_rows[:, :...  5.43 us
    ppermute x4, starting transfers between devices, on_device(): arrived = lax.ppermute(keep.pop(offset), 'tp', xor(tp_count, bit))  4.96 us
    ppermute x1, waiting for transfers between devices, on_device(): beside = lax.ppermute(beside, 'tp', xor(tp_count, 1))  4.79 us
    pallas_call x1, Pallas kernels, streamed(): pl.pallas_call(functools.partial(stream_kernel, offset), out_shape=jax.Sh...  4.07 us
  transfers between devices with their start and end apart: 13, of which 7 were waited for; matrix products, arithmetic and copies ran while one was open for 3% of the time, Pallas kernels for 24%

profile of v4, /device:TPU:0, one launch (start us, length us, event | category | flops | bytes accessed | tf_op | source)
XLA Modules:
  0.0 76.6 jit_solution(15139141716993166356)
XLA Ops:
  0.0 0.5 collective-permute-start.1
  0.5 1.0 %slice.11 = bf16[256,512]{1,0:T(8,128)(2,1)S(1)} slice(bf16[256,1024]{1,0:T(8,128)(2,1)} %v_hbm.1), slice={[0:256], [0:512]} | slice | bytes 524288 | tf_op jit(solution)/shard_map/slice | solution.py:290
  1.5 2.6 %collective-permute-start.4 = (bf16[256,512]{1,0:T(8,128)(2,1)S(1)}, bf16[256,512]{1,0:T(8,128)(2,1)S(1)}, u32[]{:S(2)}, u32[]{:S(2)}) collective-permute-start(bf16[256,512]{1,0:T(8,128)(2,1)S(1)} %slice.11), channel_id=1, source_target_pairs={{0,16},{8,24},{16,0},{24,8},{1,17},{9,25},{17,1},{25,9},{2,18},{10... | collective-permute-start | bytes 786440 | tf_op jit(solution)/shard_map/ppermute | solution.py:290
  4.0 0.2 collective-permute-start
  4.3 1.1 %slice_select_fusion = bf16[256,512]{1,0:T(8,128)(2,1)S(1)} fusion(bf16[256,1024]{1,0:T(8,128)(2,1)} %k_hbm.1, bf16[256,1024]{1,0:T(8,128)(2,1)} %q_hbm.1, pred[]{:T(512)S(6)} %ge.3), kind=kLoop, calls=%fused_computation.2 | loop fusion | flops 131072 | bytes 786433 | tf_op jit(solution)/shard_map/jit(_where)/select_n | solution.py:256
  5.3 0.4 collective-permute-start.2
  5.7 5.4 %collective-permute-done.4.refs_2_ = bf16[256,512]{1,0:T(8,128)(2,1)S(1)} collective-permute-done((bf16[256,512]{1,0:T(8,128)(2,1)S(1)}, bf16[256,512]{1,0:T(8,128)(2,1)S(1)}, u32[]{:S(2)}, u32[]{:S(2)}) %collective-permute-start.4) | collective-permute-done | bytes 262176 | tf_op jit(solution)/shard_map/ppermute | solution.py:290
  11.2 0.0 collective-permute-start.5
  11.2 5.4 %collective-permute-done.2.refs_0_.q_ref = bf16[256,512]{1,0:T(8,128)(2,1)S(1)} collective-permute-done((bf16[256,512]{1,0:T(8,128)(2,1)S(1)}, bf16[256,512]{1,0:T(8,128)(2,1)S(1)}, u32[]{:S(2)}, u32[]{:S(2)}) %collective-permute-start.2) | collective-permute-done | bytes 262176 | tf_op jit(solution)/shard_map/ppermute | solution.py:255
  16.6 0.0 collective-permute-start.3
  16.6 0.1 pad_add_fusion.place_ref
  16.7 0.0 collective-permute-done.refs_0_.refs_1_
  16.7 0.0 collective-permute-done.1.refs_1_.refs_3_
  16.7 5.9 %own.1 = (bf16[256,1024]{1,0:T(8,128)(2,1)S(1)}, f32[256,128]{1,0:T(8,128)S(1)}, bf16[256,1024]{1,0:T(8,128)(2,1)S(1)}, bf16[256,1024]{1,0:T(8,128)(2,1)S(1)}, b...) custom-call(s32[2]{0:T(128)S(1)} %pad_add_fusion.place_ref, ...), custom_call_target="tpu_custom_call" | custom-call | tf_op jit(solution)/shard_map/own/pallas_call | solution.py:267
  22.6 1.3 %cross.3 = bf16[144,512]{1,0:T(8,128)(2,1)S(1)} custom-call(s32[2]{0:T(128)S(1)} %pad_add_fusion.place_ref, bf16[256,512]{1,0:T(8,128)(2,1)S(1)} %collective-permute-done.2.refs_0_.q_ref, bf16[256,1024]{1,0:T(8,128)(2,1)S(1)} %get-tuple-element.20.refs_0_, bf16[256,1024]{1,0:T(8,128)(2,1)S(1)} %collective-permute-done.refs_0_.refs_1_, ...), custom_call_target="tpu_custom_call" | custom-call | tf_op jit(solution)/shard_map/cross/pallas_call | solution.py:300
  23.9 1.0 %collective-permute-start.7 = (bf16[144,512]{1,0:T(8,128)(2,1)S(1)}, bf16[144,512]{1,0:T(8,128)(2,1)S(1)}, u32[]{:S(2)}, u32[]{:S(2)}) collective-permute-start(bf16[144,512]{1,0:T(8,128)(2,1)S(1)} %cross.3), channel_id=1, source_target_pairs={{0,16},{8,24},{16,0},{24,8},{1,17},{9,25},{17,1},{25,9},{2,18},{10... | collective-permute-start | bytes 442376 | tf_op jit(solution)/shard_map/ppermute | solution.py:308
  25.0 0.0 collective-permute-done.5.refs_3_
  25.0 0.0 collective-permute-done.3.refs_1_
  25.0 0.6 far.3.near_ref
  25.5 4.7 %collective-permute-done.7.back_ref = bf16[144,512]{1,0:T(8,128)(2,1)S(1)} collective-permute-done((bf16[144,512]{1,0:T(8,128)(2,1)S(1)}, bf16[144,512]{1,0:T(8,128)(2,1)S(1)}, u32[]{:S(2)}, u32[]{:S(2)}) %collective-permute-start.7) | collective-permute-done | bytes 147488 | tf_op jit(solution)/shard_map/ppermute | solution.py:308
  30.2 1.5 %merge.3 = (bf16[128,1024]{1,0:T(8,128)(2,1)S(1)}, bf16[128,1024]{1,0:T(8,128)(2,1)S(1)}) custom-call(s32[2]{0:T(128)S(1)} %pad_add_fusion.place_ref, bf16[256,1024]{1,0:T(8,128)(2,1)S(1)} %get-tuple-element.17.own_ref, f32[256,128]{1,0:T(8,128)S(1)} %get-tuple-element.18.lse_ref, bf16[128,512]{1,0:T(8,128)(2,1)S(1)} %far.3.near_ref, ...), custom_call_target="tpu_custom_call" | custom-call | tf_op jit(solution)/shard_map/merge/pallas_call | solution.py:327
  31.8 1.9 %collective-permute-start.11 = (bf16[128,1024]{1,0:T(8,128)(2,1)S(1)}, bf16[128,1024]{1,0:T(8,128)(2,1)S(1)}, u32[]{:S(2)}, u32[]{:S(2)}) collective-permute-start(bf16[128,1024]{1,0:T(8,128)(2,1)S(1)} %get-tuple-element.26), channel_id=1, source_target_pairs={{0,2},{2,0},{4,6},{6,4},{1,3},{3,1},{5,7},{7,5},{8,10},{10,8},{12,... | collective-permute-start | bytes 786440 | tf_op jit(solution)/shard_map/ppermute | solution.py:379
  33.6 1.3 %cross.2 = bf16[144,512]{1,0:T(8,128)(2,1)S(1)} custom-call(s32[2]{0:T(128)S(1)} %pad_add_fusion.place_ref, bf16[256,512]{1,0:T(8,128)(2,1)S(1)} %collective-permute-done.2.refs_0_.q_ref, bf16[256,1024]{1,0:T(8,128)(2,1)S(1)} %get-tuple-element.20.refs_0_, bf16[256,1024]{1,0:T(8,128)(2,1)S(1)} %collective-permute-done.refs_0_.refs_1_, ...), custom_call_target="tpu_custom_call" | custom-call | tf_op jit(solution)/shard_map/cross/pallas_call | solution.py:300
  35.0 0.0 collective-permute-start.6
  35.0 0.6 far.2.near_ref
  35.6 4.6 %collective-permute-done.6.back_ref = bf16[144,512]{1,0:T(8,128)(2,1)S(1)} collective-permute-done((bf16[144,512]{1,0:T(8,128)(2,1)S(1)}, bf16[144,512]{1,0:T(8,128)(2,1)S(1)}, u32[]{:S(2)}, u32[]{:S(2)}) %collective-permute-start.6) | collective-permute-done | bytes 147488 | tf_op jit(solution)/shard_map/ppermute | solution.py:308
  40.2 1.5 %merge.2 = (bf16[128,1024]{1,0:T(8,128)(2,1)S(1)}, bf16[128,1024]{1,0:T(8,128)(2,1)S(1)}) custom-call(s32[2]{0:T(128)S(1)} %pad_add_fusion.place_ref, bf16[256,1024]{1,0:T(8,128)(2,1)S(1)} %get-tuple-element.17.own_ref, f32[256,128]{1,0:T(8,128)S(1)} %get-tuple-element.18.lse_ref, bf16[128,512]{1,0:T(8,128)(2,1)S(1)} %far.2.near_ref, ...), custom_call_target="tpu_custom_call" | custom-call | tf_op jit(solution)/shard_map/merge/pallas_call | solution.py:327
  41.7 0.4 collective-permute-start.9
  42.1 0.8 %project.5 = bf16[128,1024]{1,0:T(8,128)(2,1)S(1)} custom-call(f32[256,128]{1,0:T(8,128)S(1)} %get-tuple-element.16.kinds_ref, bf16[2,1024,3072]{2,1,0:T(8,128)(2,1)S(1)} %get-tuple-element.22.w_ref, bf16[128,1024]{1,0:T(8,128)(2,1)S(1)} %get-tuple-element.24.refs_1_.refs_0_), custom_call_target="tpu_custom_call" | custom-call | tf_op jit(solution)/shard_map/project/pallas_call | solution.py:355
  42.8 0.8 %project.4 = bf16[128,1024]{1,0:T(8,128)(2,1)S(1)} custom-call(f32[256,128]{1,0:T(8,128)S(1)} %get-tuple-element.16.kinds_ref, bf16[2,1024,3072]{2,1,0:T(8,128)(2,1)S(1)} %get-tuple-element.22.w_ref, bf16[128,1024]{1,0:T(8,128)(2,1)S(1)} %get-tuple-element.23.refs_0_), custom_call_target="tpu_custom_call" | custom-call | tf_op jit(solution)/shard_map/project/pallas_call | solution.py:355
  43.6 1.3 %project.3 = bf16[256,1024]{1,0:T(8,128)(2,1)S(1)} custom-call(f32[256,128]{1,0:T(8,128)S(1)} %get-tuple-element.16.kinds_ref, bf16[2,1024,3072]{2,1,0:T(8,128)(2,1)S(1)} %get-tuple-element.22.w_ref, bf16[128,1024]{1,0:T(8,128)(2,1)S(1)} %get-tuple-element.23.refs_0_, bf16[128,1024]{1,0:T(8,128)(2,1)S(1)} %get-tuple-element.24.refs_1_.refs_0_), custom_call_target="tpu_custom_call" | custom-call | tf_op jit(solution)/shard_map/project/pallas_call | solution.py:355
  44.9 1.8 %collective-permute-start.8 = (bf16[256,1024]{1,0:T(8,128)(2,1)S(1)}, bf16[256,1024]{1,0:T(8,128)(2,1)S(1)}, u32[]{:S(2)}, u32[]{:S(2)}) collective-permute-start(bf16[256,1024]{1,0:T(8,128)(2,1)S(1)} %project.3), channel_id=1, source_target_pairs={{0,2},{2,0},{4,6},{6,4},{1,3},{3,1},{5,7},{7,5},{8,10},{10,8},{12,... | collective-permute-start | bytes 1572872 | tf_op jit(solution)/shard_map/ppermute | solution.py:388
  46.7 0.0 collective-permute-done.11
  46.7 0.1 add_convert_fusion
  46.8 2.7 %collective-permute-start.12 = (bf16[128,1024]{1,0:T(8,128)(2,1)S(1)}, bf16[128,1024]{1,0:T(8,128)(2,1)S(1)}, u32[]{:S(2)}, u32[]{:S(2)}) collective-permute-start(bf16[128,1024]{1,0:T(8,128)(2,1)S(1)} %add_convert_fusion), channel_id=1, source_target_pairs={{0,4},{2,6},{4,0},{6,2},{1,5},{3,7},{5,1},{7,3},{8,12},{10,14},{12... | collective-permute-start | bytes 786440 | tf_op jit(solution)/shard_map/ppermute | solution.py:379
  49.5 9.9 %collective-permute-done.9 = bf16[128,1024]{1,0:T(8,128)(2,1)S(1)} collective-permute-done((bf16[128,1024]{1,0:T(8,128)(2,1)S(1)}, bf16[128,1024]{1,0:T(8,128)(2,1)S(1)}, u32[]{:S(2)}, u32[]{:S(2)}) %collective-permute-start.9) | collective-permute-done | bytes 262176 | tf_op jit(solution)/shard_map/ppermute | solution.py:379
  59.4 0.1 add_convert_fusion.1
  59.4 0.1 collective-permute-start.10
  59.5 4.1 %stream.1.first_ref = bf16[256,1024]{1,0:T(8,128)(2,1)S(1)} custom-call(s32[2]{0:T(128)S(1)} %pad_add_fusion.place_ref, bf16[2,1024,4096]{2,1,0:T(8,128)(2,1)} %w_hbm.3, f32[256,128]{1,0:T(8,128)S(1)} %get-tuple-element.16.kinds_ref, bf16[128,1024]{1,0:T(8,128)(2,1)S(1)} %get-tuple-element.23.refs_0_, bf16[128,1024]{1,0:T(8,128)(2,1)S(1)} %get-tuple-element.24.refs_1_.refs_0_), custom_call_target="tpu_custom_call" | custom-call | tf_op jit(solution)/shard_map/stream/pallas_call | solution.py:340
  63.6 4.8 %collective-permute-done.8.second_ref = bf16[256,1024]{1,0:T(8,128)(2,1)S(1)} collective-permute-done((bf16[256,1024]{1,0:T(8,128)(2,1)S(1)}, bf16[256,1024]{1,0:T(8,128)(2,1)S(1)}, u32[]{:S(2)}, u32[]{:S(2)}) %collective-permute-start.8) | collective-permute-done | bytes 524320 | tf_op jit(solution)/shard_map/ppermute | solution.py:388
  68.4 0.0 collective-permute-done.12.refs_1_
  68.4 7.3 %collective-permute-done.10.refs_0_ = bf16[128,1024]{1,0:T(8,128)(2,1)S(1)} collective-permute-done((bf16[128,1024]{1,0:T(8,128)(2,1)S(1)}, bf16[128,1024]{1,0:T(8,128)(2,1)S(1)}, u32[]{:S(2)}, u32[]{:S(2)}) %collective-permute-start.10) | collective-permute-done | bytes 262176 | tf_op jit(solution)/shard_map/ppermute | solution.py:379
  75.7 0.9 %total.1 = bf16[256,1024]{1,0:T(8,128)(2,1)} custom-call(bf16[256,1024]{1,0:T(8,128)(2,1)S(1)} %stream.1.first_ref, bf16[256,1024]{1,0:T(8,128)(2,1)S(1)} %collective-permute-done.8.second_ref, bf16[128,1024]{1,0:T(8,128)(2,1)S(1)} %collective-permute-done.10.refs_0_, bf16[128,1024]{1,0:T(8,128)(2,1)S(1)} %collective-permute-done.12.refs_1_), custom_call_target="tpu_custom_call" | custom-call | tf_op jit(solution)/shard_map/total/pallas_call | solution.py:390
Async XLA Ops:
  0.0 16.7 %collective-permute-start.1 = (bf16[256,1024]{1,0:T(8,128)(2,1)}, bf16[256,1024]{1,0:T(8,128)(2,1)S(1)}, u32[]{:S(2)}, u32[]{:S(2)}) collective-permute-start(bf16[256,1024]{1,0:T(8,128)(2,1)} %v_hbm.1), channel_id=1, source_target_pairs={{0,8},{8,0},{16,24},{24,16},{1,9},{9,1},{17,25},{25,17},{2,10},{10... | collective-permute-start | bytes 1572872 | tf_op jit(solution)/shard_map/ppermute | solution.py:262
  1.5 9.7 %collective-permute-start.4 = (bf16[256,512]{1,0:T(8,128)(2,1)S(1)}, bf16[256,512]{1,0:T(8,128)(2,1)S(1)}, u32[]{:S(2)}, u32[]{:S(2)}) collective-permute-start(bf16[256,512]{1,0:T(8,128)(2,1)S(1)} %slice.11), channel_id=1, source_target_pairs={{0,16},{8,24},{16,0},{24,8},{1,17},{9,25},{17,1},{25,9},{2,18},{10... | collective-permute-start | bytes 786440 | tf_op jit(solution)/shard_map/ppermute | solution.py:290
  4.0 12.7 %collective-permute-start = (bf16[256,1024]{1,0:T(8,128)(2,1)}, bf16[256,1024]{1,0:T(8,128)(2,1)S(1)}, u32[]{:S(2)}, u32[]{:S(2)}) collective-permute-start(bf16[256,1024]{1,0:T(8,128)(2,1)} %k_hbm.1), channel_id=1, source_target_pairs={{0,8},{8,0},{16,24},{24,16},{1,9},{9,1},{17,25},{25,17},{2,10},{10... | collective-permute-start | bytes 1572872 | tf_op jit(solution)/shard_map/ppermute | solution.py:261
  5.3 11.3 %collective-permute-start.2 = (bf16[256,512]{1,0:T(8,128)(2,1)S(1)}, bf16[256,512]{1,0:T(8,128)(2,1)S(1)}, u32[]{:S(2)}, u32[]{:S(2)}) collective-permute-start(bf16[256,512]{1,0:T(8,128)(2,1)S(1)} %slice_select_fusion), channel_id=1, source_target_pairs={{0,16},{8,24},{16,0},{24,8},{1,17},{9,25},{17,1},{25,9},{2,18},{10... | collective-permute-start | bytes 786440 | tf_op jit(solution)/shard_map/ppermute | solution.py:255
  11.2 13.8 %collective-permute-start.5 = (bf16[256,512]{1,0:T(8,128)(2,1)S(1)}, bf16[256,512]{1,0:T(8,128)(2,1)S(1)}, u32[]{:S(2)}, u32[]{:S(2)}) collective-permute-start(bf16[256,512]{1,0:T(8,128)(2,1)S(1)} %collective-permute-done.4.refs_2_), channel_id=1, source_target_pairs={{0,8},{8,0},{16,24},{24,16},{1,9},{9,1},{17,25},{25,17},{2,10},{10... | collective-permute-start | bytes 786440 | tf_op jit(solution)/shard_map/ppermute | solution.py:294
  16.6 8.3 %collective-permute-start.3 = (bf16[256,512]{1,0:T(8,128)(2,1)S(1)}, bf16[256,512]{1,0:T(8,128)(2,1)S(1)}, u32[]{:S(2)}, u32[]{:S(2)}) collective-permute-start(bf16[256,512]{1,0:T(8,128)(2,1)S(1)} %collective-permute-done.2.refs_0_.q_ref), channel_id=1, source_target_pairs={{0,8},{8,0},{16,24},{24,16},{1,9},{9,1},{17,25},{25,17},{2,10},{10... | collective-permute-start | bytes 786440 | tf_op jit(solution)/shard_map/ppermute | solution.py:293
  23.9 6.3 %collective-permute-start.7 = (bf16[144,512]{1,0:T(8,128)(2,1)S(1)}, bf16[144,512]{1,0:T(8,128)(2,1)S(1)}, u32[]{:S(2)}, u32[]{:S(2)}) collective-permute-start(bf16[144,512]{1,0:T(8,128)(2,1)S(1)} %cross.3), channel_id=1, source_target_pairs={{0,16},{8,24},{16,0},{24,8},{1,17},{9,25},{17,1},{25,9},{2,18},{10... | collective-permute-start | bytes 442376 | tf_op jit(solution)/shard_map/ppermute | solution.py:308
  31.8 15.0 %collective-permute-start.11 = (bf16[128,1024]{1,0:T(8,128)(2,1)S(1)}, bf16[128,1024]{1,0:T(8,128)(2,1)S(1)}, u32[]{:S(2)}, u32[]{:S(2)}) collective-permute-start(bf16[128,1024]{1,0:T(8,128)(2,1)S(1)} %get-tuple-element.26), channel_id=1, source_target_pairs={{0,2},{2,0},{4,6},{6,4},{1,3},{3,1},{5,7},{7,5},{8,10},{10,8},{12,... | collective-permute-start | bytes 786440 | tf_op jit(solution)/shard_map/ppermute | solution.py:379
  35.0 5.2 %collective-permute-start.6 = (bf16[144,512]{1,0:T(8,128)(2,1)S(1)}, bf16[144,512]{1,0:T(8,128)(2,1)S(1)}, u32[]{:S(2)}, u32[]{:S(2)}) collective-permute-start(bf16[144,512]{1,0:T(8,128)(2,1)S(1)} %cross.2), channel_id=1, source_target_pairs={{0,16},{8,24},{16,0},{24,8},{1,17},{9,25},{17,1},{25,9},{2,18},{10... | collective-permute-start | bytes 442376 | tf_op jit(solution)/shard_map/ppermute | solution.py:308
  41.7 17.7 %collective-permute-start.9 = (bf16[128,1024]{1,0:T(8,128)(2,1)S(1)}, bf16[128,1024]{1,0:T(8,128)(2,1)S(1)}, u32[]{:S(2)}, u32[]{:S(2)}) collective-permute-start(bf16[128,1024]{1,0:T(8,128)(2,1)S(1)} %get-tuple-element.25), channel_id=1, source_target_pairs={{0,2},{2,0},{4,6},{6,4},{1,3},{3,1},{5,7},{7,5},{8,10},{10,8},{12,... | collective-permute-start | bytes 786440 | tf_op jit(solution)/shard_map/ppermute | solution.py:379
  44.9 23.4 %collective-permute-start.8 = (bf16[256,1024]{1,0:T(8,128)(2,1)S(1)}, bf16[256,1024]{1,0:T(8,128)(2,1)S(1)}, u32[]{:S(2)}, u32[]{:S(2)}) collective-permute-start(bf16[256,1024]{1,0:T(8,128)(2,1)S(1)} %project.3), channel_id=1, source_target_pairs={{0,2},{2,0},{4,6},{6,4},{1,3},{3,1},{5,7},{7,5},{8,10},{10,8},{12,... | collective-permute-start | bytes 1572872 | tf_op jit(solution)/shard_map/ppermute | solution.py:388
  46.8 21.6 %collective-permute-start.12 = (bf16[128,1024]{1,0:T(8,128)(2,1)S(1)}, bf16[128,1024]{1,0:T(8,128)(2,1)S(1)}, u32[]{:S(2)}, u32[]{:S(2)}) collective-permute-start(bf16[128,1024]{1,0:T(8,128)(2,1)S(1)} %add_convert_fusion), channel_id=1, source_target_pairs={{0,4},{2,6},{4,0},{6,2},{1,5},{3,7},{5,1},{7,3},{8,12},{10,14},{12... | collective-permute-start | bytes 786440 | tf_op jit(solution)/shard_map/ppermute | solution.py:379
  59.4 16.2 %collective-permute-start.10 = (bf16[128,1024]{1,0:T(8,128)(2,1)S(1)}, bf16[128,1024]{1,0:T(8,128)(2,1)S(1)}, u32[]{:S(2)}, u32[]{:S(2)}) collective-permute-start(bf16[128,1024]{1,0:T(8,128)(2,1)S(1)} %add_convert_fusion.1), channel_id=1, source_target_pairs={{0,4},{2,6},{4,0},{6,2},{1,5},{3,7},{5,1},{7,3},{8,12},{10,14},{12... | collective-permute-start | bytes 786440 | tf_op jit(solution)/shard_map/ppermute | solution.py:379

commit v5 on v4

--- a/solution.py
+++ b/solution.py
@@ -14,7 +14,7 @@
 SHARES = (1, 2)
 BLOCK = 256
 SLICES = 4
-PIECES = 4
+PIECES = 1
 LOG2E = float(np.log2(np.e))
 
 
@@ -91,25 +91,32 @@
     return jnp.where(lanes % shipped == h, lse, found)
 
 
-def lse_terms(found, shipped):
-    lanes = lax.broadcasted_iota(jnp.int32, found.shape, 1)
-    high = found.astype(jnp.bfloat16).astype(jnp.float32)
-    middle = (found - high).astype(jnp.bfloat16).astype(jnp.float32)
-    low = found - high - middle
-    return jnp.where(lanes < shipped, high, jnp.where(lanes < 2 * shipped, middle, low))
-
-
-def lse_rows(shipped):
-    return -(-3 * shipped // 16) * 16
-
-
-def cross_kernel(count, half, skip, lo, place_ref, q_ref, *refs):
+def lse_lines(shipped, rows, width):
+    lines = -(-shipped // (width // rows))
+    return lines, -(-3 * lines // 8) * 8
+
+
+def lse_terms(found, shipped, width):
+    rows = found.shape[0]
+    flat = found.T[:shipped]
+    high = flat.astype(jnp.bfloat16).astype(jnp.float32)
+    middle = (flat - high).astype(jnp.bfloat16).astype(jnp.float32)
+    low = flat - high - middle
+    lines, extra = lse_lines(shipped, rows, width)
+    each, out = width // rows, []
+    for term in (high, middle, low):
+        for line in range(lines):
+            heads = [term[h : h + 1] for h in range(line * each, min(shipped, (line + 1) * each))]
+            pad = width - len(heads) * rows
+            out.append(jnp.concatenate(heads + [jnp.zeros((1, pad), jnp.float32)] * bool(pad), axis=1))
+    return jnp.concatenate(out + [jnp.zeros((extra - len(out), width), jnp.float32)] * (extra > len(out)), axis=0)
+
+
+def cross_kernel(count, half, skip, lo, rows, place_ref, q_ref, *refs):
     k_refs, v_refs = refs[:count], refs[count : 2 * count]
     (out_ref,) = refs[2 * count :]
     width = q_ref.shape[1]
     shipped = width // HD
-    extra = lse_rows(shipped)
-    rows = out_ref.shape[0] - extra
     out_ref[...] = jnp.zeros_like(out_ref)
 
     @pl.when(place_ref[0] < half)
@@ -123,7 +130,7 @@
             )
             out_ref[:rows, at] = result.astype(out_ref.dtype)
             found = put_lse(found, h, shipped, lse)
-        out_ref[rows:, :rows] = lse_terms(found, shipped).T[:extra].astype(out_ref.dtype)
+        out_ref[rows:, :] = lse_terms(found, shipped, width).astype(out_ref.dtype)
 
 
 def mix(own, far, share, out_dtype):
@@ -168,8 +175,13 @@
     rows = slice(lo, lo + count)
     skip, shipped = near_ref.shape[1], back_ref.shape[1] // HD
     upper = place_ref[0] >= half
-    terms = back_ref[count:, :count].astype(jnp.float32)
-    far_lse = sum(terms[i * shipped : (i + 1) * shipped] for i in range(3))
+    lines, _ = lse_lines(shipped, count, back_ref.shape[1])
+    terms = back_ref[count:, :].astype(jnp.float32)
+    terms = sum(terms[i * lines : (i + 1) * lines] for i in range(3))
+    each = back_ref.shape[1] // count
+    far_lse = jnp.concatenate(
+        [terms[h // each : h // each + 1, h % each * count : (h % each + 1) * count] for h in range(shipped)], axis=0
+    )
     before = skip // HD
     far_lse = jnp.concatenate(
         [
@@ -298,8 +310,8 @@
     back, near = [], []
     for p, (lo, hi) in enumerate(parts):
         found = pl.pallas_call(
-            functools.partial(cross_kernel, count, half, skip, lo),
-            out_shape=jax.ShapeDtypeStruct((hi - lo + lse_rows(shipped), width - skip), jnp.bfloat16),
+            functools.partial(cross_kernel, count, half, skip, lo, hi - lo),
+            out_shape=jax.ShapeDtypeStruct((hi - lo + lse_lines(shipped, hi - lo, width - skip)[1], width - skip), jnp.bfloat16),
             in_specs=[smem] + [vmem] * (1 + 2 * count),
             out_specs=vmem,
             compiler_params=params(8),

time: 76.7 us -> 76.5 us (level)
    ppermute x1, waiting for transfers between devices: 4.79 us -> 0.01 us  [on_device(): beside = lax.ppermute(beside, 'tp', xor(tp_count, 1))]
    ppermute x4, waiting for transfers between devices: 17.2 us -> 21.9 us  [on_device(): arrived = lax.ppermute(keep.pop(offset), 'tp', xor(tp_count, bit))]
where the time goes in v5:
time: 76.5 us; the launch traced here: 76.3 us
  waiting for transfers between devices  41.8 us (55%)
  Pallas kernels  20.6 us (27%)
  starting transfers between devices  11.5 us (15%)
  other arithmetic  1.27 us (2%)
  local copies, waits for them, and re-layouts  0.97 us (1%)
    ppermute x4, waiting for transfers between devices, on_device(): arrived = lax.ppermute(keep.pop(offset), 'tp', xor(tp_count, bit))  21.9 us
    ppermute x2, waiting for transfers between devices, on_device(): lax.ppermute(found, 'seq', [xor(seq_count, half), xor(seq_count, half)][p])  9 us
    pallas_call x1, Pallas kernels, on_device(): pl.pallas_call(functools.partial(own_kernel, tuple(offsets), loads[0]), o...  5.81 us
    ppermute x1, waiting for transfers between devices, on_device(): far_vals = [lax.ppermute(values[:, :skip], 'seq', xor(seq_count, half))]  5.45 us
    ppermute x1, waiting for transfers between devices, on_device(): lax.ppermute(jnp.where(place[0] >= half, queries[:, skip:], key_rows[:, :...  5.43 us
    ppermute x4, starting transfers between devices, on_device(): arrived = lax.ppermute(keep.pop(offset), 'tp', xor(tp_count, bit))  4.88 us
    pallas_call x1, Pallas kernels, streamed(): pl.pallas_call(functools.partial(stream_kernel, offset), out_shape=jax.Sh...  4.09 us
    pallas_call x2, Pallas kernels, merged(): pl.pallas_call(functools.partial(merge_kernel, half, lo, first), out_shap...  3.09 us
  transfers between devices with their start and end apart: 13, of which 7 were waited for; matrix products, arithmetic and copies ran while one was open for 3% of the time, Pallas kernels for 24%

profile of v5, /device:TPU:0, one launch (start us, length us, event | category | flops | bytes accessed | tf_op | source)
XLA Modules:
  0.0 76.3 jit_solution(11351091245026704944)
XLA Ops:
  0.0 0.5 collective-permute-start.1
  0.5 1.0 %slice.11 = bf16[256,512]{1,0:T(8,128)(2,1)S(1)} slice(bf16[256,1024]{1,0:T(8,128)(2,1)} %v_hbm.1), slice={[0:256], [0:512]} | slice | bytes 524288 | tf_op jit(solution)/shard_map/slice | solution.py:302
  1.5 2.6 %collective-permute-start.4 = (bf16[256,512]{1,0:T(8,128)(2,1)S(1)}, bf16[256,512]{1,0:T(8,128)(2,1)S(1)}, u32[]{:S(2)}, u32[]{:S(2)}) collective-permute-start(bf16[256,512]{1,0:T(8,128)(2,1)S(1)} %slice.11), channel_id=1, source_target_pairs={{0,16},{8,24},{16,0},{24,8},{1,17},{9,25},{17,1},{25,9},{2,18},{10... | collective-permute-start | bytes 786440 | tf_op jit(solution)/shard_map/ppermute | solution.py:302
  4.0 0.2 collective-permute-start
  4.3 1.1 %slice_select_fusion = bf16[256,512]{1,0:T(8,128)(2,1)S(1)} fusion(bf16[256,1024]{1,0:T(8,128)(2,1)} %k_hbm.1, bf16[256,1024]{1,0:T(8,128)(2,1)} %q_hbm.1, pred[]{:T(512)S(6)} %ge.3), kind=kLoop, calls=%fused_computation.2 | loop fusion | flops 131072 | bytes 786433 | tf_op jit(solution)/shard_map/jit(_where)/select_n | solution.py:268
  5.3 0.4 collective-permute-start.2
  5.7 5.4 %collective-permute-done.4.refs_2_ = bf16[256,512]{1,0:T(8,128)(2,1)S(1)} collective-permute-done((bf16[256,512]{1,0:T(8,128)(2,1)S(1)}, bf16[256,512]{1,0:T(8,128)(2,1)S(1)}, u32[]{:S(2)}, u32[]{:S(2)}) %collective-permute-start.4) | collective-permute-done | bytes 262176 | tf_op jit(solution)/shard_map/ppermute | solution.py:302
  11.2 0.0 collective-permute-start.5
  11.2 5.4 %collective-permute-done.2.refs_0_.q_ref = bf16[256,512]{1,0:T(8,128)(2,1)S(1)} collective-permute-done((bf16[256,512]{1,0:T(8,128)(2,1)S(1)}, bf16[256,512]{1,0:T(8,128)(2,1)S(1)}, u32[]{:S(2)}, u32[]{:S(2)}) %collective-permute-start.2) | collective-permute-done | bytes 262176 | tf_op jit(solution)/shard_map/ppermute | solution.py:267
  16.6 0.0 collective-permute-start.3
  16.6 0.1 pad_add_fusion.place_ref
  16.7 0.0 collective-permute-done.refs_0_.refs_1_
  16.7 0.0 collective-permute-done.1.refs_1_.refs_3_
  16.7 5.8 %own.1 = (bf16[256,1024]{1,0:T(8,128)(2,1)S(1)}, f32[256,128]{1,0:T(8,128)S(1)}, bf16[256,1024]{1,0:T(8,128)(2,1)S(1)}, bf16[256,1024]{1,0:T(8,128)(2,1)S(1)}, b...) custom-call(s32[2]{0:T(128)S(1)} %pad_add_fusion.place_ref, ...), custom_call_target="tpu_custom_call" | custom-call | tf_op jit(solution)/shard_map/own/pallas_call | solution.py:279
  22.5 1.3 %cross.3 = bf16[136,512]{1,0:T(8,128)(2,1)S(1)} custom-call(s32[2]{0:T(128)S(1)} %pad_add_fusion.place_ref, bf16[256,512]{1,0:T(8,128)(2,1)S(1)} %collective-permute-done.2.refs_0_.q_ref, bf16[256,1024]{1,0:T(8,128)(2,1)S(1)} %get-tuple-element.20.refs_0_, bf16[256,1024]{1,0:T(8,128)(2,1)S(1)} %collective-permute-done.refs_0_.refs_1_, ...), custom_call_target="tpu_custom_call" | custom-call | tf_op jit(solution)/shard_map/cross/pallas_call | solution.py:312
  23.9 1.0 %collective-permute-start.7 = (bf16[136,512]{1,0:T(8,128)(2,1)S(1)}, bf16[136,512]{1,0:T(8,128)(2,1)S(1)}, u32[]{:S(2)}, u32[]{:S(2)}) collective-permute-start(bf16[136,512]{1,0:T(8,128)(2,1)S(1)} %cross.3), channel_id=1, source_target_pairs={{0,16},{8,24},{16,0},{24,8},{1,17},{9,25},{17,1},{25,9},{2,18},{10... | collective-permute-start | bytes 417800 | tf_op jit(solution)/shard_map/ppermute | solution.py:320
  24.9 0.0 collective-permute-done.5.refs_3_
  24.9 0.0 collective-permute-done.3.refs_1_
  24.9 0.6 far.3.near_ref
  25.5 4.5 %collective-permute-done.7.back_ref = bf16[136,512]{1,0:T(8,128)(2,1)S(1)} collective-permute-done((bf16[136,512]{1,0:T(8,128)(2,1)S(1)}, bf16[136,512]{1,0:T(8,128)(2,1)S(1)}, u32[]{:S(2)}, u32[]{:S(2)}) %collective-permute-start.7) | collective-permute-done | bytes 139296 | tf_op jit(solution)/shard_map/ppermute | solution.py:320
  30.0 1.5 %merge.3 = (bf16[128,1024]{1,0:T(8,128)(2,1)S(1)}, bf16[128,1024]{1,0:T(8,128)(2,1)S(1)}) custom-call(s32[2]{0:T(128)S(1)} %pad_add_fusion.place_ref, bf16[256,1024]{1,0:T(8,128)(2,1)S(1)} %get-tuple-element.17.own_ref, f32[256,128]{1,0:T(8,128)S(1)} %get-tuple-element.18.lse_ref, bf16[128,512]{1,0:T(8,128)(2,1)S(1)} %far.3.near_ref, ...), custom_call_target="tpu_custom_call" | custom-call | tf_op jit(solution)/shard_map/merge/pallas_call | solution.py:339
  31.6 1.9 %collective-permute-start.11 = (bf16[128,1024]{1,0:T(8,128)(2,1)S(1)}, bf16[128,1024]{1,0:T(8,128)(2,1)S(1)}, u32[]{:S(2)}, u32[]{:S(2)}) collective-permute-start(bf16[128,1024]{1,0:T(8,128)(2,1)S(1)} %get-tuple-element.26), channel_id=1, source_target_pairs={{0,2},{2,0},{4,6},{6,4},{1,3},{3,1},{5,7},{7,5},{8,10},{10,8},{12,... | collective-permute-start | bytes 786440 | tf_op jit(solution)/shard_map/ppermute | solution.py:391
  33.4 1.3 %cross.2 = bf16[136,512]{1,0:T(8,128)(2,1)S(1)} custom-call(s32[2]{0:T(128)S(1)} %pad_add_fusion.place_ref, bf16[256,512]{1,0:T(8,128)(2,1)S(1)} %collective-permute-done.2.refs_0_.q_ref, bf16[256,1024]{1,0:T(8,128)(2,1)S(1)} %get-tuple-element.20.refs_0_, bf16[256,1024]{1,0:T(8,128)(2,1)S(1)} %collective-permute-done.refs_0_.refs_1_, ...), custom_call_target="tpu_custom_call" | custom-call | tf_op jit(solution)/shard_map/cross/pallas_call | solution.py:312
  34.8 0.1 collective-permute-start.6
  34.8 0.6 far.2.near_ref
  35.4 4.5 %collective-permute-done.6.back_ref = bf16[136,512]{1,0:T(8,128)(2,1)S(1)} collective-permute-done((bf16[136,512]{1,0:T(8,128)(2,1)S(1)}, bf16[136,512]{1,0:T(8,128)(2,1)S(1)}, u32[]{:S(2)}, u32[]{:S(2)}) %collective-permute-start.6) | collective-permute-done | bytes 139296 | tf_op jit(solution)/shard_map/ppermute | solution.py:320
  39.9 1.5 %merge.2 = (bf16[128,1024]{1,0:T(8,128)(2,1)S(1)}, bf16[128,1024]{1,0:T(8,128)(2,1)S(1)}) custom-call(s32[2]{0:T(128)S(1)} %pad_add_fusion.place_ref, bf16[256,1024]{1,0:T(8,128)(2,1)S(1)} %get-tuple-element.17.own_ref, f32[256,128]{1,0:T(8,128)S(1)} %get-tuple-element.18.lse_ref, bf16[128,512]{1,0:T(8,128)(2,1)S(1)} %far.2.near_ref, ...), custom_call_target="tpu_custom_call" | custom-call | tf_op jit(solution)/shard_map/merge/pallas_call | solution.py:339
  41.4 0.3 collective-permute-start.9
  41.7 0.8 %project.5 = bf16[128,1024]{1,0:T(8,128)(2,1)S(1)} custom-call(f32[256,128]{1,0:T(8,128)S(1)} %get-tuple-element.16.kinds_ref, bf16[2,1024,3072]{2,1,0:T(8,128)(2,1)S(1)} %get-tuple-element.22.w_ref, bf16[128,1024]{1,0:T(8,128)(2,1)S(1)} %get-tuple-element.24.refs_1_.refs_0_), custom_call_target="tpu_custom_call" | custom-call | tf_op jit(solution)/shard_map/project/pallas_call | solution.py:367
  42.5 0.8 %project.4 = bf16[128,1024]{1,0:T(8,128)(2,1)S(1)} custom-call(f32[256,128]{1,0:T(8,128)S(1)} %get-tuple-element.16.kinds_ref, bf16[2,1024,3072]{2,1,0:T(8,128)(2,1)S(1)} %get-tuple-element.22.w_ref, bf16[128,1024]{1,0:T(8,128)(2,1)S(1)} %get-tuple-element.23.refs_0_), custom_call_target="tpu_custom_call" | custom-call | tf_op jit(solution)/shard_map/project/pallas_call | solution.py:367
  43.3 1.3 %project.3 = bf16[256,1024]{1,0:T(8,128)(2,1)S(1)} custom-call(f32[256,128]{1,0:T(8,128)S(1)} %get-tuple-element.16.kinds_ref, bf16[2,1024,3072]{2,1,0:T(8,128)(2,1)S(1)} %get-tuple-element.22.w_ref, bf16[128,1024]{1,0:T(8,128)(2,1)S(1)} %get-tuple-element.23.refs_0_, bf16[128,1024]{1,0:T(8,128)(2,1)S(1)} %get-tuple-element.24.refs_1_.refs_0_), custom_call_target="tpu_custom_call" | custom-call | tf_op jit(solution)/shard_map/project/pallas_call | solution.py:367
  44.6 1.9 %collective-permute-start.8 = (bf16[256,1024]{1,0:T(8,128)(2,1)S(1)}, bf16[256,1024]{1,0:T(8,128)(2,1)S(1)}, u32[]{:S(2)}, u32[]{:S(2)}) collective-permute-start(bf16[256,1024]{1,0:T(8,128)(2,1)S(1)} %project.3), channel_id=1, source_target_pairs={{0,2},{2,0},{4,6},{6,4},{1,3},{3,1},{5,7},{7,5},{8,10},{10,8},{12,... | collective-permute-start | bytes 1572872 | tf_op jit(solution)/shard_map/ppermute | solution.py:400
  46.5 0.0 collective-permute-done.11
  46.5 0.1 add_convert_fusion
  46.6 2.7 %collective-permute-start.12 = (bf16[128,1024]{1,0:T(8,128)(2,1)S(1)}, bf16[128,1024]{1,0:T(8,128)(2,1)S(1)}, u32[]{:S(2)}, u32[]{:S(2)}) collective-permute-start(bf16[128,1024]{1,0:T(8,128)(2,1)S(1)} %add_convert_fusion), channel_id=1, source_target_pairs={{0,4},{2,6},{4,0},{6,2},{1,5},{3,7},{5,1},{7,3},{8,12},{10,14},{12... | collective-permute-start | bytes 786440 | tf_op jit(solution)/shard_map/ppermute | solution.py:391
  49.2 9.9 %collective-permute-done.9 = bf16[128,1024]{1,0:T(8,128)(2,1)S(1)} collective-permute-done((bf16[128,1024]{1,0:T(8,128)(2,1)S(1)}, bf16[128,1024]{1,0:T(8,128)(2,1)S(1)}, u32[]{:S(2)}, u32[]{:S(2)}) %collective-permute-start.9) | collective-permute-done | bytes 262176 | tf_op jit(solution)/shard_map/ppermute | solution.py:391
  59.1 0.1 add_convert_fusion.1
  59.2 0.1 collective-permute-start.10
  59.2 4.1 %stream.1.first_ref = bf16[256,1024]{1,0:T(8,128)(2,1)S(1)} custom-call(s32[2]{0:T(128)S(1)} %pad_add_fusion.place_ref, bf16[2,1024,4096]{2,1,0:T(8,128)(2,1)} %w_hbm.3, f32[256,128]{1,0:T(8,128)S(1)} %get-tuple-element.16.kinds_ref, bf16[128,1024]{1,0:T(8,128)(2,1)S(1)} %get-tuple-element.23.refs_0_, bf16[128,1024]{1,0:T(8,128)(2,1)S(1)} %get-tuple-element.24.refs_1_.refs_0_), custom_call_target="tpu_custom_call" | custom-call | tf_op jit(solution)/shard_map/stream/pallas_call | solution.py:352
  63.3 1.1 %collective-permute-done.12.refs_1_ = bf16[128,1024]{1,0:T(8,128)(2,1)S(1)} collective-permute-done((bf16[128,1024]{1,0:T(8,128)(2,1)S(1)}, bf16[128,1024]{1,0:T(8,128)(2,1)S(1)}, u32[]{:S(2)}, u32[]{:S(2)}) %collective-permute-start.12) | collective-permute-done | bytes 262176 | tf_op jit(solution)/shard_map/ppermute | solution.py:391
  64.5 10.9 %collective-permute-done.10.refs_0_ = bf16[128,1024]{1,0:T(8,128)(2,1)S(1)} collective-permute-done((bf16[128,1024]{1,0:T(8,128)(2,1)S(1)}, bf16[128,1024]{1,0:T(8,128)(2,1)S(1)}, u32[]{:S(2)}, u32[]{:S(2)}) %collective-permute-start.10) | collective-permute-done | bytes 262176 | tf_op jit(solution)/shard_map/ppermute | solution.py:391
  75.4 0.0 collective-permute-done.8.second_ref
  75.4 0.9 %total.1 = bf16[256,1024]{1,0:T(8,128)(2,1)} custom-call(bf16[256,1024]{1,0:T(8,128)(2,1)S(1)} %stream.1.first_ref, bf16[256,1024]{1,0:T(8,128)(2,1)S(1)} %collective-permute-done.8.second_ref, bf16[128,1024]{1,0:T(8,128)(2,1)S(1)} %collective-permute-done.10.refs_0_, bf16[128,1024]{1,0:T(8,128)(2,1)S(1)} %collective-permute-done.12.refs_1_), custom_call_target="tpu_custom_call" | custom-call | tf_op jit(solution)/shard_map/total/pallas_call | solution.py:402
Async XLA Ops:
  0.0 16.7 %collective-permute-start.1 = (bf16[256,1024]{1,0:T(8,128)(2,1)}, bf16[256,1024]{1,0:T(8,128)(2,1)S(1)}, u32[]{:S(2)}, u32[]{:S(2)}) collective-permute-start(bf16[256,1024]{1,0:T(8,128)(2,1)} %v_hbm.1), channel_id=1, source_target_pairs={{0,8},{8,0},{16,24},{24,16},{1,9},{9,1},{17,25},{25,17},{2,10},{10... | collective-permute-start | bytes 1572872 | tf_op jit(solution)/shard_map/ppermute | solution.py:274
  1.5 9.7 %collective-permute-start.4 = (bf16[256,512]{1,0:T(8,128)(2,1)S(1)}, bf16[256,512]{1,0:T(8,128)(2,1)S(1)}, u32[]{:S(2)}, u32[]{:S(2)}) collective-permute-start(bf16[256,512]{1,0:T(8,128)(2,1)S(1)} %slice.11), channel_id=1, source_target_pairs={{0,16},{8,24},{16,0},{24,8},{1,17},{9,25},{17,1},{25,9},{2,18},{10... | collective-permute-start | bytes 786440 | tf_op jit(solution)/shard_map/ppermute | solution.py:302
  4.0 12.7 %collective-permute-start = (bf16[256,1024]{1,0:T(8,128)(2,1)}, bf16[256,1024]{1,0:T(8,128)(2,1)S(1)}, u32[]{:S(2)}, u32[]{:S(2)}) collective-permute-start(bf16[256,1024]{1,0:T(8,128)(2,1)} %k_hbm.1), channel_id=1, source_target_pairs={{0,8},{8,0},{16,24},{24,16},{1,9},{9,1},{17,25},{25,17},{2,10},{10... | collective-permute-start | bytes 1572872 | tf_op jit(solution)/shard_map/ppermute | solution.py:273
  5.3 11.3 %collective-permute-start.2 = (bf16[256,512]{1,0:T(8,128)(2,1)S(1)}, bf16[256,512]{1,0:T(8,128)(2,1)S(1)}, u32[]{:S(2)}, u32[]{:S(2)}) collective-permute-start(bf16[256,512]{1,0:T(8,128)(2,1)S(1)} %slice_select_fusion), channel_id=1, source_target_pairs={{0,16},{8,24},{16,0},{24,8},{1,17},{9,25},{17,1},{25,9},{2,18},{10... | collective-permute-start | bytes 786440 | tf_op jit(solution)/shard_map/ppermute | solution.py:267
  11.2 13.7 %collective-permute-start.5 = (bf16[256,512]{1,0:T(8,128)(2,1)S(1)}, bf16[256,512]{1,0:T(8,128)(2,1)S(1)}, u32[]{:S(2)}, u32[]{:S(2)}) collective-permute-start(bf16[256,512]{1,0:T(8,128)(2,1)S(1)} %collective-permute-done.4.refs_2_), channel_id=1, source_target_pairs={{0,8},{8,0},{16,24},{24,16},{1,9},{9,1},{17,25},{25,17},{2,10},{10... | collective-permute-start | bytes 786440 | tf_op jit(solution)/shard_map/ppermute | solution.py:306
  16.6 8.3 %collective-permute-start.3 = (bf16[256,512]{1,0:T(8,128)(2,1)S(1)}, bf16[256,512]{1,0:T(8,128)(2,1)S(1)}, u32[]{:S(2)}, u32[]{:S(2)}) collective-permute-start(bf16[256,512]{1,0:T(8,128)(2,1)S(1)} %collective-permute-done.2.refs_0_.q_ref), channel_id=1, source_target_pairs={{0,8},{8,0},{16,24},{24,16},{1,9},{9,1},{17,25},{25,17},{2,10},{10... | collective-permute-start | bytes 786440 | tf_op jit(solution)/shard_map/ppermute | solution.py:305
  23.9 6.1 %collective-permute-start.7 = (bf16[136,512]{1,0:T(8,128)(2,1)S(1)}, bf16[136,512]{1,0:T(8,128)(2,1)S(1)}, u32[]{:S(2)}, u32[]{:S(2)}) collective-permute-start(bf16[136,512]{1,0:T(8,128)(2,1)S(1)} %cross.3), channel_id=1, source_target_pairs={{0,16},{8,24},{16,0},{24,8},{1,17},{9,25},{17,1},{25,9},{2,18},{10... | collective-permute-start | bytes 417800 | tf_op jit(solution)/shard_map/ppermute | solution.py:320
  31.6 14.9 %collective-permute-start.11 = (bf16[128,1024]{1,0:T(8,128)(2,1)S(1)}, bf16[128,1024]{1,0:T(8,128)(2,1)S(1)}, u32[]{:S(2)}, u32[]{:S(2)}) collective-permute-start(bf16[128,1024]{1,0:T(8,128)(2,1)S(1)} %get-tuple-element.26), channel_id=1, source_target_pairs={{0,2},{2,0},{4,6},{6,4},{1,3},{3,1},{5,7},{7,5},{8,10},{10,8},{12,... | collective-permute-start | bytes 786440 | tf_op jit(solution)/shard_map/ppermute | solution.py:391
  34.8 5.1 %collective-permute-start.6 = (bf16[136,512]{1,0:T(8,128)(2,1)S(1)}, bf16[136,512]{1,0:T(8,128)(2,1)S(1)}, u32[]{:S(2)}, u32[]{:S(2)}) collective-permute-start(bf16[136,512]{1,0:T(8,128)(2,1)S(1)} %cross.2), channel_id=1, source_target_pairs={{0,16},{8,24},{16,0},{24,8},{1,17},{9,25},{17,1},{25,9},{2,18},{10... | collective-permute-start | bytes 417800 | tf_op jit(solution)/shard_map/ppermute | solution.py:320
  41.4 17.7 %collective-permute-start.9 = (bf16[128,1024]{1,0:T(8,128)(2,1)S(1)}, bf16[128,1024]{1,0:T(8,128)(2,1)S(1)}, u32[]{:S(2)}, u32[]{:S(2)}) collective-permute-start(bf16[128,1024]{1,0:T(8,128)(2,1)S(1)} %get-tuple-element.25), channel_id=1, source_target_pairs={{0,2},{2,0},{4,6},{6,4},{1,3},{3,1},{5,7},{7,5},{8,10},{10,8},{12,... | collective-permute-start | bytes 786440 | tf_op jit(solution)/shard_map/ppermute | solution.py:391
  44.6 30.8 %collective-permute-start.8 = (bf16[256,1024]{1,0:T(8,128)(2,1)S(1)}, bf16[256,1024]{1,0:T(8,128)(2,1)S(1)}, u32[]{:S(2)}, u32[]{:S(2)}) collective-permute-start(bf16[256,1024]{1,0:T(8,128)(2,1)S(1)} %project.3), channel_id=1, source_target_pairs={{0,2},{2,0},{4,6},{6,4},{1,3},{3,1},{5,7},{7,5},{8,10},{10,8},{12,... | collective-permute-start | bytes 1572872 | tf_op jit(solution)/shard_map/ppermute | solution.py:400
  46.6 17.9 %collective-permute-start.12 = (bf16[128,1024]{1,0:T(8,128)(2,1)S(1)}, bf16[128,1024]{1,0:T(8,128)(2,1)S(1)}, u32[]{:S(2)}, u32[]{:S(2)}) collective-permute-start(bf16[128,1024]{1,0:T(8,128)(2,1)S(1)} %add_convert_fusion), channel_id=1, source_target_pairs={{0,4},{2,6},{4,0},{6,2},{1,5},{3,7},{5,1},{7,3},{8,12},{10,14},{12... | collective-permute-start | bytes 786440 | tf_op jit(solution)/shard_map/ppermute | solution.py:391
  59.2 16.2 %collective-permute-start.10 = (bf16[128,1024]{1,0:T(8,128)(2,1)S(1)}, bf16[128,1024]{1,0:T(8,128)(2,1)S(1)}, u32[]{:S(2)}, u32[]{:S(2)}) collective-permute-start(bf16[128,1024]{1,0:T(8,128)(2,1)S(1)} %add_convert_fusion.1), channel_id=1, source_target_pairs={{0,4},{2,6},{4,0},{6,2},{1,5},{3,7},{5,1},{7,3},{8,12},{10,14},{12... | collective-permute-start | bytes 786440 | tf_op jit(solution)/shard_map/ppermute | solution.py:391
